TPU v7x, 32 devices: a whole 2x2x4 slice. The times are simulated.
32 devices in a mesh: ulysses: 2 (over y), blk: 16 (over z, x, core).
Axes of the slice: x: 2, y: 2, z: 4, core: 2. Of those that a mesh axis runs over, the one named last changes fastest.
Arguments:
- tokens: bfloat16 [4096, 768], P(('ulysses', 'blk')), may hold values from -6 to 6
- condition: float32 [128], replicated, may hold values from -6 to 6
- ada_weight: bfloat16 [128, 4608], P(None, ('ulysses', 'blk')), may hold values from -0.25 to 0.25
- ada_bias: bfloat16 [4608], P(('ulysses', 'blk')), may hold values from -3 to 3
- first_gain: bfloat16 [768], P(('ulysses', 'blk')), may hold values from 0.099609375 to 1.8984375
- second_gain: bfloat16 [768], P(('ulysses', 'blk')), may hold values from 0.099609375 to 1.8984375
- project_weight: bfloat16 [768, 2304], P(None, ('ulysses', 'blk')), may hold values from -0.21875 to 0.21875
- output_weight: bfloat16 [768, 768], P(('ulysses', 'blk')), may hold values from -4 to 4
- expand_weight: bfloat16 [768, 3072], P(None, ('ulysses', 'blk')), may hold values from -0.21875 to 0.21875
- expand_bias: bfloat16 [3072], P(('ulysses', 'blk')), may hold values from -3 to 3
- reduce_weight: bfloat16 [3072, 768], P(('ulysses', 'blk')), may hold values from -0.109375 to 0.109375
- reduce_bias: bfloat16 [768], P(('ulysses', 'blk')), may hold values from -1.75 to 1.75
- cotangent: bfloat16 [4096, 768], P(('ulysses', 'blk')), may hold values from -6 to 6
Outputs:
- result: bfloat16 [4096, 768], P(('ulysses', 'blk'))
- grad_tokens: float32 [4096, 768], P(('ulysses', 'blk'))
- grad_condition: float32 [128], replicated
- grad_ada_weight: float32 [128, 4608], P(None, ('ulysses', 'blk'))
- grad_ada_bias: float32 [4608], P(('ulysses', 'blk'))
- grad_first_gain: float32 [768], P(('ulysses', 'blk'))
- grad_second_gain: float32 [768], P(('ulysses', 'blk'))
- grad_project_weight: float32 [768, 2304], P(None, ('ulysses', 'blk'))
- grad_output_weight: float32 [768, 768], P(('ulysses', 'blk'))
- grad_expand_weight: float32 [768, 3072], P(None, ('ulysses', 'blk'))
- grad_expand_bias: float32 [3072], P(('ulysses', 'blk'))
- grad_reduce_weight: float32 [3072, 768], P(('ulysses', 'blk'))
- grad_reduce_bias: float32 [768], P(('ulysses', 'blk'))
All inputs are finite; a program needn't handle non-finite values.
Results may differ from a plain program's by a relative error of at most 0.025.
Values may be sent and summed in bfloat16 or wider, within the bound.
A program may use at most 320 MiB of HBM per device.

v0:
```python
from functools import partial
import math

import jax
import jax.numpy as jnp
from jax import lax
from jax.sharding import PartitionSpec as P

HEAD_DIM = 64


eps = 1e-05
highest = lax.Precision.HIGHEST


def layer_norm(value):
    center = value - jnp.mean(value, axis=-1, keepdims=True)
    inverse = lax.rsqrt(jnp.mean(center * center, axis=-1, keepdims=True) + eps)
    return (center * inverse, inverse)


def norm_back(grad_normed, normed, inverse):
    first = jnp.mean(grad_normed, axis=-1, keepdims=True)
    second = jnp.mean(grad_normed * normed, axis=-1, keepdims=True)
    return inverse * (grad_normed - first - normed * second)


def rotary_tables(positions, head_dim):
    half_dim = head_dim // 2
    frequency = jnp.exp(
        jnp.arange(half_dim, dtype=jnp.float32) * (-2.0 * math.log(10000.0) / head_dim)
    )
    angles = positions[:, None] * frequency[None, :]
    return (jnp.cos(angles)[:, None, :], jnp.sin(angles)[:, None, :])


def rotate(value, cosine, sine):
    half_dim = value.shape[-1] // 2
    first = value[..., :half_dim]
    second = value[..., half_dim:]
    return jnp.concatenate(
        [first * cosine - second * sine, second * cosine + first * sine], axis=-1
    )


def rotate_back(grad_value, cosine, sine):
    half_dim = grad_value.shape[-1] // 2
    first = grad_value[..., :half_dim]
    second = grad_value[..., half_dim:]
    return jnp.concatenate(
        [first * cosine + second * sine, second * cosine - first * sine], axis=-1
    )


def over_blocks(block_step, carried, pieces, key_block):
    length = pieces[0].shape[1]
    complete = length // key_block
    stacked = tuple(
        (
            jnp.moveaxis(
                member.reshape((member.shape[0], complete, key_block) + member.shape[2:]), 1, 0
            )
            for member in pieces
        )
    )
    offsets = jnp.arange(complete, dtype=jnp.int32) * key_block

    def scan_step(carried_in, inputs):
        return (block_step(carried_in, inputs[:-1], inputs[-1]), None)

    carried, unused = lax.scan(scan_step, carried, stacked + (offsets,))
    return carried


def on_device(
    tokens,
    condition,
    ada_weight,
    ada_bias,
    first_gain,
    second_gain,
    project_weight,
    output_weight,
    expand_weight,
    expand_bias,
    reduce_weight,
    reduce_bias,
    cotangent,
):
    row_count = tokens.shape[0]
    model_width = tokens.shape[1]
    cycle_size = lax.axis_size("blk")
    cycle_place = lax.axis_index("blk")
    seq_count = lax.axis_size("ulysses")
    (
        ada_full,
        ada_shift,
        gain_one,
        gain_two,
        project_full,
        output_full,
        expand_full,
        expand_shift,
        reduce_full,
        reduce_shift,
    ) = (
        lax.all_gather(ada_weight, ("ulysses", "blk"), axis=1, tiled=True),
        lax.all_gather(ada_bias, ("ulysses", "blk"), axis=0, tiled=True),
        lax.all_gather(first_gain, ("ulysses", "blk"), axis=0, tiled=True),
        lax.all_gather(second_gain, ("ulysses", "blk"), axis=0, tiled=True),
        lax.all_gather(project_weight, ("ulysses", "blk"), axis=1, tiled=True),
        lax.all_gather(output_weight, ("ulysses", "blk"), axis=0, tiled=True),
        lax.all_gather(expand_weight, ("ulysses", "blk"), axis=1, tiled=True),
        lax.all_gather(expand_bias, ("ulysses", "blk"), axis=0, tiled=True),
        lax.all_gather(reduce_weight, ("ulysses", "blk"), axis=0, tiled=True),
        lax.all_gather(reduce_bias, ("ulysses", "blk"), axis=0, tiled=True),
    )
    ada_float = ada_full.astype(jnp.float32)
    modulation = jnp.dot(condition, ada_float, precision=highest) + ada_shift.astype(jnp.float32)
    shift_one, scale_one, gate_one, shift_two, scale_two, gate_two = jnp.split(modulation, 6)
    gain_one_f = gain_one.astype(jnp.float32)
    gain_two_f = gain_two.astype(jnp.float32)
    inputs = tokens.astype(jnp.float32)
    normed_one, inverse_one = layer_norm(inputs)
    gain_first = gain_one_f * (1.0 + scale_one)
    mixed_one = (normed_one * gain_first + shift_one).astype(jnp.bfloat16)
    projected = jnp.dot(mixed_one, project_full, preferred_element_type=jnp.float32)
    packed = projected.astype(jnp.bfloat16).reshape(row_count, 3, model_width)
    regrouped = lax.all_to_all(packed, "ulysses", split_axis=2, concat_axis=0, tiled=True)
    local_rows = regrouped.shape[0]
    local_width = regrouped.shape[2]
    head_count = local_width // HEAD_DIM
    by_seq = regrouped.reshape(seq_count, row_count, 3, local_width)
    positions = cycle_place * row_count + jnp.arange(row_count, dtype=jnp.int32)
    cosine, sine = rotary_tables(positions.astype(jnp.float32), HEAD_DIM)
    query_rot = rotate(
        by_seq[:, :, 0].astype(jnp.float32).reshape(seq_count, row_count, head_count, HEAD_DIM),
        cosine,
        sine,
    ).astype(jnp.bfloat16)
    key_rot = rotate(
        by_seq[:, :, 1].astype(jnp.float32).reshape(seq_count, row_count, head_count, HEAD_DIM),
        cosine,
        sine,
    ).astype(jnp.bfloat16)
    value_flat = by_seq[:, :, 2]
    value_own = value_flat.reshape(seq_count, row_count, head_count, HEAD_DIM)
    key_flat = key_rot.reshape(seq_count, row_count, local_width)
    score_scale = HEAD_DIM ** (-0.5)
    key_block = row_count * -(-512 // row_count)

    def attend_step(carried, pieces, offset):
        maximum, denominator, weighted = carried
        key_rows = pieces[0].reshape(seq_count, -1, head_count, HEAD_DIM)
        value_rows = pieces[1].reshape(seq_count, -1, head_count, HEAD_DIM)
        scores = (
            jnp.einsum("sqhd,skhd->shqk", query_rot, key_rows, preferred_element_type=jnp.float32)
            * score_scale
        )
        new_maximum = jnp.maximum(maximum, jnp.max(scores, axis=-1))
        weights = jnp.exp(scores - new_maximum[..., None])
        factor = jnp.exp(maximum - new_maximum)
        denominator = denominator * factor + jnp.sum(weights, axis=-1)
        weighted = weighted * jnp.transpose(factor, (0, 2, 1))[..., None] + jnp.einsum(
            "shqk,skhd->sqhd",
            weights.astype(jnp.bfloat16),
            value_rows,
            preferred_element_type=jnp.float32,
        )
        return (new_maximum, denominator, weighted)

    start_state = (
        jnp.full((seq_count, head_count, row_count), -1e30, jnp.float32),
        jnp.zeros((seq_count, head_count, row_count), jnp.float32),
        jnp.zeros((seq_count, row_count, head_count, HEAD_DIM), jnp.float32),
    )
    maximum, denominator, weighted = over_blocks(
        attend_step,
        start_state,
        (
            lax.all_gather(key_flat, "blk", axis=1, tiled=True),
            lax.all_gather(value_flat, "blk", axis=1, tiled=True),
        ),
        key_block,
    )
    log_total = maximum + jnp.log(denominator)
    attended = (
        (weighted / jnp.transpose(denominator, (0, 2, 1))[..., None])
        .astype(jnp.bfloat16)
        .reshape(local_rows, local_width)
    )
    attended_tokens = lax.all_to_all(attended, "ulysses", split_axis=0, concat_axis=1, tiled=True)
    attn_branch = jnp.dot(attended_tokens, output_full, preferred_element_type=jnp.float32)
    middle = inputs + gate_one * attn_branch
    normed_two, inverse_two = layer_norm(middle)
    gain_second = gain_two_f * (1.0 + scale_two)
    mixed_two = (normed_two * gain_second + shift_two).astype(jnp.bfloat16)
    hidden = jnp.dot(
        mixed_two, expand_full, preferred_element_type=jnp.float32
    ) + expand_shift.astype(jnp.float32)
    activated, gelu_back = jax.vjp(partial(jax.nn.gelu, approximate=True), hidden)
    activated_low = activated.astype(jnp.bfloat16)
    mlp_branch = jnp.dot(
        activated_low, reduce_full, preferred_element_type=jnp.float32
    ) + reduce_shift.astype(jnp.float32)
    result = (middle + gate_two * mlp_branch).astype(jnp.bfloat16)
    grad_result = cotangent.astype(jnp.float32)
    grad_gate_two = jnp.sum(grad_result * mlp_branch, axis=0)
    grad_branch = (gate_two * grad_result).astype(jnp.bfloat16)
    grad_reduce = jnp.einsum(
        "tf,td->fd", activated_low, grad_branch, preferred_element_type=jnp.float32
    )
    grad_reduce_shift = jnp.sum(grad_branch.astype(jnp.float32), axis=0)
    grad_activated = jnp.einsum(
        "td,fd->tf", grad_branch, reduce_full, preferred_element_type=jnp.float32
    )
    grad_hidden = gelu_back(grad_activated)[0].astype(jnp.bfloat16)
    grad_expand = jnp.einsum(
        "td,tf->df", mixed_two, grad_hidden, preferred_element_type=jnp.float32
    )
    grad_expand_shift = jnp.sum(grad_hidden.astype(jnp.float32), axis=0)
    grad_mixed_two = jnp.einsum(
        "tf,df->td", grad_hidden, expand_full, preferred_element_type=jnp.float32
    )
    grad_shift_two = jnp.sum(grad_mixed_two, axis=0)
    grad_scale_two = jnp.sum(grad_mixed_two * normed_two * gain_two_f, axis=0)
    grad_gain_two = jnp.sum(grad_mixed_two * normed_two * (1.0 + scale_two), axis=0)
    grad_middle = grad_result + norm_back(grad_mixed_two * gain_second, normed_two, inverse_two)
    grad_gate_one = jnp.sum(grad_middle * attn_branch, axis=0)
    grad_attn = (gate_one * grad_middle).astype(jnp.bfloat16)
    grad_output = jnp.einsum(
        "tc,td->cd", attended_tokens, grad_attn, preferred_element_type=jnp.float32
    )
    grad_heads = jnp.einsum(
        "td,cd->tc", grad_attn, output_full, preferred_element_type=jnp.float32
    ).astype(jnp.bfloat16)
    grad_local = lax.all_to_all(grad_heads, "ulysses", split_axis=1, concat_axis=0, tiled=True)
    grad_local_heads = grad_local.reshape(seq_count, row_count, head_count, HEAD_DIM)
    row_dots = jnp.sum(
        (grad_local.astype(jnp.float32) * attended.astype(jnp.float32)).reshape(
            seq_count, row_count, head_count, HEAD_DIM
        ),
        axis=-1,
    )
    row_dots_t = jnp.transpose(row_dots, (0, 2, 1))

    def query_step(carried, pieces, offset):
        key_rows = pieces[0].reshape(seq_count, -1, head_count, HEAD_DIM)
        value_rows = pieces[1].reshape(seq_count, -1, head_count, HEAD_DIM)
        scores = (
            jnp.einsum("sqhd,skhd->shqk", query_rot, key_rows, preferred_element_type=jnp.float32)
            * score_scale
        )
        shares = jnp.exp(scores - log_total[..., None])
        grad_shares = jnp.einsum(
            "sqhd,skhd->shqk", grad_local_heads, value_rows, preferred_element_type=jnp.float32
        )
        grad_scores = (shares * (grad_shares - row_dots_t[..., None])).astype(jnp.bfloat16)
        return (
            carried
            + jnp.einsum(
                "shqk,skhd->sqhd", grad_scores, key_rows, preferred_element_type=jnp.float32
            )
            * score_scale
        )

    grad_query_rot = over_blocks(
        query_step,
        jnp.zeros((seq_count, row_count, head_count, HEAD_DIM), jnp.float32),
        (
            lax.all_gather(key_flat, "blk", axis=1, tiled=True),
            lax.all_gather(value_flat, "blk", axis=1, tiled=True),
        ),
        key_block,
    )

    def key_step(carried, pieces, offset):
        grad_keys_acc, grad_values_acc = carried
        query_rows = pieces[0].reshape(seq_count, -1, head_count, HEAD_DIM)
        slope_rows = pieces[1].reshape(seq_count, -1, head_count, HEAD_DIM)
        scores = (
            jnp.einsum("sqhd,skhd->shqk", query_rows, key_rot, preferred_element_type=jnp.float32)
            * score_scale
        )
        shares = jnp.exp(scores - jnp.transpose(pieces[2], (0, 2, 1))[..., None])
        grad_values_acc = grad_values_acc + jnp.einsum(
            "shqk,sqhd->skhd",
            shares.astype(jnp.bfloat16),
            slope_rows,
            preferred_element_type=jnp.float32,
        )
        grad_shares = jnp.einsum(
            "sqhd,skhd->shqk", slope_rows, value_own, preferred_element_type=jnp.float32
        )
        grad_scores = (
            shares * (grad_shares - jnp.transpose(pieces[3], (0, 2, 1))[..., None])
        ).astype(jnp.bfloat16)
        grad_keys_acc = (
            grad_keys_acc
            + jnp.einsum(
                "shqk,sqhd->skhd", grad_scores, query_rows, preferred_element_type=jnp.float32
            )
            * score_scale
        )
        return (grad_keys_acc, grad_values_acc)

    query_wide = query_rot.reshape(seq_count, row_count, local_width)
    slope_wide = grad_local.reshape(seq_count, row_count, local_width)
    key_init = (
        jnp.zeros((seq_count, row_count, head_count, HEAD_DIM), jnp.float32),
        jnp.zeros((seq_count, row_count, head_count, HEAD_DIM), jnp.float32),
    )
    grad_key_rot, grad_value_sum = over_blocks(
        key_step,
        key_init,
        (
            lax.all_gather(query_wide.astype(jnp.float32), "blk", axis=1, tiled=True).astype(
                jnp.bfloat16
            ),
            lax.all_gather(slope_wide.astype(jnp.float32), "blk", axis=1, tiled=True).astype(
                jnp.bfloat16
            ),
            lax.all_gather(jnp.transpose(log_total, (0, 2, 1)), "blk", axis=1, tiled=True),
            lax.all_gather(row_dots, "blk", axis=1, tiled=True),
        ),
        key_block,
    )
    grad_query = (
        rotate_back(grad_query_rot, cosine, sine)
        .astype(jnp.bfloat16)
        .reshape(local_rows, local_width)
    )
    grad_key = (
        rotate_back(grad_key_rot, cosine, sine)
        .astype(jnp.bfloat16)
        .reshape(local_rows, local_width)
    )
    grad_value = grad_value_sum.astype(jnp.bfloat16).reshape(local_rows, local_width)
    grad_packed = jnp.stack([grad_query, grad_key, grad_value], axis=1)
    grad_tokens_qkv = lax.all_to_all(
        grad_packed, "ulysses", split_axis=0, concat_axis=2, tiled=True
    ).reshape(row_count, 3 * model_width)
    grad_project = jnp.einsum(
        "tc,tk->ck", mixed_one, grad_tokens_qkv, preferred_element_type=jnp.float32
    )
    grad_mixed_one = jnp.einsum(
        "tk,ck->tc", grad_tokens_qkv, project_full, preferred_element_type=jnp.float32
    )
    grad_shift_one = jnp.sum(grad_mixed_one, axis=0)
    grad_scale_one = jnp.sum(grad_mixed_one * normed_one * gain_one_f, axis=0)
    grad_gain_one = jnp.sum(grad_mixed_one * normed_one * (1.0 + scale_one), axis=0)
    grad_input = grad_middle + norm_back(grad_mixed_one * gain_first, normed_one, inverse_one)
    mod_terms = jnp.concatenate(
        [
            grad_shift_one,
            grad_scale_one,
            grad_gate_one,
            grad_shift_two,
            grad_scale_two,
            grad_gate_two,
        ]
    )
    grad_modulation = lax.psum(mod_terms, ("ulysses", "blk"))
    grad_condition = jnp.dot(ada_float, grad_modulation, precision=highest)
    piece_width = ada_weight.shape[1]
    flat_index = lax.axis_index("ulysses") * cycle_size + cycle_place
    mod_piece = lax.dynamic_slice_in_dim(grad_modulation, flat_index * piece_width, piece_width, 0)
    grad_ada = condition[:, None] * mod_piece[None, :]
    shards = (
        lax.psum_scatter(grad_gain_one, ("ulysses", "blk"), scatter_dimension=0, tiled=True),
        lax.psum_scatter(grad_gain_two, ("ulysses", "blk"), scatter_dimension=0, tiled=True),
        lax.psum_scatter(grad_project, ("ulysses", "blk"), scatter_dimension=1, tiled=True),
        lax.psum_scatter(grad_output, ("ulysses", "blk"), scatter_dimension=0, tiled=True),
        lax.psum_scatter(grad_expand, ("ulysses", "blk"), scatter_dimension=1, tiled=True),
        lax.psum_scatter(grad_expand_shift, ("ulysses", "blk"), scatter_dimension=0, tiled=True),
        lax.psum_scatter(grad_reduce, ("ulysses", "blk"), scatter_dimension=0, tiled=True),
        lax.psum_scatter(grad_reduce_shift, ("ulysses", "blk"), scatter_dimension=0, tiled=True),
    )
    return (
        result,
        grad_input,
        grad_condition,
        grad_ada,
        mod_piece,
        shards[0],
        shards[1],
        shards[2],
        shards[3],
        shards[4],
        shards[5],
        shards[6],
        shards[7],
    )


def solution(mesh):
    return jax.shard_map(
        on_device,
        mesh=mesh,
        in_specs=(
            P(("ulysses", "blk"), None),
            P(),
            P(None, ("ulysses", "blk")),
            P(("ulysses", "blk")),
            P(("ulysses", "blk")),
            P(("ulysses", "blk")),
            P(None, ("ulysses", "blk")),
            P(("ulysses", "blk"), None),
            P(None, ("ulysses", "blk")),
            P(("ulysses", "blk")),
            P(("ulysses", "blk"), None),
            P(("ulysses", "blk")),
            P(("ulysses", "blk"), None),
        ),
        out_specs=(
            P(("ulysses", "blk"), None),
            P(("ulysses", "blk"), None),
            P(),
            P(None, ("ulysses", "blk")),
            P(("ulysses", "blk")),
            P(("ulysses", "blk")),
            P(("ulysses", "blk")),
            P(None, ("ulysses", "blk")),
            P(("ulysses", "blk"), None),
            P(None, ("ulysses", "blk")),
            P(("ulysses", "blk")),
            P(("ulysses", "blk"), None),
            P(("ulysses", "blk")),
        ),
        check_vma=False,
    )
```

profile of v0, /device:TPU:5, one launch (start us, length us, event | category | flops | bytes accessed | tf_op | source)
XLA Modules:
  0.0 1042.6 jit_solution(8975379541207277995)
XLA Ops:
  12.9 40.7 %all-reduce.10 = (bf16[4608]{0:T(1024)(128)(2,1)S(1)}, bf16[768]{0:T(1024)(128)(2,1)S(1)}, bf16[768]{0:T(1024)(128)(2,1)}, bf16[3072]{0:T(1024)(128)(2,1)}, bf16[768]{0:T(1024)(128)(2,1)S(1)}) all-reduce(bf16[4608]{0:T(1024)(128)(2,1)S(1)} %dynamic-update-slice, ...), channel_id=1, replica_groups=mesh['ulysses'=2,'blk'=16] {'ulysses','blk'}, use_global_device_ids=true, to_apply=%add | all-reduce | flops 9984 | bytes 39936
  55.8 10.8 %all-gather.11.cloned.1.call-done = bf16[128,4608]{0,1:T(8,128)(2,1)} async-done(((bf16[128,144]{0,1:T(8,128)(2,1)}), bf16[128,4608]{0,1:T(8,128)(2,1)}) %all-gather.11.cloned.1.call-update) | async-done | bytes 1179664 | tf_op jit(solution)/shard_map/all_gather | solution.py:107
  69.6 58.9 %all-gather.13.cloned.1.call-done = bf16[768,2304]{0,1:T(8,128)(2,1)} async-done(((bf16[768,72]{0,1:T(8,128)(2,1)}), bf16[768,2304]{0,1:T(8,128)(2,1)}) %all-gather.13.cloned.1.call-update) | async-done | bytes 3538960 | tf_op jit(solution)/shard_map/all_gather | solution.py:111
  137.6 9.4 all-to-all-done
  152.0 44.5 %all-gather.15.cloned.1.call-done = bf16[2,2048,384]{1,2,0:T(8,128)(2,1)} async-done(((bf16[2,128,384]{1,2,0:T(8,128)(2,1)}), bf16[2,2048,384]{1,2,0:T(8,128)(2,1)}) %all-gather.15.cloned.1.call-update) | async-done | bytes 3145744 | tf_op jit(solution)/shard_map/all_gather | solution.py:181
  202.9 41.6 %all-gather.27.cloned.1.call-done = bf16[2,2048,1,384]{1,3,0,2:T(8,128)(2,1)} async-done(((bf16[2,128,1,384]{1,3,0,2:T(8,128)(2,1)}), bf16[2,2048,1,384]{1,3,0,2:T(8,128)(2,1)}) %all-gather.27.cloned.1.call-update) | async-done | bytes 3145744 | tf_op jit(solution)/shard_map/all_gather | solution.py:182
  250.8 23.5 %while.39 = (s32[]{:T(128)}, f32[2,6,128]{2,1,0:T(8,128)S(1)}, f32[2,6,128]{2,1,0:T(8,128)}, f32[2,128,6,64]{1,3,2,0:T(8,128)}, bf16[4,2,512,384]{2,3,1,0:T(8,12...) while((s32[]{:T(128)}, f32[2,6,128]{2,1,0:T(8,128)S(1)}, ...), condition=%wide.region_5.6_spmd.clone, body=%wide.region_2.5_spmd.clone.sunk | while | flops 207922176 | bytes 21577984 | solution.py:71
  281.8 17.6 %all-gather.17.cloned.1.call-done = bf16[768,768]{1,0:T(8,128)(2,1)} async-done(((bf16[24,768]{1,0:T(8,128)(2,1)}), bf16[768,768]{1,0:T(8,128)(2,1)}) %all-gather.17.cloned.1.call-update) | async-done | bytes 1179664 | tf_op jit(solution)/shard_map/all_gather | solution.py:112
  302.0 62.7 %all-gather.19.cloned.1.call-done = bf16[768,3072]{0,1:T(8,128)(2,1)} async-done(((bf16[768,96]{0,1:T(8,128)(2,1)}), bf16[768,3072]{0,1:T(8,128)(2,1)}) %all-gather.19.cloned.1.call-update) | async-done | bytes 4718608 | tf_op jit(solution)/shard_map/all_gather | solution.py:113
  368.8 61.2 %all-gather.21.cloned.1.call-done = bf16[3072,768]{1,0:T(8,128)(2,1)} async-done(((bf16[96,768]{1,0:T(8,128)(2,1)}), bf16[3072,768]{1,0:T(8,128)(2,1)}) %all-gather.21.cloned.1.call-update) | async-done | bytes 4718608 | tf_op jit(solution)/shard_map/all_gather | solution.py:115
  430.0 5.1 convert_reduce_fusion
  441.1 6.6 all_to_all.65
  449.6 6.2 fusion.72
  456.8 5.3 fusion.61
  462.8 21.0 %all_gather.63 = f32[2,2048,6]{1,2,0:T(8,128)S(1)} all-gather(f32[2,128,6]{1,2,0:T(8,128)S(1)} %bitcast.240), channel_id=1, replica_groups=mesh['ulysses'=2,'blk'=16] {'blk'}, dimensions={1}, use_global_device_ids=true | all-gather | bytes 104448 | tf_op jit(solution)/shard_map/all_gather | solution.py:323
  484.5 4.8 copy.114
  489.4 18.1 %all_gather.65 = f32[2,2048,6]{1,2,0:T(8,128)S(1)} all-gather(f32[2,128,6]{1,2,0:T(8,128)S(1)} %multiply_reduce_fusion.5), channel_id=1, replica_groups=mesh['ulysses'=2,'blk'=16] {'blk'}, dimensions={1}, use_global_device_ids=true | all-gather | bytes 104448 | tf_op jit(solution)/shard_map/all_gather | solution.py:324
  508.2 29.4 %while.40 = (s32[]{:T(128)}, f32[2,128,6,64]{1,3,2,0:T(8,128)}, bf16[4,2,512,384]{2,3,1,0:T(8,128)(2,1)}, bf16[2,128,6,64]{1,3,2,0:T(8,128)(2,1)S(1)}, f32[2,6,1...) while((s32[]{:T(128)}, f32[2,128,6,64]{1,3,2,0:T(8,128)}, ...), condition=%wide.region_12.13_spmd.clone, body=%wide.region_11.12_spmd.clone.sunk | while | flops 306216960 | bytes 16134295 | solution.py:71
  542.4 70.2 %while.41 = (s32[]{:T(128)}, f32[2,128,6,64]{1,3,2,0:T(8,128)}, f32[2,128,6,64]{1,3,2,0:T(8,128)S(1)}, bf16[4,2,512,384]{3,2,0,1:T(8,128)(2,1)}, bf16[2,128,6,64...) while((s32[]{:T(128)}, f32[2,128,6,64]{1,3,2,0:T(8,128)}, ...), condition=%wide.region_14.15_spmd.clone, body=%wide.region_13.14_spmd.clone.sunk | while | flops 409436160 | bytes 21110920 | solution.py:71
  615.9 13.9 %all_to_all.66 = bf16[256,3,384]{2,1,0:T(4,128)(2,1)S(1)} all-to-all(bf16[256,3,384]{2,1,0:T(4,128)(2,1)S(1)} %copy.124), channel_id=1, replica_groups=mesh['ulysses'=2,'blk'=16] {'ulysses'}, dimensions={0} | all-to-all | bytes 1179648 | tf_op jit(solution)/shard_map/all_to_all | solution.py:340
  640.3 39.4 %all-reduce.9 = (f32[4608]{0:T(1024)S(1)}, f32[768]{0:T(1024)S(1)}, f32[768]{0:T(1024)S(1)}, f32[3072]{0:T(1024)S(1)}, f32[768]{0:T(1024)S(1)}) all-reduce(f32[4608]{0:T(1024)} %copy-done.32, f32[768]{0:T(1024)} %get-tuple-element.343, f32[768]{0:T(1024)} %get-tuple-element.340, ...), channel_id=1, replica_groups=mesh['ulysses'=2,'blk'=16] {'ulysses','blk'}, use_global_device_ids=true, to_apply=%region_23.24 | all-reduce | flops 9984 | bytes 79872 | tf_op jit(solution)/shard_map/psum | solution.py:363
  689.2 80.2 %reduce-scatter.9.cloned.1.call-done = f32[768,96]{0,1:T(8,128)} async-done(((f32[768,3072]{0,1:T(8,128)}), f32[768,96]{0,1:T(8,128)}) %reduce-scatter.9.cloned.1.call-update) | async-done | bytes 294928 | tf_op jit(solution)/shard_map/reduce_scatter | solution.py:374
  769.3 141.0 %reduce-scatter.11.cloned.1.call-done = f32[96,768]{1,0:T(8,128)} async-done(((f32[3072,768]{1,0:T(8,128)}), f32[96,768]{1,0:T(8,128)}) %reduce-scatter.11.cloned.1.call-update) | async-done | bytes 294928 | tf_op jit(solution)/shard_map/reduce_scatter | solution.py:376
  910.3 125.7 %reduce-scatter.5.cloned.1.call-done = f32[768,72]{0,1:T(8,128)} async-done(((f32[768,2304]{0,1:T(8,128)}), f32[768,72]{0,1:T(8,128)}) %reduce-scatter.5.cloned.1.call-update) | async-done | bytes 221200 | tf_op jit(solution)/shard_map/reduce_scatter | solution.py:372
  (338 shorter events, 213.1 us)
Async XLA Ops:
  7.2 59.4 %all-gather.11.cloned.1.call-start = ((), (), s32[]{:S(2)}) async-start(), calls=%async_computation.8 | async-start | bytes 1216512 | tf_op jit(solution)/shard_map/all_gather | solution.py:107
  7.9 120.5 %all-gather.13.cloned.1.call-start = ((), (), s32[]{:S(2)}) async-start(), calls=%async_computation.9 | async-start | bytes 3649536 | tf_op jit(solution)/shard_map/all_gather | solution.py:111
  53.6 74.9 %copy-start.41 = (bf16[768]{0:T(1024)(128)(2,1)}, bf16[768]{0:T(1024)(128)(2,1)S(1)}, u32[]{:S(2)}) copy-start(bf16[768]{0:T(1024)(128)(2,1)S(1)} %get-tuple-element.406) | copy-start | bytes 4612
  53.6 74.9 %copy-start.42 = (bf16[768]{0:T(1024)(128)(2,1)}, bf16[768]{0:T(1024)(128)(2,1)S(1)}, u32[]{:S(2)}) copy-start(bf16[768]{0:T(1024)(128)(2,1)S(1)} %get-tuple-element.409) | copy-start | bytes 4612
  54.6 73.8 %copy-start.37 = (f32[128]{0:T(128)}, f32[128]{0:T(128)S(1)}, u32[]{:S(2)}) copy-start(f32[128]{0:T(128)S(1)} %broadcast_multiply_fusion.6) | copy-start | bytes 1540
  55.8 72.7 %copy-start.39 = (f32[128]{0:T(128)}, f32[128]{0:T(128)S(1)}, u32[]{:S(2)}) copy-start(f32[128]{0:T(128)S(1)} %add_rsqrt_fusion.1) | copy-start | bytes 1540
  133.6 13.3 %all-to-all-start = ((bf16[128,3,768]{0,1,2:T(4,128)(2,1)}), bf16[128,3,768]{0,1,2:T(4,128)(2,1)S(1)}, u32[]{:S(2)}, u32[]{:S(2)}) async-start(bf16[128,3,768]{0,1,2:T(4,128)(2,1)} %copy.104), calls=%async_computation | async-start | bytes 1572864 | tf_op jit(solution)/shard_map/all_to_all | solution.py:129
  137.4 59.1 %all-gather.15.cloned.1.call-start = ((), (), s32[]{:S(2)}) async-start(), calls=%async_computation.10 | async-start | bytes 3342336 | tf_op jit(solution)/shard_map/all_gather | solution.py:181
  148.7 95.8 %all-gather.27.cloned.1.call-start = ((), (), s32[]{:S(2)}) async-start(), calls=%async_computation.20 | async-start | bytes 3342336 | tf_op jit(solution)/shard_map/all_gather | solution.py:182
  149.3 150.1 %all-gather.17.cloned.1.call-start = ((), (), s32[]{:S(2)}) async-start(), calls=%async_computation.11 | async-start | bytes 1216512 | tf_op jit(solution)/shard_map/all_gather | solution.py:112
  149.9 214.8 %all-gather.19.cloned.1.call-start = ((), (), s32[]{:S(2)}) async-start(), calls=%async_computation.12 | async-start | bytes 4866048 | tf_op jit(solution)/shard_map/all_gather | solution.py:113
  150.4 279.6 %all-gather.21.cloned.1.call-start = ((), (), s32[]{:S(2)}) async-start(), calls=%async_computation.13 | async-start | bytes 4866048 | tf_op jit(solution)/shard_map/all_gather | solution.py:115
  151.2 333.3 %all-gather.23.cloned.1.call-start = ((), (), s32[]{:S(2)}) async-start(), calls=%async_computation.14 | async-start | bytes 3342336 | tf_op jit(solution)/shard_map/all_gather | solution.py:317
  274.3 90.4 %copy-start.19 = (f32[768]{0:T(1024)S(1)}, f32[768]{0:T(1024)}, u32[]{:S(2)}) copy-start(f32[768]{0:T(1024)} %get-tuple-element.445) | copy-start | bytes 9220
  274.3 90.4 %copy-start.20 = (f32[768]{0:T(1024)S(1)}, f32[768]{0:T(1024)}, u32[]{:S(2)}) copy-start(f32[768]{0:T(1024)} %get-tuple-element.447) | copy-start | bytes 9220
  276.0 23.4 %all-to-all-start.1 = ((bf16[2,128,384]{1,2,0:T(8,128)(2,1)}), bf16[2,128,384]{1,2,0:T(8,128)(2,1)S(1)}, u32[]{:S(2)}, u32[]{:S(2)}) async-start(bf16[2,128,384]{1,2,0:T(8,128)(2,1)} %bitcast.15), calls=%async_computation.1 | async-start | bytes 393216 | tf_op jit(solution)/shard_map/all_to_all | solution.py:192
  279.7 257.9 %all-gather.25.cloned.1.call-start = ((), (), s32[]{:S(2)}) async-start(), calls=%async_computation.15 | async-start | bytes 3342336 | tf_op jit(solution)/shard_map/all_gather | solution.py:320
  364.7 70.4 %slice-start = ((s8[4718592]{0:T(1024)(128)(4,1)}), s8[524288]{0:T(1024)(128)(4,1)S(1)}, s32[]{:S(2)}) async-start(s8[4718592]{0:T(1024)(128)(4,1)} %bitcast.211), calls=%async_computation.21 | async-start | bytes 1048576
  447.6 241.5 %reduce-scatter.7.cloned.1.call-start = ((), (), s32[]{:S(2)}) async-start(), calls=%async_computation.17 | async-start | bytes 2433024 | tf_op jit(solution)/shard_map/reduce_scatter | solution.py:373
  449.6 319.8 %reduce-scatter.9.cloned.1.call-start = ((), (), s32[]{:S(2)}) async-start(), calls=%async_computation.18 | async-start | bytes 9732096 | tf_op jit(solution)/shard_map/reduce_scatter | solution.py:374
  455.9 454.4 %reduce-scatter.11.cloned.1.call-start = ((), (), s32[]{:S(2)}) async-start(), calls=%async_computation.19 | async-start | bytes 9732096 | tf_op jit(solution)/shard_map/reduce_scatter | solution.py:376
  462.1 573.9 %reduce-scatter.5.cloned.1.call-start = ((), (), s32[]{:S(2)}) async-start(), calls=%async_computation.16 | async-start | bytes 7299072 | tf_op jit(solution)/shard_map/reduce_scatter | solution.py:372
  542.4 70.5 %copy-start.24 = (f32[128,32]{0,1:T(8,128)S(1)}, f32[128,32]{0,1:T(8,128)}, u32[]{:S(2)}) copy-start(f32[128,32]{0,1:T(8,128)} %copy-done.23) | copy-start | bytes 49156
  679.7 356.3 %copy-start.43 = (f32[144]{0:T(256)}, f32[144]{0:T(256)S(1)}, u32[]{:S(2)}) copy-start(f32[144]{0:T(256)S(1)} %dynamic_slice.29) | copy-start | bytes 1732
  (58 other events, 505.3 us)
Sparse Core Ops, SparseCore 0:
  10.9 55.6 all-gather.10
  69.5 58.9 all-gather.12
  148.8 47.6 all-gather.14
  199.1 45.3 all-gather.26
  247.2 52.1 all-gather.16
  302.2 62.5 all-gather.18
  367.6 62.3 all-gather.20
  432.2 46.6 all-gather.22
  481.0 45.6 all-gather.24
  532.4 95.1 reduce-scatter.6
  635.0 134.2 reduce-scatter.8
  775.7 134.5 reduce-scatter.10
  917.5 118.4 reduce-scatter.4
where the time goes:
time: 1050 us; the launch traced here: 1040 us
  waiting for transfers between devices  657 us (63%)
  blocking collectives  140 us (13%)
  matrix products  105 us (10%)
  local copies, waits for them, and re-layouts  100 us (10%)
  other arithmetic  17.9 us (2%)
  between operations  14.5 us (1%)
    reduce_scatter x1, waiting for transfers between devices, on_device(): lax.psum_scatter(grad_reduce, ('ulysses', 'blk'), scatter_dimension=0, ti...  141 us
    reduce_scatter x1, waiting for transfers between devices, on_device(): lax.psum_scatter(grad_project, ('ulysses', 'blk'), scatter_dimension=1, t...  126 us
    reduce_scatter x1, waiting for transfers between devices, on_device(): lax.psum_scatter(grad_expand, ('ulysses', 'blk'), scatter_dimension=1, ti...  80.2 us
    all_gather x1, waiting for transfers between devices, on_device(): lax.all_gather(expand_weight, ('ulysses', 'blk'), axis=1, tiled=True)  62.7 us
    all_gather x1, waiting for transfers between devices, on_device(): lax.all_gather(reduce_weight, ('ulysses', 'blk'), axis=0, tiled=True)  61.2 us
    all_gather x1, waiting for transfers between devices, on_device(): lax.all_gather(project_weight, ('ulysses', 'blk'), axis=1, tiled=True)  58.9 us
    dynamic_slice x32, local copies, waits for them, and re-layouts, over_blocks(): carried, unused = lax.scan(scan_step, carried, stacked + (offsets,))  51.4 us
    all_gather x1, waiting for transfers between devices, on_device(): lax.all_gather(key_flat, 'blk', axis=1, tiled=True)  44.5 us
  transfers between devices with their start and end apart: 15, of which 11 were waited for; matrix products, arithmetic and copies ran while one was open for 19% of the time, Pallas kernels for 0%

commit v1 on v0

--- a/solution.py
+++ b/solution.py
@@ -3,7 +3,10 @@
 
 import jax
 import jax.numpy as jnp
+import numpy as np
 from jax import lax
+from jax.experimental import pallas as pl
+from jax.experimental.pallas import tpu as pltpu
 from jax.sharding import PartitionSpec as P
 
 HEAD_DIM = 64
@@ -393,9 +396,1025 @@
     )
 
 
+MESH = pl.DeviceIdType.MESH
+Y, ZH, ZL, X, C = 16, 8, 4, 2, 1
+TP = (0, X, ZL, X + ZL)
+DP = (0, C, Y, Y + C, ZH, ZH + C, ZH + Y, ZH + Y + C)
+BLK = 128
+f32 = jnp.float32
+bf16 = jnp.bfloat16
+
+
+def place():
+    blk = lax.axis_index("blk")
+    return (lax.axis_index("ulysses"), blk // 8, (blk // 4) % 2, (blk // 2) % 2, blk % 2)
+
+
+def flip(offset):
+    return tuple(
+        1 - bit if (offset // weight) % 2 else bit
+        for bit, weight in zip(place(), (Y, ZH, ZL, X, C))
+    )
+
+
+def peer(offset):
+    y, zh, zl, x, c = flip(offset)
+    return (y, zh * 8 + zl * 4 + x * 2 + c)
+
+
+def peer_loop(offset):
+    y, zh, zl, x, c = (
+        (bit + (offset // weight) % 2) % 2 for bit, weight in zip(place(), (Y, ZH, ZL, X, C))
+    )
+    return (y, zh * 8 + zl * 4 + x * 2 + c)
+
+
+def flat(device):
+    return device[0] * 16 + device[1]
+
+
+def share(offset):
+    y, zh, zl, x, c = flip(offset)
+    return zh * 4 + y * 2 + c
+
+
+def enter(offsets):
+    barrier = pltpu.get_barrier_semaphore()
+    for offset in offsets:
+        pl.semaphore_signal(barrier, inc=1, device_id=peer(offset), device_id_type=MESH)
+    pl.semaphore_wait(barrier, len(offsets))
+
+
+def remote(source, target, send_sem, recv_sem, offset):
+    return pltpu.make_async_remote_copy(
+        src_ref=source,
+        dst_ref=target,
+        send_sem=send_sem,
+        recv_sem=recv_sem,
+        device_id=peer(offset),
+        device_id_type=MESH,
+    )
+
+
+def dot_nn(a, b):
+    return jnp.dot(a, b, preferred_element_type=f32)
+
+
+def dot_nt(a, b):
+    return lax.dot_general(a, b, (((1,), (1,)), ((), ())), preferred_element_type=f32)
+
+
+def dot_tn(a, b):
+    return lax.dot_general(a, b, (((0,), (0,)), ((), ())), preferred_element_type=f32)
+
+
+class Gather:
+    def __init__(self, buffer, send_sem, recv_sem):
+        self.buffer, self.send_sem, self.recv_sem = buffer, send_sem, recv_sem
+        self.sent = []
+
+    def send(self, have, to):
+        slot = self.buffer.at[share(have)]
+        index = len(self.sent)
+        copy = remote(
+            slot, slot, self.send_sem.at[index], self.recv_sem.at[DP.index(have + to)], to
+        )
+        copy.start()
+        self.sent.append(copy)
+
+    def arrive(self, what):
+        slot = self.buffer.at[share(what)]
+        remote(
+            slot, slot, self.send_sem.at[0], self.recv_sem.at[DP.index(what)], C
+        ).wait_recv()
+
+    def first(self):
+        self.send(0, ZH)
+        self.send(0, Y)
+        self.send(0, C)
+
+    def second(self):
+        self.arrive(ZH)
+        self.send(ZH, Y)
+        self.send(ZH, C)
+
+    def third(self):
+        self.arrive(Y)
+        self.send(Y, C)
+        self.arrive(ZH + Y)
+        self.send(ZH + Y, C)
+
+    def last(self):
+        for what in (C, Y + C, ZH + C, ZH + Y + C):
+            self.arrive(what)
+        for copy in self.sent:
+            copy.wait_send()
+
+
+def turn(value, cosine, sine):
+    lane = lax.broadcasted_iota(jnp.int32, value.shape, 1)
+    swapped = jnp.where(
+        lane < HEAD_DIM // 2,
+        pltpu.roll(value, BLK - HEAD_DIM // 2, 1),
+        pltpu.roll(value, HEAD_DIM // 2, 1),
+    )
+    return value * cosine + swapped * sine
+
+
+def head_rows(first, count, low):
+    for row in range(first, first + count, 8):
+        yield row - first, (row // HEAD_DIM) * BLK + row % HEAD_DIM + (0 if low else HEAD_DIM)
+
+
+def forward_kernel(
+    tokens_ref, cotangent_ref, condition_ref, ada_ref, rows_ref, chunk_ref, mlp_e_ref, mlp_r_ref,
+    cos_hbm, sin_hbm,
+    mods_ref, attn_ref, mixed_ref, query_ref, kv_ref, att_ref, logt_ref, weight_ref,
+    cot_ref, expand_ref, reduce_ref, cos_ref, sin_ref,
+    vec_own, vecs, chunks, tok, mod_row, gain_rows, state_m, state_l, acc, part_send, part_recv,
+    vec_ss, vec_rs, chunk_ss, chunk_rs, local_sem, tok_ss, tok_rs, cot_ss, cot_rs,
+    a_ss, a_rs, e_ss, e_rs, r_ss, r_rs, kv_ss, kv_rs, part_ss, part_rs,
+):
+    rows = tokens_ref.shape[0]
+    width = tokens_ref.shape[1]
+    heads = query_ref.shape[1] // BLK
+    me = flat(peer(0))
+    tables = []
+    for slot in range(4):
+        start = pl.multiple_of(peer(TP[slot])[1] * rows, rows)
+        for which, (source, target) in enumerate(((cos_hbm, cos_ref), (sin_hbm, sin_ref))):
+            copy = pltpu.make_async_copy(
+                source.at[pl.ds(start, rows)],
+                target.at[pl.ds(slot * rows, rows)],
+                local_sem.at[4 + slot * 2 + which],
+            )
+            copy.start()
+            tables.append(copy)
+    piece = jnp.sum(condition_ref[...] * ada_ref[...].astype(f32), axis=0, keepdims=True)
+    vec_own[...] = rows_ref[...]
+    vec_own[0:1, 0 : ada_ref.shape[1]] += piece
+    mod_shift = (me % 8) * 16
+    gain_shift = ((3 * me) % 16) * 8
+    vec_own[0:8, :] = pltpu.roll(vec_own[0:8, :], mod_shift, 1)
+    vec_own[8:16, :] = pltpu.roll(vec_own[8:16, :], gain_shift, 1)
+    vec_own[16:24, :] = pltpu.roll(vec_own[16:24, :], gain_shift, 1)
+    vec_own[24:32, :] = pltpu.roll(vec_own[24:32, :], gain_shift, 1)
+    for index in range(1, 4):
+        vec_own[index : index + 1, :] = vec_own[8 * index : 8 * index + 1, :]
+    vecs[me] = vec_own[0:8, :]
+    tok[0] = tokens_ref[...]
+    cot_ref[0] = cotangent_ref[...]
+    own = share(0)
+    expand_ref[own] = mlp_e_ref[...]
+    reduce_ref[own] = mlp_r_ref[...]
+
+    enter(range(1, 32))
+
+    targets = []
+    for index in range(4):
+        if index < 3:
+            number = 3 * me + index
+            part, place_in = number // 32, number % 32
+        else:
+            part, place_in = 3, me
+        rank, slot = place_in // 8, place_in % 8
+        device = (
+            (slot // 2) % 2,
+            (slot // 4) * 8 + (rank // 2) * 4 + (rank % 2) * 2 + slot % 2,
+        )
+        targets.append((part, slot, device, flat(device) == me))
+
+    def chunk_copies(index):
+        part, slot, device, stays = targets[index]
+        far = pltpu.make_async_remote_copy(
+            src_ref=chunk_ref.at[index],
+            dst_ref=chunks.at[slot, part],
+            send_sem=chunk_ss.at[index],
+            recv_sem=chunk_rs.at[index],
+            device_id=device,
+            device_id_type=MESH,
+        )
+        near = pltpu.make_async_copy(
+            chunk_ref.at[index], chunks.at[slot, part], local_sem.at[index]
+        )
+        return far, near, stays
+
+    for index in range(4):
+        far, near, stays = chunk_copies(index)
+
+        @pl.when(jnp.logical_not(stays))
+        def _():
+            far.start()
+
+        @pl.when(stays)
+        def _():
+            near.start()
+
+    def vec_copy(offset):
+        return pltpu.make_async_remote_copy(
+            src_ref=vecs.at[me],
+            dst_ref=vecs.at[me],
+            send_sem=vec_ss.at[offset],
+            recv_sem=vec_rs.at[offset],
+            device_id=peer_loop(offset),
+            device_id_type=MESH,
+        )
+
+    @pl.loop(1, 32)
+    def _(offset):
+        vec_copy(offset).start()
+
+    token_copies = [
+        remote(tok.at[0], tok.at[slot], tok_ss.at[slot], tok_rs.at[slot], TP[slot])
+        for slot in range(1, 4)
+    ]
+    for copy in token_copies:
+        copy.start()
+
+    for index in range(4):
+        far, near, stays = chunk_copies(index)
+
+        @pl.when(jnp.logical_not(stays))
+        def _():
+            far.wait()
+
+        @pl.when(stays)
+        def _():
+            near.wait()
+
+    gather_a = Gather(chunks, a_ss, a_rs)
+    gather_e = Gather(expand_ref, e_ss, e_rs)
+    gather_r = Gather(reduce_ref, r_ss, r_rs)
+    gather_a.first()
+
+    @pl.loop(1, 32)
+    def _(offset):
+        other = flat(peer_loop(offset))
+        copy = pltpu.make_async_remote_copy(
+            src_ref=vecs.at[other],
+            dst_ref=vecs.at[other],
+            send_sem=vec_ss.at[offset],
+            recv_sem=vec_rs.at[offset],
+            device_id=peer_loop(offset),
+            device_id_type=MESH,
+        )
+        copy.wait()
+
+    mod_row[...] = jnp.zeros_like(mod_row)
+    gain_rows[...] = jnp.zeros_like(gain_rows)
+    for index in range(32):
+        tile = (9 * index) // 8 * BLK
+        mod_row[0:1, tile : tile + 2 * BLK] += vecs[index, 0:1, :]
+        tile = (3 * index) // 16 * BLK
+        gain_rows[0:8, tile : tile + 2 * BLK] += vecs[index]
+    for index in range(6):
+        mods_ref[index : index + 1, :] = mod_row[0:1, index * width : (index + 1) * width]
+    for index in range(3):
+        mods_ref[6 + index : 7 + index, :] = gain_rows[index + 1 : index + 2, 0:width]
+    mods_ref[9:16, :] = jnp.zeros((7, width), f32)
+
+    shift_one = mods_ref[0:1, :]
+    gain_first = mods_ref[6:7, :] * (1.0 + mods_ref[1:2, :])
+    gather_a.second()
+    for slot in range(4):
+        if slot:
+            token_copies[slot - 1].wait()
+        normed, _unused = layer_norm(tok[slot].astype(f32))
+        mixed_ref[slot * rows : (slot + 1) * rows, :] = (normed * gain_first + shift_one).astype(
+            bf16
+        )
+    gather_a.third()
+    cot_copies = [
+        remote(cot_ref.at[0], cot_ref.at[slot], cot_ss.at[slot], cot_rs.at[slot], TP[slot])
+        for slot in range(1, 4)
+    ]
+    for copy in cot_copies:
+        copy.start()
+    gather_e.first()
+    gather_r.first()
+    gather_a.last()
+    zero = jnp.zeros((HEAD_DIM, width), bf16)
+    half = heads * BLK
+    for head in range(heads):
+        weight_ref[head * BLK + HEAD_DIM : (head + 1) * BLK, :] = zero
+        weight_ref[2 * half + head * BLK : 2 * half + head * BLK + HEAD_DIM, :] = zero
+    count = chunks.shape[2]
+    for slot in range(8):
+        for part, base, low in ((0, 0, True), (1, half, True), (2, half, False), (3, 2 * half, False)):
+            for row, target in head_rows(slot * count, count, low):
+                weight_ref[base + target : base + target + 8, :] = chunks[slot, part, row : row + 8, :]
+
+    for copy in tables:
+        copy.wait()
+
+    @pl.loop(0, 4)
+    def _(slot):
+        here = pl.ds(pl.multiple_of(slot * rows, rows), rows)
+        mixed = mixed_ref[here, :]
+        cosine, sine = cos_ref[here, :], sin_ref[here, :]
+        for head in range(heads):
+            lanes = slice(head * BLK, (head + 1) * BLK)
+            query = dot_nt(mixed, weight_ref[lanes, :]).astype(bf16).astype(f32)
+            query_ref[here, lanes] = (
+                turn(query, cosine, sine).astype(bf16).astype(f32) * (HEAD_DIM ** (-0.5))
+            ).astype(bf16)
+            both = dot_nt(mixed, weight_ref[half + head * BLK : half + (head + 1) * BLK, :])
+            kv_ref[0, here, lanes] = turn(both.astype(bf16).astype(f32), cosine, sine).astype(bf16)
+
+    kv_copies = [
+        remote(kv_ref.at[0], kv_ref.at[2], kv_ss.at[0], kv_rs.at[2], ZH),
+        remote(kv_ref.at[0], kv_ref.at[1], kv_ss.at[1], kv_rs.at[1], C),
+    ]
+    for copy in kv_copies:
+        copy.start()
+
+    state_m[...] = jnp.full_like(state_m, -1e30)
+    state_l[...] = jnp.zeros_like(state_l)
+    acc[...] = jnp.zeros_like(acc)
+
+    def attend(slot):
+        @pl.loop(0, heads)
+        def _(head):
+            lanes = pl.ds(pl.multiple_of(head * BLK, BLK), BLK)
+            keys = kv_ref[slot, :, lanes]
+            scores = dot_nt(keys, query_ref[:, lanes])
+            before = state_m[head]
+            maximum = jnp.maximum(before, jnp.max(scores, axis=0, keepdims=True))
+            weights = jnp.exp(scores - maximum)
+            factor = jnp.exp(before - maximum)
+            state_m[head] = maximum
+            state_l[head] = state_l[head] * factor + jnp.sum(weights, axis=0, keepdims=True)
+            acc[head] = acc[head] * factor + dot_tn(keys, weights.astype(bf16))
+
+    attend(0)
+    kv_copies[1].wait_recv()
+    attend(1)
+    kv_copies[0].wait_recv()
+    forwarded = remote(kv_ref.at[2], kv_ref.at[3], kv_ss.at[2], kv_rs.at[3], C)
+    forwarded.start()
+    attend(2)
+    forwarded.wait_recv()
+    attend(3)
+    gather_e.second()
+    gather_r.second()
+
+    row = lax.broadcasted_iota(jnp.int32, (BLK, acc.shape[2]), 0)
+    for head in range(heads):
+        value = jnp.where(row < HEAD_DIM, 0.0, acc[head] / state_l[head])
+        att_ref[head * BLK : (head + 1) * BLK, :] = value.astype(bf16)
+        logt_ref[head] = state_m[head] + jnp.log(state_l[head])
+
+    part_copies = []
+    for slot in (3, 2, 1, 0):
+        here = slice(slot * rows, (slot + 1) * rows)
+        partial_sum = dot_tn(att_ref[:, here], weight_ref[2 * half : 3 * half, :])
+        if slot:
+            part_send[slot - 1] = partial_sum.astype(bf16)
+            copy = remote(
+                part_send.at[slot - 1], part_recv.at[slot - 1],
+                part_ss.at[slot], part_rs.at[slot], TP[slot],
+            )
+            copy.start()
+            part_copies.append(copy)
+        else:
+            attn_ref[...] = partial_sum
+    gather_e.third()
+    gather_r.third()
+    for copy in part_copies:
+        copy.wait()
+    attn_ref[...] += (
+        part_recv[0].astype(f32) + part_recv[1].astype(f32) + part_recv[2].astype(f32)
+    )
+    gather_e.last()
+    gather_r.last()
+    for copy in kv_copies:
+        copy.wait_send()
+    forwarded.wait_send()
+    for copy in cot_copies:
+        copy.wait()
+
+
+def gelu_pair(hidden):
+    scale = math.sqrt(2.0 / math.pi)
+    square = hidden * hidden
+    bend = jnp.tanh(scale * hidden * (1.0 + 0.044715 * square))
+    half = 0.5 * (1.0 + bend)
+    slope = half + 0.5 * hidden * (1.0 - bend * bend) * (
+        scale * (1.0 + 3.0 * 0.044715 * square)
+    )
+    return hidden * half, slope
+
+
+def mlp_kernel(
+    tokens_ref, mods_ref, attn_ref, cot_ref, expand_in, reduce_in,
+    mlp_ref, gm_ref, middle_ref, expand_grad, reduce_grad,
+    expand_ref, reduce_ref, mix, branch, active, grad_hid, mlp_send, mlp_recv, gm_send, gm_recv,
+    mix_ss, mix_rs, mlp_ss, mlp_rs, gm_ss, gm_rs,
+):
+    rows, width = tokens_ref.shape
+    units = expand_ref.shape[0]
+    per = units // 8
+    enter(TP[1:])
+    gate_one, shift_two, scale_two, gate_two = (
+        mods_ref[index : index + 1, :] for index in (2, 3, 4, 5)
+    )
+    middle = tokens_ref[...].astype(f32) + gate_one * attn_ref[...]
+    middle_ref[...] = middle
+    normed, _unused = layer_norm(middle)
+    gain = mods_ref[7:8, :] * (1.0 + scale_two)
+    mixed = (normed * gain + shift_two).astype(bf16)
+    lane = lax.broadcasted_iota(jnp.int32, (rows, BLK), 1)
+    ones = jnp.where(lane == 0, 1.0, 0.0).astype(bf16)
+    for slot in range(4):
+        mix[slot, :, width:] = ones
+    mix[0, :, :width] = mixed
+    mix_copies = [
+        remote(
+            mix.at[0, :, pl.ds(0, width)], mix.at[slot, :, pl.ds(0, width)],
+            mix_ss.at[slot], mix_rs.at[slot], TP[slot],
+        )
+        for slot in range(1, 4)
+    ]
+    for copy in mix_copies:
+        copy.start()
+    for index in range(8):
+        expand_ref[index * per : (index + 1) * per, :] = expand_in[index]
+        reduce_ref[index * per : (index + 1) * per, :] = reduce_in[index]
+
+    copies = []
+    for slot in range(4):
+        here = slice(slot * rows, (slot + 1) * rows)
+        if slot:
+            mix_copies[slot - 1].wait_recv()
+        grad_branch = (gate_two * cot_ref[slot].astype(f32)).astype(bf16)
+        branch[here, :] = grad_branch
+        hidden = dot_nt(mix[slot], expand_ref[...])
+        activated, slope = gelu_pair(hidden)
+        activated = activated.astype(bf16)
+        active[here, :] = activated
+        grad_hidden = (dot_nt(grad_branch, reduce_ref[...]) * slope).astype(bf16)
+        grad_hid[here, :] = grad_hidden
+        gm_part = dot_nn(grad_hidden, expand_ref[:, :width])
+        mlp_part = dot_nn(activated, reduce_ref[...])
+        if slot:
+            gm_send[slot - 1] = gm_part.astype(bf16)
+            mlp_send[slot - 1] = mlp_part.astype(bf16)
+            for source, target, ss, rs in (
+                (gm_send, gm_recv, gm_ss, gm_rs), (mlp_send, mlp_recv, mlp_ss, mlp_rs),
+            ):
+                copy = remote(
+                    source.at[slot - 1], target.at[slot - 1], ss.at[slot], rs.at[slot], TP[slot]
+                )
+                copy.start()
+                copies.append(copy)
+        else:
+            gm_ref[...] = gm_part
+            mlp_ref[...] = mlp_part + mods_ref[8:9, :]
+
+    @pl.loop(0, units // BLK)
+    def _(index):
+        lanes = pl.ds(pl.multiple_of(index * BLK, BLK), BLK)
+        grad_reduce = dot_tn(active[:, lanes], branch[...])
+        reduce_grad[lanes, :] = grad_reduce.astype(bf16)
+        left = grad_hid[:, lanes]
+        total = dot_tn(left, mix[0:4].reshape(4 * rows, width + BLK))
+        expand_grad[lanes, :] = total.astype(bf16)
+
+    for copy in mix_copies:
+        copy.wait_send()
+    for copy in copies:
+        copy.wait()
+    for slot in range(3):
+        gm_ref[...] += gm_recv[slot].astype(f32)
+        mlp_ref[...] += mlp_recv[slot].astype(f32)
+
+
+class Scatter:
+    def __init__(self, blocks, from_core, from_y, from_z, send_sem, recv_sem):
+        self.blocks, self.send_sem, self.recv_sem = blocks, send_sem, recv_sem
+        self.place = {C: from_core, Y: from_y, ZH: from_z}
+        self.base = {C: 0, Y: 4, ZH: 6}
+        self.sent = []
+
+    def step(self, to, kept):
+        copies = []
+        for index, offset in enumerate(kept):
+            number = self.base[to] + index
+            copy = remote(
+                self.blocks.at[share(offset + to)], self.place[to].at[index],
+                self.send_sem.at[number], self.recv_sem.at[number], to,
+            )
+            copy.start()
+            copies.append(copy)
+        self.sent.append((to, kept, copies))
+
+    def add(self):
+        to, kept, copies = self.sent[-1]
+        for index, offset in enumerate(kept):
+            copies[index].wait_recv()
+            slot = share(offset)
+            self.blocks[slot] = (
+                self.blocks[slot].astype(f32) + self.place[to][index].astype(f32)
+            ).astype(bf16)
+
+    def finish(self):
+        for _to, _kept, copies in self.sent:
+            for copy in copies:
+                copy.wait_send()
+
+
+KEPT = ((C, (0, Y, ZH, Y + ZH)), (Y, (0, ZH)), (ZH, (0,)))
+
+
+def column_sum(value):
+    return jnp.sum(value, axis=0, keepdims=True)
+
+
+def backward_kernel(
+    tokens_ref, cotangent_ref, mods_ref, attn_ref, middle_ref, mlp_ref, gm_ref,
+    mixed_ref, query_ref, kv_ref, att_ref, logt_ref, weight_ref, cos_ref, sin_ref,
+    expand_in, reduce_in, condition_ref, ada_ref,
+    result_ref, gtok_ref, gcond_ref, gvec_ref, gexp_ref, gred_ref, gchunk_ref,
+    gattn, dout, dout_t, rdots, dq, dkv, dkv_send, dkv_recv, dqkv, part_send, part_recv,
+    gmid, blocks_e, blocks_r, blocks_a, wide, from_e, from_r, from_a, from_e2, from_r2, from_a2,
+    from_e3, from_r3, from_a3, rowsum, vec_send, vec_recv, cond_send, cond_recv, chunk_send,
+    chunk_recv,
+    ga_ss, ga_rs, dkv_ss, dkv_rs, part_ss, part_rs, e_ss, e_rs, r_ss, r_rs, a_ss, a_rs,
+    vec_ss, vec_rs, cond_ss, cond_rs, chunk_ss, chunk_rs, local_sem,
+):
+    rows, width = tokens_ref.shape
+    heads = query_ref.shape[1] // BLK
+    half = heads * BLK
+    per = expand_in.shape[0] // 8
+    me = flat(peer(0))
+    enter(range(1, 32))
+    shift_one, scale_one, gate_one, shift_two, scale_two, gate_two, gain_one, gain_two = (
+        mods_ref[index : index + 1, :] for index in range(8)
+    )
+    cot = cotangent_ref[...].astype(f32)
+    middle = middle_ref[...]
+    mlp_branch = mlp_ref[...]
+    grad_mixed = gm_ref[...]
+    normed, inverse = layer_norm(middle)
+    gain = gain_two * (1.0 + scale_two)
+    grad_middle = cot + norm_back(grad_mixed * gain, normed, inverse)
+    gmid[...] = grad_middle
+    gattn[0] = (gate_one * grad_middle).astype(bf16)
+    ga_copies = [
+        remote(gattn.at[0], gattn.at[slot], ga_ss.at[slot], ga_rs.at[slot], TP[slot])
+        for slot in range(1, 4)
+    ]
+    for copy in ga_copies:
+        copy.start()
+    for index in range(8):
+        here = slice(index * per, (index + 1) * per)
+        blocks_e[index] = expand_in[here, :]
+        blocks_r[index] = reduce_in[here, :]
+    scatter_e = Scatter(blocks_e, from_e, from_e2, from_e3, e_ss, e_rs)
+    scatter_r = Scatter(blocks_r, from_r, from_r2, from_r3, r_ss, r_rs)
+    scatter_e.step(*KEPT[0])
+    scatter_r.step(*KEPT[0])
+    result_ref[...] = (middle + gate_two * mlp_branch).astype(bf16)
+    weighted = column_sum(grad_mixed * normed)
+    rowsum[2:3, :] = column_sum(grad_middle * attn_ref[...])
+    rowsum[3:4, :] = column_sum(grad_mixed)
+    rowsum[4:5, :] = weighted * gain_two
+    rowsum[5:6, :] = column_sum(cot * mlp_branch)
+    rowsum[7:8, :] = weighted * (1.0 + scale_two)
+    rowsum[8:9, :] = column_sum((gate_two * cot).astype(bf16).astype(f32))
+
+    for slot in range(4):
+        if slot:
+            ga_copies[slot - 1].wait_recv()
+        here = slice(slot * rows, (slot + 1) * rows)
+        values = dot_nt(gattn[slot], weight_ref[2 * half :, :]).astype(bf16).astype(f32)
+        dout[here, :] = values.astype(bf16)
+        for head in range(heads):
+            lanes = slice(head * BLK, (head + 1) * BLK)
+            turned = values[:, lanes].T
+            dout_t[lanes, here] = turned.astype(bf16)
+            rdots[head, :, here] = column_sum(turned * att_ref[lanes, here].astype(f32))
+    scatter_e.add()
+    scatter_r.add()
+    scatter_e.step(*KEPT[1])
+    scatter_r.step(*KEPT[1])
+
+    dq[...] = jnp.zeros_like(dq)
+
+    def back(slot):
+        @pl.loop(0, heads)
+        def _(head):
+            lanes = pl.ds(pl.multiple_of(head * BLK, BLK), BLK)
+            keys = kv_ref[slot, :, lanes]
+            query = query_ref[:, lanes]
+            shares = jnp.exp(dot_nt(keys, query) - logt_ref[head])
+            grad_shares = dot_nn(keys, dout_t[lanes, :])
+            grad_scores = (shares * (grad_shares - rdots[head])).astype(bf16)
+            dkv[:, lanes] = dot_nn(grad_scores, query) + dot_nn(
+                shares.astype(bf16), dout[:, lanes]
+            )
+            dq[head] += dot_tn(keys, grad_scores)
+
+    dkv_copies = []
+
+    def dkv_copy(index, offset):
+        copy = remote(
+            dkv_send.at[index], dkv_recv.at[index], dkv_ss.at[index], dkv_rs.at[index], offset
+        )
+        copy.start()
+        dkv_copies.append(copy)
+
+    back(3)
+    dkv_send[0] = dkv[...].astype(bf16)
+    dkv_copy(0, C)
+    back(2)
+    dkv_copies[0].wait_recv()
+    dkv_send[1] = (dkv[...] + dkv_recv[0].astype(f32)).astype(bf16)
+    dkv_copy(1, ZH)
+    back(1)
+    dkv_send[2] = dkv[...].astype(bf16)
+    dkv_copy(2, C)
+    back(0)
+    count = blocks_a.shape[2]
+
+    def spread(part, base, low):
+        for slot in range(8):
+            for row, target in head_rows(slot * count, count, low):
+                blocks_a[slot, part, row : row + 8, :] = wide[
+                    base + target : base + target + 8, :
+                ].astype(bf16)
+
+    @pl.loop(0, heads)
+    def _(head):
+        lanes = pl.ds(pl.multiple_of(head * BLK, BLK), BLK)
+        wide[lanes, :] = dot_nn(att_ref[lanes, :], gattn[0:4].reshape(4 * rows, width))
+
+    spread(3, 0, False)
+    scatter_e.add()
+    scatter_r.add()
+    scatter_e.step(*KEPT[2])
+    scatter_r.step(*KEPT[2])
+    for head in range(heads):
+        lanes = slice(head * BLK, (head + 1) * BLK)
+        value = dq[head].T * (HEAD_DIM ** (-0.5))
+        dqkv[:, lanes] = turn(value, cos_ref[...], -sin_ref[...]).astype(bf16)
+    dkv_copies[2].wait_recv()
+    dkv[...] += dkv_recv[2].astype(f32)
+    dkv_copies[1].wait_recv()
+    for head in range(heads):
+        lanes = slice(head * BLK, (head + 1) * BLK)
+        value = dkv[:, lanes] + dkv_recv[1, :, lanes].astype(f32)
+        dqkv[:, half + head * BLK : half + (head + 1) * BLK] = turn(
+            value, cos_ref[...], -sin_ref[...]
+        ).astype(bf16)
+
+    part_copies = []
+    for slot in (3, 2, 1, 0):
+        here = slice(slot * rows, (slot + 1) * rows)
+        partial_sum = dot_nn(dqkv[here, :], weight_ref[0 : 2 * half, :])
+        if slot:
+            part_send[slot - 1] = partial_sum.astype(bf16)
+            copy = remote(
+                part_send.at[slot - 1], part_recv.at[slot - 1],
+                part_ss.at[slot], part_rs.at[slot], TP[slot],
+            )
+            copy.start()
+            part_copies.append(copy)
+        else:
+            gtok_ref[...] = partial_sum
+
+    @pl.loop(0, 2 * heads)
+    def _(head):
+        lanes = pl.ds(pl.multiple_of(head * BLK, BLK), BLK)
+        wide[lanes, :] = dot_tn(dqkv[:, lanes], mixed_ref[...])
+
+    spread(0, 0, True)
+    spread(1, half, True)
+    spread(2, half, False)
+    scatter_a = Scatter(blocks_a, from_a, from_a2, from_a3, a_ss, a_rs)
+    scatter_a.step(*KEPT[0])
+    for copy in part_copies:
+        copy.wait()
+    grad_mixed_one = (
+        gtok_ref[...]
+        + part_recv[0].astype(f32) + part_recv[1].astype(f32) + part_recv[2].astype(f32)
+    )
+    scatter_a.add()
+    scatter_a.step(*KEPT[1])
+    normed_one, inverse_one = layer_norm(tokens_ref[...].astype(f32))
+    gain_first = gain_one * (1.0 + scale_one)
+    gtok_ref[...] = gmid[...] + norm_back(grad_mixed_one * gain_first, normed_one, inverse_one)
+    weighted = column_sum(grad_mixed_one * normed_one)
+    rowsum[0:1, :] = column_sum(grad_mixed_one)
+    rowsum[1:2, :] = weighted * gain_one
+    rowsum[6:7, :] = weighted * (1.0 + scale_one)
+    vec_send[...] = jnp.zeros_like(vec_send)
+    tiles = width // BLK
+    for owner in range(32):
+        for tile in range(2):
+            at = (9 * owner) // 8 + tile
+            vec_send[owner, 0:1, tile * BLK : (tile + 1) * BLK] = rowsum[
+                at // tiles : at // tiles + 1, (at % tiles) * BLK : (at % tiles + 1) * BLK
+            ]
+            at = (3 * owner) // 16 + tile
+            if at < tiles:
+                vec_send[owner, 1:4, tile * BLK : (tile + 1) * BLK] = rowsum[
+                    6:9, at * BLK : (at + 1) * BLK
+                ]
+
+    def vec_copy(offset):
+        return pltpu.make_async_remote_copy(
+            src_ref=vec_send.at[flat(peer_loop(offset))],
+            dst_ref=vec_recv.at[offset],
+            send_sem=vec_ss.at[offset],
+            recv_sem=vec_rs.at[offset],
+            device_id=peer_loop(offset),
+            device_id_type=MESH,
+        )
+
+    @pl.loop(1, 32)
+    def _(offset):
+        vec_copy(offset).start()
+
+    scatter_e.add()
+    scatter_r.add()
+    own = share(0)
+    gexp_ref[...] = blocks_e[own].astype(f32)
+    gred_ref[...] = blocks_r[own].astype(f32)
+    scatter_a.add()
+    scatter_a.step(*KEPT[2])
+    vec_recv[0] = vec_send[me]
+
+    @pl.loop(1, 32)
+    def _(offset):
+        vec_copy(offset).wait()
+
+    total = jnp.zeros(vec_recv.shape[1:], f32)
+    for index in range(32):
+        total = total + vec_recv[index]
+    mod_shift = (me % 8) * 16
+    gain_shift = ((3 * me) % 16) * 8
+    gvec_ref[0:8, :] = pltpu.roll(total, (256 - mod_shift) % 256, 1)
+    gvec_ref[8:16, :] = pltpu.roll(total, (256 - gain_shift) % 256, 1)
+    piece = ada_ref.shape[1]
+    cond_send[...] = lax.dot_general(
+        gvec_ref[0:8, 0:piece], ada_ref[...].astype(f32), (((1,), (1,)), ((), ())),
+        preferred_element_type=f32, precision=highest,
+    )
+
+    def cond_copy(offset):
+        return pltpu.make_async_remote_copy(
+            src_ref=cond_send.at[pl.ds(0, 1)],
+            dst_ref=cond_recv.at[offset],
+            send_sem=cond_ss.at[offset],
+            recv_sem=cond_rs.at[offset],
+            device_id=peer_loop(offset),
+            device_id_type=MESH,
+        )
+
+    @pl.loop(1, 32)
+    def _(offset):
+        cond_copy(offset).start()
+
+    scatter_a.add()
+    chunk_send[...] = blocks_a[own]
+    place_in = 8 * ((me // 4) % 2 * 2 + (me // 2) % 2) + own
+
+    def chunk_copies(part):
+        if part < 3:
+            number = 32 * part + place_in
+            owner, slot = number // 3, number % 3
+        else:
+            owner, slot = place_in, 3
+        stays = owner == me
+        far = pltpu.make_async_remote_copy(
+            src_ref=chunk_send.at[part], dst_ref=chunk_recv.at[slot],
+            send_sem=chunk_ss.at[part], recv_sem=chunk_rs.at[slot],
+            device_id=(owner // 16, owner % 16), device_id_type=MESH,
+        )
+        near = pltpu.make_async_copy(
+            chunk_send.at[part], chunk_recv.at[slot], local_sem.at[part]
+        )
+        return far, near, stays
+
+    for part in range(4):
+        far, near, stays = chunk_copies(part)
+
+        @pl.when(jnp.logical_not(stays))
+        def _():
+            far.start()
+
+        @pl.when(stays)
+        def _():
+            near.start()
+
+    @pl.loop(1, 32)
+    def _(offset):
+        cond_copy(offset).wait()
+
+    cond_recv[0] = cond_send[0:1, :]
+    gradient = jnp.zeros((1, BLK), f32)
+    for index in range(32):
+        gradient = gradient + cond_recv[index]
+    gcond_ref[...] = gradient
+
+    for part in range(4):
+        far, near, stays = chunk_copies(part)
+
+        @pl.when(jnp.logical_not(stays))
+        def _():
+            far.wait_send()
+
+        @pl.when(stays)
+        def _():
+            near.wait()
+
+    for slot in range(4):
+        if slot < 3:
+            number = 3 * me + slot
+            part, place_of = number // 32, number % 32
+        else:
+            part, place_of = 3, me
+        rank, dp = place_of // 8, place_of % 8
+        keeper = ((dp // 2) % 2) * 16 + (dp // 4) * 8 + (rank // 2) * 4 + (rank % 2) * 2 + dp % 2
+
+        @pl.when(keeper != me)
+        def _():
+            pltpu.make_async_remote_copy(
+                src_ref=chunk_send.at[slot], dst_ref=chunk_recv.at[slot],
+                send_sem=chunk_ss.at[slot], recv_sem=chunk_rs.at[slot],
+                device_id=(keeper // 16, keeper % 16), device_id_type=MESH,
+            ).wait_recv()
+
+    gchunk_ref[...] = chunk_recv[...].astype(f32)
+    for copy in ga_copies:
+        copy.wait_send()
+    for copy in dkv_copies:
+        copy.wait_send()
+    scatter_e.finish()
+    scatter_r.finish()
+    scatter_a.finish()
+
+
+def rotary_blocks(length):
+    half_dim = HEAD_DIM // 2
+    frequency = np.exp(
+        np.arange(half_dim, dtype=np.float32) * np.float32(-2.0 * math.log(10000.0) / HEAD_DIM)
+    ).astype(np.float32)
+    angles = (np.arange(length, dtype=np.float32)[:, None] * frequency[None, :]).astype(np.float32)
+    cosine, sine = np.cos(angles.astype(np.float64)), np.sin(angles.astype(np.float64))
+    one, zero = np.ones((length, HEAD_DIM)), np.zeros((length, HEAD_DIM))
+    return (
+        np.concatenate([cosine, cosine, one], axis=1).astype(np.float32),
+        np.concatenate([-sine, sine, zero], axis=1).astype(np.float32),
+    )
+
+
+def vmem(*shape, kind=jnp.bfloat16):
+    return pltpu.VMEM(shape, kind)
+
+
+def dma(*count):
+    return pltpu.SemaphoreType.DMA(count)
+
+
+def call(body, outs, scratch, number, operands, hbm=()):
+    whole = pl.BlockSpec(memory_space=pltpu.VMEM)
+    return pl.pallas_call(
+        body,
+        out_shape=tuple(jax.ShapeDtypeStruct(shape, kind) for shape, kind in outs),
+        in_specs=[
+            pl.BlockSpec(memory_space=pl.ANY) if index in hbm else whole
+            for index in range(len(operands))
+        ],
+        out_specs=tuple(whole for _ in outs),
+        scratch_shapes=scratch,
+        compiler_params=pltpu.CompilerParams(
+            collective_id=number, has_side_effects=True, vmem_limit_bytes=60 * 2**20
+        ),
+    )(*operands)
+
+
+def on_device_fast(
+    tokens, condition, ada_weight, ada_bias, first_gain, second_gain, project_weight,
+    output_weight, expand_weight, expand_bias, reduce_weight, reduce_bias, cotangent,
+):
+    rows, width = tokens.shape
+    cycle = lax.axis_size("blk")
+    group = 4 * rows
+    heads = width // HEAD_DIM // 4
+    half = heads * BLK
+    per = reduce_weight.shape[0]
+    units = 8 * per
+    count = output_weight.shape[0]
+    piece = ada_weight.shape[1]
+
+    def line(value):
+        return jnp.pad(value.astype(f32)[None, :], ((0, 7), (0, 256 - value.shape[0])))
+
+    lines = jnp.concatenate(
+        [line(ada_bias), line(first_gain), line(second_gain), line(reduce_bias)], axis=0
+    )
+    chunk = jnp.concatenate(
+        [project_weight.T.reshape(3, count, width), output_weight[None]], axis=0
+    )
+    expand_rows = jnp.concatenate(
+        [expand_weight.T, expand_bias[:, None], jnp.zeros((per, BLK - 1), bf16)], axis=1
+    )
+    column = condition[:, None]
+    cosine, sine = (jnp.asarray(table) for table in rotary_blocks(cycle * rows))
+    (
+        mods, attn, mixed, query, kv, att, logt, weight, cot_all, expand_all, reduce_all,
+        cos_rows, sin_rows,
+    ) = call(
+        forward_kernel,
+        [
+            ((16, width), f32), ((rows, width), f32), ((group, width), bf16),
+            ((group, half), bf16), ((4, group, half), bf16), ((half, group), bf16),
+            ((heads, 1, group), f32), ((3 * half, width), bf16), ((4, rows, width), bf16),
+            ((8, per, width + BLK), bf16), ((8, per, width), bf16),
+            ((group, BLK), f32), ((group, BLK), f32),
+        ],
+        [
+            vmem(32, 256, kind=f32), vmem(32, 8, 256, kind=f32), vmem(8, 4, count, width),
+            vmem(4, rows, width), vmem(1, 6 * width, kind=f32), vmem(8, width + BLK, kind=f32),
+            vmem(heads, 1, group, kind=f32), vmem(heads, 1, group, kind=f32),
+            vmem(heads, BLK, group, kind=f32), vmem(3, rows, width), vmem(3, rows, width),
+            dma(32), dma(32), dma(4), dma(4), dma(12), dma(4), dma(4), dma(4), dma(4),
+            dma(8), dma(8), dma(8), dma(8), dma(8), dma(8), dma(4), dma(4), dma(4), dma(4),
+        ],
+        1,
+        (
+            tokens, cotangent, column, ada_weight, lines, chunk, expand_rows, reduce_weight,
+            cosine, sine,
+        ),
+        hbm=(8, 9),
+    )
+    mlp, grad_mixed, middle, expand_grad, reduce_grad = call(
+        mlp_kernel,
+        [
+            ((rows, width), f32), ((rows, width), f32), ((rows, width), f32),
+            ((units, width + BLK), bf16), ((units, width), bf16),
+        ],
+        [
+            vmem(units, width + BLK), vmem(units, width), vmem(4, rows, width + BLK),
+            vmem(group, width), vmem(group, units), vmem(group, units),
+            vmem(3, rows, width), vmem(3, rows, width), vmem(3, rows, width),
+            vmem(3, rows, width),
+            dma(4), dma(4), dma(4), dma(4), dma(4), dma(4),
+        ],
+        2,
+        (tokens, mods, attn, cot_all, expand_all, reduce_all),
+    )
+    result, grad_tokens, grad_condition, grad_vec, grad_expand, grad_reduce, grad_chunk = call(
+        backward_kernel,
+        [
+            ((rows, width), bf16), ((rows, width), f32), ((1, BLK), f32), ((16, 256), f32),
+            ((per, width + BLK), f32), ((per, width), f32), ((4, count, width), f32),
+        ],
+        [
+            vmem(4, rows, width), vmem(group, half), vmem(half, group),
+            vmem(heads, 1, group, kind=f32), vmem(heads, BLK, group, kind=f32),
+            vmem(group, half, kind=f32), vmem(3, group, half), vmem(3, group, half),
+            vmem(group, 2 * half), vmem(3, rows, width), vmem(3, rows, width),
+            vmem(rows, width, kind=f32), vmem(8, per, width + BLK), vmem(8, per, width),
+            vmem(8, 4, count, width), vmem(2 * half, width, kind=f32),
+            vmem(4, per, width + BLK), vmem(4, per, width), vmem(4, 4, count, width),
+            vmem(2, per, width + BLK), vmem(2, per, width), vmem(2, 4, count, width),
+            vmem(1, per, width + BLK), vmem(1, per, width), vmem(1, 4, count, width),
+            vmem(16, width, kind=f32), vmem(32, 8, 256, kind=f32), vmem(32, 8, 256, kind=f32),
+            vmem(8, BLK, kind=f32), vmem(32, 1, BLK, kind=f32), vmem(4, count, width),
+            vmem(4, count, width),
+            dma(4), dma(4), dma(4), dma(4), dma(4), dma(4), dma(7), dma(7), dma(7), dma(7),
+            dma(7), dma(7), dma(32), dma(32), dma(32), dma(32), dma(4), dma(4), dma(4),
+        ],
+        3,
+        (
+            tokens, cotangent, mods, attn, middle, mlp, grad_mixed, mixed, query, kv, att, logt,
+            weight, cos_rows, sin_rows, expand_grad, reduce_grad, column, ada_weight,
+        ),
+    )
+    mod_piece = grad_vec[0, :piece]
+    return (
+        result,
+        grad_tokens,
+        grad_condition.reshape(-1),
+        condition[:, None] * mod_piece[None, :],
+        mod_piece,
+        grad_vec[9, :count],
+        grad_vec[10, :count],
+        grad_chunk[:3].reshape(3 * count, width).T,
+        grad_chunk[3],
+        grad_expand[:, :width].T,
+        grad_expand[:, width],
+        grad_reduce,
+        grad_vec[11, :count],
+    )
+
+
 def solution(mesh):
     return jax.shard_map(
-        on_device,
+        on_device_fast if mesh.shape["ulysses"] * mesh.shape["blk"] == 32 else on_device,
         mesh=mesh,
         in_specs=(
             P(("ulysses", "blk"), None),

time: 1050 us -> 226 us (0.22)
  waiting for transfers between devices: 657 us -> 0 us
  Pallas kernels: 0 us -> 202 us
  blocking collectives: 140 us -> 0 us
  matrix products: 105 us -> 0 us
  local copies, waits for them, and re-layouts: 100 us -> 15.4 us
  between operations: 14.5 us -> 0.72 us
  other arithmetic: 17.9 us -> 5.23 us
    reduce_scatter x4 -> x0, waiting for transfers between devices: 347 us -> none  [the longest x1 141 us: on_device(): lax.psum_scatter(grad_reduce, ('ulysses', 'blk'), scatter_dimension=0, ti...]
    all_gather x9 -> x0, waiting for transfers between devices: 297 us -> none  [the longest x1 62.7 us: on_device(): lax.all_gather(expand_weight, ('ulysses', 'blk'), axis=1, tiled=True)]
    pallas_call x0 -> x3, Pallas kernels: none -> 202 us  [call(): pl.pallas_call(body, out_shape=tuple((jax.ShapeDtypeStruct(shape, kind) f...]
    dot_general x42 -> x0, matrix products: 105 us -> none  [the longest x4 18.5 us: key_step(): jnp.einsum('shqk,sqhd->skhd', grad_scores, query_rows, preferred_element_...]
    dynamic_slice x33 -> x0, local copies, waits for them, and re-layouts: 51.5 us -> none  [the longest x32 51.4 us: over_blocks(): carried, unused = lax.scan(scan_step, carried, stacked + (offsets,))]
    unnamed x1 -> x0, blocking collectives: 40.7 us -> none
    psum x1 -> x0, blocking collectives: 39.4 us -> none  [on_device(): grad_modulation = lax.psum(mod_terms, ('ulysses', 'blk'))]
    all_gather x2 -> x0, blocking collectives: 39.1 us -> none  [the longest x1 21 us: on_device(): lax.all_gather(jnp.transpose(log_total, (0, 2, 1)), 'blk', axis=1, tiled=...]
  transfers between devices with their start and end apart: 15 -> 0, of which waited for: 11 -> 0; matrix products, arithmetic and copies ran while one was open for 19% -> 0% of each run, Pallas kernels for 0% -> 0%
where the time goes in v1:
time: 226 us; the launch traced here: 223 us
  Pallas kernels  202 us (89%)
  local copies, waits for them, and re-layouts  15.4 us (7%)
  other arithmetic  5.23 us (2%)
    pallas_call x3, Pallas kernels, call(): pl.pallas_call(body, out_shape=tuple((jax.ShapeDtypeStruct(shape, kind) f...  202 us

profile of v1, /device:TPU:5, one launch (start us, length us, event | category | flops | bytes accessed | tf_op | source)
XLA Modules:
  0.0 223.2 jit_solution(9248029262369482312)
XLA Ops:
  0.6 0.7 broadcast_in_dim.30
  1.3 0.1 pad.24.clone
  1.4 0.8 copy.33
  2.2 1.3 fusion.8.rows_ref
  3.5 1.5 copy.35.ada_ref
  5.0 1.4 copy.34.condition_ref
  6.4 1.6 maximum_maximum_fusion.mlp_e_ref
  8.0 1.6 pad_maximum_fusion.chunk_ref
  9.6 82.9 %shard_map.246 = (f32[16,768]{1,0:T(8,128)}, f32[128,768]{1,0:T(8,128)}, bf16[512,768]{1,0:T(8,128)(2,1)}, bf16[512,384]{1,0:T(8,128)(2,1)}, bf16[4,512,384]{2,1...) custom-call(bf16[128,768]{1,0:T(8,128)(2,1)} %tokens_ref.5, ...), custom_call_target="tpu_custom_call" | custom-call | tf_op jit(solution)/shard_map/pallas_call | solution.py:1283
  92.5 32.2 %shard_map.247 = (f32[128,768]{1,0:T(8,128)}, f32[128,768]{1,0:T(8,128)}, f32[128,768]{1,0:T(8,128)}, bf16[768,896]{1,0:T(8,128)(2,1)}, bf16[768,768]{1,0:T(8,128)(2,1)}) custom-call(bf16[128,768]{1,0:T(8,128)(2,1)} %tokens_ref.5, f32[16,768]{1,0:T(8,128)} %get-tuple-element.38.mods_ref, f32[128,768]{1,0:T(8,128)} %get-tuple-element.39.attn_ref, ...), custom_call_target="tpu_custom_call" | custom-call | tf_op jit(solution)/shard_map/pallas_call | solution.py:1283
  124.6 0.0 copy-start.4
  124.6 86.7 %shard_map.248 = (bf16[128,768]{1,0:T(8,128)(2,1)}, f32[128,768]{1,0:T(8,128)}, f32[1,128]{1,0:T(1,128)}, f32[16,256]{1,0:T(8,128)}, f32[96,896]{1,0:T(8,128)}, ...) custom-call(bf16[128,768]{1,0:T(8,128)(2,1)} %tokens_ref.5, bf16[128,768]{1,0:T(8,128)(2,1)} %cotangent_ref.3, ...), custom_call_target="tpu_custom_call" | custom-call | tf_op jit(solution)/shard_map/pallas_call | solution.py:1283
  211.4 1.5 slice_reduce_fusion
  212.9 1.7 slice_bitcast_fusion
  214.6 0.7 slice.24
  215.3 1.3 slice_bitcast_fusion.2
  216.6 0.7 broadcast_multiply_fusion
  217.4 1.5 slice_bitcast_fusion.1
  218.9 1.6 slice.27
  220.5 0.0 copy-done.2
  220.5 0.7 copy.42
  221.2 0.7 copy.43
  222.0 0.5 copy.44
  222.5 0.7 copy.45
  (11 shorter events, 0.0 us)
Async XLA Ops:
  124.6 92.0 %copy-start.4 = (f32[128]{0:T(128)S(1)}, f32[128]{0:T(128)}, u32[]{:S(2)}) copy-start(f32[128]{0:T(128)} %param.16) | copy-start | bytes 1540
  211.4 9.1 %copy-start.2 = (bf16[128,768]{1,0:T(8,128)(2,1)S(1)}, bf16[128,768]{1,0:T(8,128)(2,1)}, u32[]{:S(2)}) copy-start(bf16[128,768]{1,0:T(8,128)(2,1)} %get-tuple-element.79) | copy-start | bytes 589828
  211.4 9.8 %copy-start = (f32[128,768]{1,0:T(8,128)S(1)}, f32[128,768]{1,0:T(8,128)}, u32[]{:S(2)}) copy-start(f32[128,768]{1,0:T(8,128)} %get-tuple-element.80) | copy-start | bytes 1179652
  211.4 10.5 %copy-start.5 = (f32[1,128]{1,0:T(1,128)S(1)}, f32[1,128]{1,0:T(1,128)}, u32[]{:S(2)}) copy-start(f32[1,128]{1,0:T(1,128)} %get-tuple-element.58) | copy-start | bytes 1540
  211.4 11.0 %copy-start.1 = (f32[96,768]{1,0:T(8,128)S(1)}, f32[96,768]{1,0:T(8,128)}, u32[]{:S(2)}) copy-start(f32[96,768]{1,0:T(8,128)} %get-tuple-element.90) | copy-start | bytes 884740
  215.3 7.8 %copy-start.3 = (f32[1,144]{1,0:T(1,128)}, f32[1,144]{1,0:T(1,128)S(1)}, u32[]{:S(2)}) copy-start(f32[1,144]{1,0:T(1,128)S(1)} %slice.24) | copy-start | bytes 1732

commit v2 on v0

--- a/solution.py
+++ b/solution.py
@@ -1,9 +1,13 @@
 from functools import partial
 import math
+import types
 
 import jax
 import jax.numpy as jnp
+import numpy as np
 from jax import lax
+from jax.experimental import pallas as pl
+from jax.experimental.pallas import tpu as pltpu
 from jax.sharding import PartitionSpec as P
 
 HEAD_DIM = 64
@@ -393,9 +397,1097 @@
     )
 
 
+MESH = pl.DeviceIdType.MESH
+Y, ZH, ZL, X, C = 16, 8, 4, 2, 1
+TP = (0, X, ZL, X + ZL)
+DP = (0, C, Y, Y + C, ZH, ZH + C, ZH + Y, ZH + Y + C)
+BLK = 128
+f32 = jnp.float32
+bf16 = jnp.bfloat16
+
+
+def place():
+    blk = lax.axis_index("blk")
+    return (lax.axis_index("ulysses"), blk // 8, (blk // 4) % 2, (blk // 2) % 2, blk % 2)
+
+
+def flip(offset):
+    return tuple(
+        1 - bit if (offset // weight) % 2 else bit
+        for bit, weight in zip(place(), (Y, ZH, ZL, X, C))
+    )
+
+
+def device_at(y, zh, zl, x, c):
+    return (y, zh * 8 + zl * 4 + x * 2 + c)
+
+
+def peer(offset):
+    return device_at(*flip(offset))
+
+
+def peer_loop(offset):
+    return device_at(
+        *(
+            (bit + (offset // weight) % 2) % 2
+            for bit, weight in zip(place(), (Y, ZH, ZL, X, C))
+        )
+    )
+
+
+def flat(device):
+    return device[0] * 16 + device[1]
+
+
+def share(offset):
+    y, zh, zl, x, c = flip(offset)
+    return zh * 4 + y * 2 + c
+
+
+def rank(offset):
+    y, zh, zl, x, c = flip(offset)
+    return zl * 2 + x
+
+
+def member(which, slot):
+    return device_at((slot // 2) % 2, slot // 4, which // 2, which % 2, slot % 2)
+
+
+def enter(offsets):
+    barrier = pltpu.get_barrier_semaphore()
+    for offset in offsets:
+        pl.semaphore_signal(barrier, inc=1, device_id=peer(offset), device_id_type=MESH)
+    pl.semaphore_wait(barrier, len(offsets))
+
+
+def remote_to(source, target, send_sem, recv_sem, device):
+    return pltpu.make_async_remote_copy(
+        src_ref=source,
+        dst_ref=target,
+        send_sem=send_sem,
+        recv_sem=recv_sem,
+        device_id=device,
+        device_id_type=MESH,
+    )
+
+
+def remote(source, target, send_sem, recv_sem, offset):
+    return remote_to(source, target, send_sem, recv_sem, peer(offset))
+
+
+def dot_nn(a, b):
+    return jnp.dot(a, b, preferred_element_type=f32)
+
+
+def dot_nt(a, b):
+    return lax.dot_general(a, b, (((1,), (1,)), ((), ())), preferred_element_type=f32)
+
+
+def dot_tn(a, b):
+    return lax.dot_general(a, b, (((0,), (0,)), ((), ())), preferred_element_type=f32)
+
+
+def exact(a, b, contract):
+    return lax.dot_general(
+        a, b, (contract, ((), ())), preferred_element_type=f32, precision=highest
+    )
+
+
+def column_sum(value):
+    return jnp.sum(value, axis=0, keepdims=True)
+
+
+class Gather:
+    def __init__(self, view, send_sem, recv_sem):
+        self.view, self.send_sem, self.recv_sem = view, send_sem, recv_sem
+        self.sent = []
+
+    def send(self, have, to):
+        slot = self.view(share(have))
+        index = len(self.sent)
+        copy = remote(
+            slot, slot, self.send_sem.at[index], self.recv_sem.at[DP.index(have + to)], to
+        )
+        copy.start()
+        self.sent.append(copy)
+
+    def arrive(self, what):
+        slot = self.view(share(what))
+        remote(
+            slot, slot, self.send_sem.at[0], self.recv_sem.at[DP.index(what)], C
+        ).wait_recv()
+
+    def near(self):
+        self.send(0, Y)
+        self.send(0, C)
+
+    def far(self):
+        self.send(0, ZH)
+
+    def second(self):
+        self.arrive(ZH)
+        self.send(ZH, Y)
+        self.send(ZH, C)
+
+    def third(self):
+        self.arrive(Y)
+        self.send(Y, C)
+        self.arrive(ZH + Y)
+        self.send(ZH + Y, C)
+
+    def last(self):
+        for what in (C, Y + C, ZH + C, ZH + Y + C):
+            self.arrive(what)
+
+    def finish(self):
+        for copy in self.sent:
+            copy.wait_send()
+
+
+class Scatter:
+    KEPT = {C: (0, Y, ZH, Y + ZH), Y: (0, ZH), ZH: (0,)}
+
+    def __init__(self, view, inbox, send_sem, recv_sem):
+        self.view, self.inbox = view, inbox
+        self.send_sem, self.recv_sem = send_sem, recv_sem
+        self.base = {C: 0, Y: 4, ZH: 6}
+        self.copies = {}
+
+    def step(self, to):
+        self.copies[to] = []
+        for index, offset in enumerate(self.KEPT[to]):
+            number = self.base[to] + index
+            copy = remote(
+                self.view(share(offset + to)), self.inbox(number),
+                self.send_sem.at[number], self.recv_sem.at[number], to,
+            )
+            copy.start()
+            self.copies[to].append(copy)
+
+    def add(self, to):
+        for index, offset in enumerate(self.KEPT[to]):
+            self.copies[to][index].wait_recv()
+            block = self.view(share(offset))
+            block[...] = (
+                block[...].astype(f32) + self.inbox(self.base[to] + index)[...].astype(f32)
+            ).astype(bf16)
+
+    def finish(self):
+        for copies in self.copies.values():
+            for copy in copies:
+                copy.wait_send()
+
+
+def turn(value, cosine, sine):
+    lane = lax.broadcasted_iota(jnp.int32, value.shape, 1)
+    swapped = jnp.where(
+        lane < HEAD_DIM // 2,
+        pltpu.roll(value, BLK - HEAD_DIM // 2, 1),
+        pltpu.roll(value, HEAD_DIM // 2, 1),
+    )
+    return value * cosine + swapped * sine
+
+
+def head_rows(first, count, low):
+    for row in range(first, first + count, 8):
+        yield row - first, row // HEAD_DIM, row % HEAD_DIM + (0 if low else HEAD_DIM)
+
+
+def gelu_pair(hidden):
+    scale = math.sqrt(2.0 / math.pi)
+    square = hidden * hidden
+    bend = jnp.tanh(scale * hidden * (1.0 + 0.044715 * square))
+    half = 0.5 * (1.0 + bend)
+    slope = half + 0.5 * hidden * (1.0 - bend * bend) * (
+        scale * (1.0 + 3.0 * 0.044715 * square)
+    )
+    return hidden * half, slope
+
+
+def to_column(row):
+    count = row.shape[1]
+    one = lax.broadcasted_iota(jnp.int32, (count, count), 0)
+    two = lax.broadcasted_iota(jnp.int32, (count, count), 1)
+    return jnp.sum(jnp.where(one == two, row, 0.0), axis=1, keepdims=True)
+
+
+def to_row(column):
+    count = column.shape[0]
+    one = lax.broadcasted_iota(jnp.int32, (count, count), 0)
+    two = lax.broadcasted_iota(jnp.int32, (count, count), 1)
+    return jnp.sum(jnp.where(one == two, column, 0.0), axis=0, keepdims=True)
+
+
+def block_kernel(names, *refs):
+    s = types.SimpleNamespace(**dict(zip(names, refs)))
+    rows, width = s.tokens.shape
+    heads = s.query.shape[0]
+    count = s.output_weight.shape[0]
+    per = s.reduce_weight.shape[0]
+    units = 8 * per
+    scale = HEAD_DIM ** (-0.5)
+    me = flat(peer(0))
+    own = share(0)
+    my_rank = rank(0)
+
+    def here(slot):
+        return slice(slot * rows, (slot + 1) * rows)
+
+    tables = []
+    for slot in range(4):
+        start = pl.multiple_of(peer(TP[slot])[1] * rows, rows)
+        for which, (source, target) in enumerate(((s.cos_hbm, s.cos), (s.sin_hbm, s.sin))):
+            copy = pltpu.make_async_copy(
+                source.at[pl.ds(start, rows)],
+                target.at[pl.ds(slot * rows, rows)],
+                s.table_sem.at[slot * 2 + which],
+            )
+            copy.start()
+            tables.append(copy)
+    piece = s.ada.shape[0]
+    s.vec_own[...] = jnp.zeros_like(s.vec_own)
+    s.vec_own[0:8, 0:piece] = exact(
+        jnp.broadcast_to(s.condition[...], (8, s.condition.shape[1])),
+        s.ada[...].astype(f32), ((1,), (1,)),
+    )
+    s.vec_own[0:1, 0:piece] += s.ada_bias[...].astype(f32)
+    for index, ref in enumerate((s.first_gain, s.second_gain, s.reduce_bias)):
+        s.vec_own[8 + index : 9 + index, 0:count] = ref[...].astype(f32)
+    mod_shift = (me % 8) * 16
+    gain_shift = ((3 * me) % 16) * 8
+    s.vecs[me, 0:1, :] = pltpu.roll(s.vec_own[0:8, :], mod_shift, 1)[0:1, :]
+    s.vecs[me, 1:4, :] = pltpu.roll(s.vec_own[8:16, :], gain_shift, 1)[0:3, :]
+    s.cot[0] = s.cotangent[...]
+    s.expand[own, :, 0:width] = s.expand_weight[...]
+    lane = lax.broadcasted_iota(jnp.int32, (per, BLK), 1)
+    s.expand[own, :, width:] = jnp.where(
+        lane == 0, to_column(s.expand_bias[...].astype(f32)), 0.0
+    ).astype(bf16)
+    s.reduce[own] = s.reduce_weight[...]
+    s.outw[me] = s.output_weight[...]
+
+    enter(range(1, 32))
+
+    def chunk_out(index):
+        number = 3 * me + index
+        part, place_in = number // 32, number % 32
+        slot = place_in % 8
+        device = member(place_in // 8, slot)
+        target = s.chunks.at[slot, part]
+        far = remote_to(
+            s.project_weight.at[index], target, s.chunk_ss.at[index], s.chunk_rs.at[index], device
+        )
+        near = pltpu.make_async_copy(s.project_weight.at[index], target, s.local_sem.at[index])
+        return far, near, flat(device) == me
+
+    for index in range(3):
+        far, near, stays = chunk_out(index)
+
+        @pl.when(jnp.logical_not(stays))
+        def _():
+            far.start()
+
+        @pl.when(stays)
+        def _():
+            near.start()
+
+    def vec_copy(offset, device):
+        return remote_to(
+            s.vecs.at[device], s.vecs.at[device], s.vec_ss.at[offset], s.vec_rs.at[offset],
+            peer_loop(offset),
+        )
+
+    @pl.loop(1, 32)
+    def _(offset):
+        vec_copy(offset, me).start()
+
+    token_copies = [
+        remote(s.tokens, s.tok.at[slot], s.tok_ss.at[slot], s.tok_rs.at[slot], TP[slot])
+        for slot in range(1, 4)
+    ]
+    for copy in token_copies:
+        copy.start()
+
+    for index in range(3):
+        far, near, stays = chunk_out(index)
+
+        @pl.when(jnp.logical_not(stays))
+        def _():
+            far.wait()
+
+        @pl.when(stays)
+        def _():
+            near.wait()
+
+    gather_kv = Gather(lambda slot: s.chunks.at[slot, pl.ds(1, 2)], s.akv_ss, s.akv_rs)
+    gather_q = Gather(lambda slot: s.chunks.at[slot, 0], s.aq_ss, s.aq_rs)
+    gather_e = Gather(lambda slot: s.expand.at[slot], s.e_ss, s.e_rs)
+    gather_r = Gather(lambda slot: s.reduce.at[slot], s.r_ss, s.r_rs)
+    gather_kv.far()
+    gather_kv.near()
+    gather_q.far()
+    gather_q.near()
+    outw_sent = []
+
+    def outw_copy(have, to, number):
+        slot = s.outw.at[flat(peer(have))]
+        return remote(slot, slot, s.o_ss.at[number], s.o_rs.at[number], to)
+
+    def outw_send(have, to, number):
+        copy = outw_copy(have, to, number)
+        copy.start()
+        outw_sent.append(copy)
+
+    def outw_arrive(what, number):
+        outw_copy(what, C, number).wait_recv()
+
+    outw_send(0, ZH, 0)
+
+    @pl.loop(1, 32)
+    def _(offset):
+        vec_copy(offset, flat(peer_loop(offset))).wait()
+
+    s.mod_row[...] = jnp.zeros_like(s.mod_row)
+    s.gain_rows[...] = jnp.zeros_like(s.gain_rows)
+    for index in range(32):
+        tile = (9 * index) // 8 * BLK
+        s.mod_row[0:1, tile : tile + 2 * BLK] += s.vecs[index, 0:1, :]
+        tile = (3 * index) // 16 * BLK
+        s.gain_rows[0:3, tile : tile + 2 * BLK] += s.vecs[index, 1:4, :]
+    shift_one, scale_one, gate_one, shift_two, scale_two, gate_two = range(6)
+    for index in range(6):
+        s.mods[index : index + 1, :] = s.mod_row[0:1, index * width : (index + 1) * width]
+    s.mods[6:9, :] = s.gain_rows[0:3, 0:width]
+    s.mods[9:10, :] = s.mods[6:7, :] * (1.0 + s.mods[scale_one : scale_one + 1, :])
+    s.mods[10:11, :] = s.mods[7:8, :] * (1.0 + s.mods[scale_two : scale_two + 1, :])
+
+    def mod(index):
+        return s.mods[index : index + 1, :]
+
+    gather_kv.second()
+    gather_q.second()
+    outw_arrive(ZH, 0)
+    outw_send(0, Y, 1)
+    outw_send(ZH, Y, 2)
+    for slot in range(4):
+        if slot:
+            token_copies[slot - 1].wait()
+        source = s.tok[slot] if slot else s.tokens[...]
+        normed, _unused = layer_norm(source.astype(f32))
+        s.mixed[here(slot), :] = (normed * mod(9) + mod(shift_one)).astype(bf16)
+    gather_kv.third()
+    gather_q.third()
+    cot_copies = [
+        remote(s.cot.at[0], s.cot.at[slot], s.cot_ss.at[slot], s.cot_rs.at[slot], TP[slot])
+        for slot in range(1, 4)
+    ]
+    for copy in cot_copies:
+        copy.start()
+    gather_e.near()
+    gather_r.near()
+    zero = jnp.zeros((HEAD_DIM, width), bf16)
+    for head in range(heads):
+        s.weight[head, HEAD_DIM:, :] = zero
+
+    def assemble(part, base, low):
+        for slot in range(8):
+            for row, head, target in head_rows(slot * count, count, low):
+                s.weight[base + head, target : target + 8, :] = s.chunks[
+                    slot, part, row : row + 8, :
+                ]
+
+    gather_kv.last()
+    assemble(1, heads, True)
+    assemble(2, heads, False)
+    for copy in tables:
+        copy.wait()
+    kv_far = [
+        remote(s.kv.at[0, head], s.kv.at[2, head], s.kv_ss.at[head], s.kv_rs.at[head], ZH)
+        for head in range(heads)
+    ]
+    kv_near = [
+        remote(
+            s.kv.at[0, head], s.kv.at[1, head], s.kv_ss.at[heads + head],
+            s.kv_rs.at[heads + head], C,
+        )
+        for head in range(heads)
+    ]
+    for head in range(heads):
+        both = dot_nt(s.mixed[...], s.weight[heads + head]).astype(bf16).astype(f32)
+        s.kv[0, head] = turn(both, s.cos[...], s.sin[...]).astype(bf16)
+        kv_far[head].start()
+        kv_near[head].start()
+    gather_q.last()
+    assemble(0, 0, True)
+    for head in range(heads):
+        query = dot_nt(s.mixed[...], s.weight[head]).astype(bf16).astype(f32)
+        query = turn(query, s.cos[...], s.sin[...]).astype(bf16).astype(f32)
+        s.query[head] = (query * scale).astype(bf16)
+    outw_arrive(Y, 1)
+    outw_arrive(Y + ZH, 2)
+    number = 3
+    for slot in range(1, 4):
+        for have in (0, ZH, Y, Y + ZH):
+            outw_send(have, TP[slot], number)
+            number += 1
+
+    s.state_m[...] = jnp.full_like(s.state_m, -1e30)
+    s.state_l[...] = jnp.zeros_like(s.state_l)
+    s.acc[...] = jnp.zeros_like(s.acc)
+
+    def attend(slot, head):
+        keys = s.kv[slot, head]
+        scores = dot_nt(keys, s.query[head])
+        before = s.state_m[head]
+        maximum = jnp.maximum(before, jnp.max(scores, axis=0, keepdims=True))
+        weights = jnp.exp(scores - maximum)
+        factor = jnp.exp(before - maximum)
+        s.state_m[head] = maximum
+        s.state_l[head] = s.state_l[head] * factor + column_sum(weights)
+        s.acc[head] = s.acc[head] * factor + dot_tn(keys, weights.astype(bf16))
+
+    for head in range(heads):
+        kv_near[head].wait_recv()
+
+    @pl.loop(0, heads)
+    def _(head):
+        attend(0, head)
+        attend(1, head)
+
+    number = 3
+    for slot in range(1, 4):
+        for have in (0, ZH, Y, Y + ZH):
+            outw_arrive(have + TP[slot], number)
+            number += 1
+    for tp in TP:
+        for have in (0, ZH, Y, Y + ZH):
+            outw_send(have + tp, C, number)
+            number += 1
+
+    def kv_forward(head):
+        return remote(
+            s.kv.at[2, head], s.kv.at[3, head], s.kv_ss.at[2 * heads + head],
+            s.kv_rs.at[2 * heads + head], C,
+        )
+
+    @pl.loop(0, heads)
+    def _(head):
+        remote(
+            s.kv.at[0, head], s.kv.at[2, head], s.kv_ss.at[head], s.kv_rs.at[head], ZH
+        ).wait_recv()
+        forward = kv_forward(head)
+        forward.start()
+        attend(2, head)
+        forward.wait_recv()
+        attend(3, head)
+        value = (s.acc[head] / s.state_l[head]).astype(bf16)
+        s.att[head] = value[HEAD_DIM:, :]
+        s.logt[head] = s.state_m[head] + jnp.log(s.state_l[head])
+
+    gather_e.far()
+    gather_r.far()
+
+    for slot in range(4):
+        for head in range(heads):
+            s.att_send[slot, head] = s.att[head, :, here(slot)]
+    att_copies = [
+        remote(
+            s.att_send.at[slot], s.att_all.at[my_rank], s.att_ss.at[slot], s.att_rs.at[slot],
+            TP[slot],
+        )
+        for slot in range(1, 4)
+    ]
+    for copy in att_copies:
+        copy.start()
+    s.att_all[my_rank] = s.att_send[0]
+    number = 15
+    for tp in TP:
+        for have in (0, ZH, Y, Y + ZH):
+            outw_arrive(have + tp + C, number)
+            number += 1
+    for index in range(32):
+        s.out_full[index * count : (index + 1) * count, :] = s.outw[index]
+    for slot in range(1, 4):
+        where = s.att_all.at[rank(TP[slot])]
+        remote(where, where, s.att_ss.at[slot], s.att_rs.at[slot], TP[slot]).wait_recv()
+    s.attn[...] = dot_tn(s.att_all[...].reshape(width, rows), s.out_full[...])
+    s.middle[...] = s.tokens[...].astype(f32) + mod(gate_one) * s.attn[...]
+    normed, inverse = layer_norm(s.middle[...])
+    s.normed[...] = normed
+    s.inverse[...] = inverse
+    s.mix[0, :, :width] = (normed * mod(10) + mod(shift_two)).astype(bf16)
+    mix_copies = [
+        remote(
+            s.mix.at[0, :, pl.ds(0, width)], s.mix.at[slot, :, pl.ds(0, width)],
+            s.mix_ss.at[slot], s.mix_rs.at[slot], TP[slot],
+        )
+        for slot in range(1, 4)
+    ]
+    for copy in mix_copies:
+        copy.start()
+    gather_e.second()
+    lane = lax.broadcasted_iota(jnp.int32, (rows, BLK), 1)
+    ones = jnp.where(lane == 0, 1.0, 0.0).astype(bf16)
+    for slot in range(4):
+        if slot:
+            cot_copies[slot - 1].wait()
+        s.mix[slot, :, width:] = ones
+        s.branch[here(slot), :] = (mod(gate_two) * s.cot[slot].astype(f32)).astype(bf16)
+    gather_e.third()
+    gather_r.second()
+    gather_e.last()
+    for index in range(8):
+        s.expand_full[index * per : (index + 1) * per, :] = s.expand[index]
+    gather_r.third()
+    gather_r.last()
+    for index in range(8):
+        s.reduce_full[index * per : (index + 1) * per, :] = s.reduce[index]
+
+    gm_copies, mlp_copies = [], []
+    for slot in range(4):
+        if slot:
+            mix_copies[slot - 1].wait_recv()
+        hidden = dot_nt(s.mix[slot], s.expand_full[...])
+        activated, slope = gelu_pair(hidden)
+        activated = activated.astype(bf16)
+        s.active[here(slot), :] = activated
+        grad_hidden = (dot_nt(s.branch[here(slot), :], s.reduce_full[...]) * slope).astype(bf16)
+        s.grad_hid[here(slot), :] = grad_hidden
+        gm_part = dot_nn(grad_hidden, s.expand_full[:, :width])
+        if slot:
+            s.gm_send[slot - 1] = gm_part.astype(bf16)
+            copy = remote(
+                s.gm_send.at[slot - 1], s.gm_recv.at[slot - 1], s.gm_ss.at[slot],
+                s.gm_rs.at[slot], TP[slot],
+            )
+            copy.start()
+            gm_copies.append(copy)
+        else:
+            s.grad_mixed[...] = gm_part
+    for slot in range(4):
+        mlp_part = dot_nn(s.active[here(slot), :], s.reduce_full[...])
+        if slot:
+            s.mlp_send[slot - 1] = mlp_part.astype(bf16)
+            copy = remote(
+                s.mlp_send.at[slot - 1], s.mlp_recv.at[slot - 1], s.mlp_ss.at[slot],
+                s.mlp_rs.at[slot], TP[slot],
+            )
+            copy.start()
+            mlp_copies.append(copy)
+        else:
+            s.mlp[...] = mlp_part + mod(8)
+    for copy in gm_copies:
+        copy.wait()
+    grad_mixed = (
+        s.grad_mixed[...]
+        + s.gm_recv[0].astype(f32) + s.gm_recv[1].astype(f32) + s.gm_recv[2].astype(f32)
+    )
+    cot = s.cotangent[...].astype(f32)
+    normed = s.normed[...]
+    grad_middle = cot + norm_back(grad_mixed * mod(10), normed, s.inverse[...])
+    s.gmid[...] = grad_middle
+    grad_attn = (mod(gate_one) * grad_middle).astype(bf16)
+    s.gattn[0] = grad_attn
+    s.dout_send[...] = dot_nt(s.out_full[...], grad_attn).astype(bf16).reshape(
+        s.dout_send.shape
+    )
+    dout_copies = [
+        remote(
+            s.dout_send.at[rank(TP[slot])], s.dout_recv.at[slot], s.dout_ss.at[slot],
+            s.dout_rs.at[slot], TP[slot],
+        )
+        for slot in range(1, 4)
+    ]
+    for copy in dout_copies:
+        copy.start()
+    s.dout_recv[0] = s.dout_send[my_rank]
+    ga_copies = [
+        remote(s.gattn.at[0], s.gattn.at[slot], s.ga_ss.at[slot], s.ga_rs.at[slot], TP[slot])
+        for slot in range(1, 4)
+    ]
+    for copy in ga_copies:
+        copy.start()
+    weighted = column_sum(grad_mixed * normed)
+    s.rowsum[2:3, :] = column_sum(grad_middle * s.attn[...])
+    s.rowsum[3:4, :] = column_sum(grad_mixed)
+    s.rowsum[4:5, :] = weighted * mod(7)
+    s.rowsum[7:8, :] = weighted * (1.0 + mod(scale_two))
+    s.rowsum[8:9, :] = column_sum(s.branch[here(0), :].astype(f32))
+
+    for index in range(units // BLK):
+        lanes = slice(index * BLK, (index + 1) * BLK)
+        s.wide[lanes, 0:width] = dot_tn(s.active[:, lanes], s.branch[...])
+    for index in range(8):
+        s.blocks_r[index] = s.wide[index * per : (index + 1) * per, 0:width].astype(bf16)
+    scatter_r = Scatter(lambda slot: s.blocks_r.at[slot], lambda k: s.from_r.at[k], s.sr_ss, s.sr_rs)
+    scatter_r.step(C)
+    for index in range(units // BLK):
+        lanes = slice(index * BLK, (index + 1) * BLK)
+        s.wide[lanes, :] = dot_tn(
+            s.grad_hid[:, lanes], s.mix[...].reshape(4 * rows, width + BLK)
+        )
+    for index in range(8):
+        s.blocks_e[index] = s.wide[index * per : (index + 1) * per, :].astype(bf16)
+    scatter_e = Scatter(lambda slot: s.blocks_e.at[slot], lambda k: s.from_e.at[k], s.se_ss, s.se_rs)
+    scatter_e.step(C)
+    scatter_r.add(C)
+    scatter_r.step(Y)
+
+    s.dout_t[...] = jnp.zeros_like(s.dout_t)
+    for slot in range(4):
+        if slot:
+            dout_copies[slot - 1].wait()
+        for head in range(heads):
+            s.dout_t[head, HEAD_DIM:, here(slot)] = s.dout_recv[slot, head]
+    for head in range(heads):
+        value = s.dout_t[head].astype(f32)
+        s.dout[head] = value.T.astype(bf16)
+        s.rdots[head] = column_sum(value[HEAD_DIM:, :] * s.att[head].astype(f32))
+    scatter_e.add(C)
+    scatter_e.step(Y)
+    s.dq[...] = jnp.zeros_like(s.dq)
+
+    def back(slot, head):
+        keys = s.kv[slot, head]
+        query = s.query[head]
+        shares = jnp.exp(dot_nt(keys, query) - s.logt[head])
+        grad_shares = dot_nn(keys, s.dout_t[head])
+        grad_scores = (shares * (grad_shares - s.rdots[head])).astype(bf16)
+        s.dq[head] += dot_tn(keys, grad_scores)
+        return dot_nn(grad_scores, query) + dot_nn(shares.astype(bf16), s.dout[head])
+
+    def dkv_copy(stage, head, offset):
+        index = stage * heads + head
+        return remote(
+            s.dkv_send.at[index], s.dkv_recv.at[index], s.dkv_ss.at[index], s.dkv_rs.at[index],
+            offset,
+        )
+
+    @pl.loop(0, heads)
+    def _(head):
+        s.dkv_send[head] = back(3, head).astype(bf16)
+        first = dkv_copy(0, head, C)
+        first.start()
+        part = back(2, head)
+        first.wait_recv()
+        s.dkv_send[heads + head] = (part + s.dkv_recv[head].astype(f32)).astype(bf16)
+        dkv_copy(1, head, ZH).start()
+
+    @pl.loop(0, heads)
+    def _(head):
+        s.dkv_send[2 * heads + head] = back(1, head).astype(bf16)
+        dkv_copy(2, head, C).start()
+        s.dkv[head] = back(0, head)
+        value = s.dq[head].T * scale
+        s.dqkv[head] = turn(value, s.cos[...], -s.sin[...]).astype(bf16)
+
+    for copy in ga_copies:
+        copy.wait()
+    gattn = s.gattn[...].reshape(4 * rows, width)
+
+    def spread(part, low, of):
+        for slot in range(8):
+            for row, head, target in head_rows(slot * count, count, low):
+                s.blocks_a[slot, part, row : row + 8, :] = s.wide[
+                    of * heads * BLK + head * BLK + target
+                    : of * heads * BLK + head * BLK + target + 8, 0:width
+                ].astype(bf16)
+
+    for head in range(heads):
+        s.wide[head * BLK + HEAD_DIM : (head + 1) * BLK, 0:width] = dot_nn(s.att[head], gattn)
+    spread(3, False, 0)
+    for head in range(heads):
+        at = (heads + head) * BLK
+        s.wide[at : at + BLK, 0:width] = dot_tn(s.dqkv[head], s.mixed[...])
+    spread(0, True, 1)
+
+    def scatter_part(part, ss, rs):
+        return Scatter(
+            lambda slot: s.blocks_a.at[slot, part],
+            lambda k: s.from_a.at[k, part],
+            ss, rs,
+        )
+
+    scatter_o = scatter_part(3, s.so_ss, s.so_rs)
+    scatter_q = scatter_part(0, s.sq_ss, s.sq_rs)
+    scatter_k = scatter_part(1, s.sk_ss, s.sk_rs)
+    scatter_v = scatter_part(2, s.sv_ss, s.sv_rs)
+    scatter_o.step(C)
+    scatter_q.step(C)
+    scatter_r.add(Y)
+    scatter_e.add(Y)
+    for copy in mlp_copies:
+        copy.wait()
+    mlp_branch = (
+        s.mlp[...]
+        + s.mlp_recv[0].astype(f32) + s.mlp_recv[1].astype(f32) + s.mlp_recv[2].astype(f32)
+    )
+    s.result[...] = (s.middle[...] + mod(gate_two) * mlp_branch).astype(bf16)
+    s.rowsum[5:6, :] = column_sum(s.cotangent[...].astype(f32) * mlp_branch)
+    query_part = dot_nn(s.dqkv[0], s.weight[0])
+    for head in range(1, heads):
+        query_part = query_part + dot_nn(s.dqkv[head], s.weight[head])
+    s.part[...] = query_part
+    scatter_o.add(C)
+    scatter_q.add(C)
+    scatter_o.step(Y)
+    scatter_q.step(Y)
+
+    for head in range(heads):
+        dkv_copy(2, head, C).wait_recv()
+        s.dkv[head] += s.dkv_recv[2 * heads + head].astype(f32)
+    for head in range(heads):
+        dkv_copy(1, head, ZH).wait_recv()
+        value = s.dkv[head] + s.dkv_recv[heads + head].astype(f32)
+        s.dqkv[heads + head] = turn(value, s.cos[...], -s.sin[...]).astype(bf16)
+    scatter_r.step(ZH)
+    scatter_e.step(ZH)
+
+    kv_part = s.part[...]
+    for head in range(heads, 2 * heads):
+        kv_part = kv_part + dot_nn(s.dqkv[head], s.weight[head])
+    part_copies = []
+    for slot in (3, 2, 1):
+        s.part_send[slot - 1] = kv_part[here(slot), :].astype(bf16)
+        copy = remote(
+            s.part_send.at[slot - 1], s.part_recv.at[slot - 1], s.part_ss.at[slot],
+            s.part_rs.at[slot], TP[slot],
+        )
+        copy.start()
+        part_copies.append(copy)
+    s.grad_mixed[...] = kv_part[here(0), :]
+    for head in range(heads):
+        s.wide[head * BLK : (head + 1) * BLK, 0:width] = dot_tn(
+            s.dqkv[heads + head], s.mixed[...]
+        )
+    spread(1, True, 0)
+    spread(2, False, 0)
+    scatter_k.step(C)
+    scatter_v.step(C)
+    scatter_o.add(Y)
+    scatter_q.add(Y)
+
+    def chunk_back(part, half):
+        slot = half * 4 + own % 4
+        place_in = 8 * my_rank + slot
+        if part < 3:
+            number = 32 * part + place_in
+            owner, at = number // 3, number % 3
+        else:
+            owner, at = place_in, 3
+        zh = own // 4
+        index = part * 2 + half
+        source = s.blocks_a.at[slot, part]
+        target = s.owned.at[zh, at]
+        far = remote_to(
+            source, target, s.back_ss.at[index], s.back_rs.at[zh * 4 + at],
+            (owner // 16, owner % 16),
+        )
+        near = pltpu.make_async_copy(source, target, s.local_sem.at[index])
+        return far, near, owner == me
+
+    def chunks_back(parts, act):
+        for part in parts:
+            for half in range(2):
+                far, near, stays = chunk_back(part, half)
+
+                @pl.when(jnp.logical_not(stays))
+                def _():
+                    far.start() if act else far.wait_send()
+
+                @pl.when(stays)
+                def _():
+                    near.start() if act else near.wait()
+
+    chunks_back((0, 3), True)
+    scatter_k.add(C)
+    scatter_v.add(C)
+    scatter_k.step(Y)
+    scatter_v.step(Y)
+    for copy in part_copies:
+        copy.wait()
+    grad_mixed_one = (
+        s.grad_mixed[...]
+        + s.part_recv[0].astype(f32) + s.part_recv[1].astype(f32) + s.part_recv[2].astype(f32)
+    )
+    normed_one, inverse_one = layer_norm(s.tokens[...].astype(f32))
+    weighted = column_sum(grad_mixed_one * normed_one)
+    s.rowsum[0:1, :] = column_sum(grad_mixed_one)
+    s.rowsum[1:2, :] = weighted * mod(6)
+    s.rowsum[6:7, :] = weighted * (1.0 + mod(scale_one))
+    tiles = width // BLK
+    s.vec_send[...] = jnp.zeros_like(s.vec_send)
+    for owner in range(32):
+        for tile in range(2):
+            lanes = slice(tile * BLK, (tile + 1) * BLK)
+            at = (9 * owner) // 8 + tile
+            s.vec_send[owner, 0:1, lanes] = s.rowsum[
+                at // tiles : at // tiles + 1, (at % tiles) * BLK : (at % tiles + 1) * BLK
+            ]
+            at = (3 * owner) // 16 + tile
+            if at < tiles:
+                s.vec_send[owner, 1:4, lanes] = s.rowsum[6:9, at * BLK : (at + 1) * BLK]
+
+    def sum_copy(offset):
+        return remote_to(
+            s.vec_send.at[flat(peer_loop(offset))], s.vec_recv.at[offset],
+            s.sum_ss.at[offset], s.sum_rs.at[offset], peer_loop(offset),
+        )
+
+    @pl.loop(1, 32)
+    def _(offset):
+        sum_copy(offset).start()
+
+    scatter_k.add(Y)
+    scatter_v.add(Y)
+    chunks_back((1, 2), True)
+    s.grad_tokens[...] = s.gmid[...] + norm_back(
+        grad_mixed_one * mod(9), normed_one, inverse_one
+    )
+    s.vec_recv[0] = s.vec_send[me]
+
+    @pl.loop(1, 32)
+    def _(offset):
+        sum_copy(offset).wait()
+
+    total = jnp.zeros(s.vec_recv.shape[1:], f32)
+    for index in range(32):
+        total = total + s.vec_recv[index]
+    s.vec_own[0:4, :] = total
+    s.vec_own[8:12, :] = total
+    s.sums[0:8, :] = pltpu.roll(s.vec_own[0:8, :], (256 - mod_shift) % 256, 1)
+    s.sums[8:16, :] = pltpu.roll(s.vec_own[8:16, :], (256 - gain_shift) % 256, 1)
+    s.cond_send[...] = exact(s.sums[0:8, 0:piece], s.ada[...].astype(f32), ((1,), (0,)))
+
+    def cond_copy(offset):
+        return remote_to(
+            s.cond_send.at[pl.ds(0, 1)], s.cond_recv.at[offset], s.cond_ss.at[offset],
+            s.cond_rs.at[offset], peer_loop(offset),
+        )
+
+    @pl.loop(1, 32)
+    def _(offset):
+        cond_copy(offset).start()
+
+    s.grad_r[0] = s.blocks_r[own]
+    s.grad_e[0] = s.blocks_e[own]
+    for index, scatter, target in ((0, scatter_r, s.grad_r), (1, scatter_e, s.grad_e)):
+        scatter.copies[ZH][0].wait_recv()
+        target[1] = scatter.inbox(6)[...]
+
+    @pl.loop(1, 32)
+    def _(offset):
+        cond_copy(offset).wait()
+
+    gradient = s.cond_send[0:1, :]
+    for index in range(1, 32):
+        gradient = gradient + s.cond_recv[index]
+    s.grad_cond[...] = gradient
+
+    chunks_back(range(4), False)
+    for at in range(4):
+        if at < 3:
+            number = 3 * me + at
+            part, place_in = number // 32, number % 32
+        else:
+            part, place_in = 3, me
+        slot = place_in % 8
+        for zh in range(2):
+            keeper = flat(member(place_in // 8, zh * 4 + slot % 4))
+
+            @pl.when(keeper != me)
+            def _():
+                target = s.owned.at[zh, at]
+                remote(
+                    target, target, s.back_ss.at[0], s.back_rs.at[zh * 4 + at], C
+                ).wait_recv()
+
+    for copies in (kv_far, kv_near, mix_copies, outw_sent, att_copies):
+        for copy in copies:
+            copy.wait_send()
+    for gather in (gather_kv, gather_q, gather_e, gather_r):
+        gather.finish()
+    for scatter in (scatter_e, scatter_r, scatter_o, scatter_q, scatter_k, scatter_v):
+        scatter.finish()
+
+    @pl.loop(0, heads)
+    def _(head):
+        kv_forward(head).wait_send()
+        dkv_copy(0, head, C).wait_send()
+        dkv_copy(1, head, ZH).wait_send()
+        dkv_copy(2, head, C).wait_send()
+
+
+def finish_kernel(
+    result, grad_tokens, grad_cond, sums, grad_e, grad_r, owned, condition,
+    result_out, tokens_out, cond_out, ada_out, ada_bias_out, first_out, second_out, project_out,
+    output_out, expand_out, expand_bias_out, reduce_out, reduce_bias_out,
+):
+    width = result.shape[1]
+    count = output_out.shape[0]
+    piece = ada_out.shape[0]
+    result_out[...] = result[...]
+    tokens_out[...] = grad_tokens[...]
+    cond_out[...] = grad_cond[...]
+    first = lax.broadcasted_iota(jnp.int32, (8, piece), 0) == 0
+    row = jnp.where(first, sums[0:8, 0:piece], 0.0)
+    ada_out[...] = exact(
+        row, jnp.broadcast_to(condition[...], (8, condition.shape[1])), ((0,), (0,))
+    )
+    ada_bias_out[...] = sums[0:1, 0:piece]
+    first_out[...] = sums[9:10, 0:count]
+    second_out[...] = sums[10:11, 0:count]
+    reduce_bias_out[...] = sums[11:12, 0:count]
+    both = owned[0].astype(f32) + owned[1].astype(f32)
+    project_out[...] = both[0:3]
+    output_out[...] = both[3]
+    expand = grad_e[0].astype(f32) + grad_e[1].astype(f32)
+    expand_out[...] = expand[:, 0:width]
+    expand_bias_out[...] = to_row(expand[:, width : width + 1])
+    reduce_out[...] = grad_r[0].astype(f32) + grad_r[1].astype(f32)
+
+
+def rotary_blocks(length):
+    half_dim = HEAD_DIM // 2
+    frequency = np.exp(
+        np.arange(half_dim, dtype=np.float32) * np.float32(-2.0 * math.log(10000.0) / HEAD_DIM)
+    ).astype(np.float32)
+    angles = (np.arange(length, dtype=np.float32)[:, None] * frequency[None, :]).astype(np.float32)
+    cosine, sine = np.cos(angles.astype(np.float64)), np.sin(angles.astype(np.float64))
+    one, zero = np.ones((length, HEAD_DIM)), np.zeros((length, HEAD_DIM))
+    return (
+        np.concatenate([cosine, cosine, one], axis=1).astype(np.float32),
+        np.concatenate([-sine, sine, zero], axis=1).astype(np.float32),
+    )
+
+
+def on_device_fast(
+    tokens, condition, ada_weight, ada_bias, first_gain, second_gain, project_weight,
+    output_weight, expand_weight, expand_bias, reduce_weight, reduce_bias, cotangent,
+):
+    rows, width = tokens.shape
+    group = 4 * rows
+    heads = width // HEAD_DIM // 4
+    per = reduce_weight.shape[0]
+    units = 8 * per
+    count = output_weight.shape[0]
+    piece = ada_weight.shape[1]
+    wide = width + BLK
+    cosine, sine = (
+        jnp.asarray(table) for table in rotary_blocks(lax.axis_size("blk") * rows)
+    )
+    line = condition[None, :]
+    inputs = dict(
+        tokens=tokens, cotangent=cotangent, condition=line, ada=ada_weight.T,
+        ada_bias=ada_bias[None, :], first_gain=first_gain[None, :],
+        second_gain=second_gain[None, :], reduce_bias=reduce_bias[None, :],
+        expand_bias=expand_bias[None, :],
+        project_weight=project_weight.T.reshape(3, count, width), output_weight=output_weight,
+        expand_weight=expand_weight.T, reduce_weight=reduce_weight, cos_hbm=cosine, sin_hbm=sine,
+    )
+    outputs = dict(
+        result=((rows, width), bf16), grad_tokens=((rows, width), f32),
+        grad_cond=((1, line.shape[1]), f32), sums=((16, 256), f32),
+        grad_e=((2, per, wide), bf16), grad_r=((2, per, width), bf16),
+        owned=((2, 4, count, width), bf16),
+    )
+    head_block = (group, BLK)
+    scratch = dict(
+        cos=(head_block, f32), sin=(head_block, f32), vec_own=((16, 256), f32),
+        vecs=((32, 4, 256), f32), mod_row=((1, 6 * width), f32), gain_rows=((3, wide), f32),
+        mods=((16, width), f32), chunks=((8, 3, count, width), bf16),
+        tok=((4, rows, width), bf16), cot=((4, rows, width), bf16),
+        expand=((8, per, wide), bf16), reduce=((8, per, width), bf16),
+        outw=((32, count, width), bf16), out_full=((width, width), bf16),
+        weight=((2 * heads, BLK, width), bf16), mixed=((group, width), bf16),
+        query=((heads,) + head_block, bf16), kv=((4, heads) + head_block, bf16),
+        state_m=((heads, 1, group), f32), state_l=((heads, 1, group), f32),
+        acc=((heads, BLK, group), f32), att=((heads, HEAD_DIM, group), bf16),
+        logt=((heads, 1, group), f32), att_send=((4, heads, HEAD_DIM, rows), bf16),
+        att_all=((4, heads, HEAD_DIM, rows), bf16), attn=((rows, width), f32),
+        middle=((rows, width), f32), normed=((rows, width), f32), inverse=((rows, 1), f32),
+        mix=((4, rows, wide), bf16), branch=((group, width), bf16),
+        expand_full=((units, wide), bf16), reduce_full=((units, width), bf16),
+        active=((group, units), bf16), grad_hid=((group, units), bf16),
+        gm_send=((3, rows, width), bf16), gm_recv=((3, rows, width), bf16),
+        mlp_send=((3, rows, width), bf16), mlp_recv=((3, rows, width), bf16),
+        grad_mixed=((rows, width), f32), mlp=((rows, width), f32), gmid=((rows, width), f32),
+        gattn=((4, rows, width), bf16), dout_send=((4, heads, HEAD_DIM, rows), bf16),
+        dout_recv=((4, heads, HEAD_DIM, rows), bf16), rowsum=((16, width), f32),
+        wide=((units, wide), f32), blocks_r=((8, per, width), bf16),
+        blocks_e=((8, per, wide), bf16), blocks_a=((8, 4, count, width), bf16),
+        from_r=((7, per, width), bf16), from_e=((7, per, wide), bf16),
+        from_a=((6, 4, count, width), bf16), dout_t=((heads, BLK, group), bf16),
+        dout=((heads,) + head_block, bf16), rdots=((heads, 1, group), f32),
+        dq=((heads, BLK, group), f32), dkv=((heads,) + head_block, f32),
+        dkv_send=((3 * heads,) + head_block, bf16), dkv_recv=((3 * heads,) + head_block, bf16),
+        dqkv=((2 * heads,) + head_block, bf16), part=((group, width), f32),
+        part_send=((3, rows, width), bf16), part_recv=((3, rows, width), bf16),
+        vec_send=((32, 4, 256), f32), vec_recv=((32, 4, 256), f32),
+        cond_send=((8, line.shape[1]), f32), cond_recv=((32, 1, line.shape[1]), f32),
+    )
+    semaphores = dict(
+        table_sem=8, local_sem=8, chunk_ss=3, chunk_rs=3, vec_ss=32, vec_rs=32, tok_ss=4,
+        tok_rs=4, akv_ss=8, akv_rs=8, aq_ss=8, aq_rs=8, e_ss=8, e_rs=8, r_ss=8, r_rs=8, o_ss=31,
+        o_rs=31, cot_ss=4, cot_rs=4, kv_ss=3 * heads, kv_rs=3 * heads, att_ss=4, att_rs=4,
+        mix_ss=4, mix_rs=4, gm_ss=4, gm_rs=4, mlp_ss=4, mlp_rs=4, dout_ss=4, dout_rs=4, ga_ss=4,
+        ga_rs=4, sr_ss=7, sr_rs=7, se_ss=7, se_rs=7, so_ss=6, so_rs=6, sq_ss=6, sq_rs=6, sk_ss=6,
+        sk_rs=6, sv_ss=6, sv_rs=6, dkv_ss=3 * heads, dkv_rs=3 * heads, part_ss=4, part_rs=4,
+        back_ss=8, back_rs=8, sum_ss=32, sum_rs=32, cond_ss=32, cond_rs=32,
+    )
+    whole = pl.BlockSpec(memory_space=pltpu.VMEM)
+    names = (*inputs, *outputs, *scratch, *semaphores)
+    staged = pl.pallas_call(
+        partial(block_kernel, names),
+        out_shape=tuple(jax.ShapeDtypeStruct(*spec) for spec in outputs.values()),
+        in_specs=[
+            pl.BlockSpec(memory_space=pl.ANY) if name.endswith("_hbm") else whole
+            for name in inputs
+        ],
+        out_specs=tuple(whole for _ in outputs),
+        scratch_shapes=[pltpu.VMEM(*spec) for spec in scratch.values()]
+        + [pltpu.SemaphoreType.DMA((number,)) for number in semaphores.values()],
+        compiler_params=pltpu.CompilerParams(
+            collective_id=1, has_side_effects=True, vmem_limit_bytes=62 * 2**20
+        ),
+    )(*inputs.values())
+    (
+        result, grad_tokens, grad_condition, grad_ada, grad_ada_bias, grad_first, grad_second,
+        grad_project, grad_output, grad_expand, grad_expand_bias, grad_reduce, grad_reduce_bias,
+    ) = pl.pallas_call(
+        finish_kernel,
+        out_shape=tuple(
+            jax.ShapeDtypeStruct(shape, kind)
+            for shape, kind in (
+                ((rows, width), bf16), ((rows, width), f32), (line.shape, f32),
+                ((piece, line.shape[1]), f32), ((1, piece), f32), ((1, count), f32),
+                ((1, count), f32), ((3, count, width), f32), ((count, width), f32),
+                ((per, width), f32), ((1, per), f32), ((per, width), f32), ((1, count), f32),
+            )
+        ),
+        in_specs=[whole] * 8,
+        out_specs=(whole,) * 13,
+    )(*staged, line)
+    return (
+        result,
+        grad_tokens,
+        grad_condition.reshape(-1),
+        grad_ada.T,
+        grad_ada_bias.reshape(-1),
+        grad_first.reshape(-1),
+        grad_second.reshape(-1),
+        grad_project.reshape(3 * count, width).T,
+        grad_output,
+        grad_expand.T,
+        grad_expand_bias.reshape(-1),
+        grad_reduce,
+        grad_reduce_bias.reshape(-1),
+    )
+
+
 def solution(mesh):
     return jax.shard_map(
-        on_device,
+        on_device_fast if mesh.shape["ulysses"] * mesh.shape["blk"] == 32 else on_device,
         mesh=mesh,
         in_specs=(
             P(("ulysses", "blk"), None),

time: 1050 us -> 173 us (0.16)
  waiting for transfers between devices: 657 us -> 0 us
  Pallas kernels: 0 us -> 170 us
  blocking collectives: 140 us -> 0 us
  matrix products: 105 us -> 0 us
  local copies, waits for them, and re-layouts: 100 us -> 1.21 us
  other arithmetic: 17.9 us -> 0 us
  between operations: 14.5 us -> 0.82 us
    reduce_scatter x4 -> x0, waiting for transfers between devices: 347 us -> none  [the longest x1 141 us: on_device(): lax.psum_scatter(grad_reduce, ('ulysses', 'blk'), scatter_dimension=0, ti...]
    all_gather x9 -> x0, waiting for transfers between devices: 297 us -> none  [the longest x1 62.7 us: on_device(): lax.all_gather(expand_weight, ('ulysses', 'blk'), axis=1, tiled=True)]
    pallas_call x0 -> x2, Pallas kernels: none -> 170 us  [the longest x1 167 us: on_device_fast(): pl.pallas_call(partial(block_kernel, names), out_shape=tuple((jax.ShapeDt...]
    dot_general x42 -> x0, matrix products: 105 us -> none  [the longest x4 18.5 us: key_step(): jnp.einsum('shqk,sqhd->skhd', grad_scores, query_rows, preferred_element_...]
    dynamic_slice x33 -> x0, local copies, waits for them, and re-layouts: 51.5 us -> none  [the longest x32 51.4 us: over_blocks(): carried, unused = lax.scan(scan_step, carried, stacked + (offsets,))]
    unnamed x1 -> x0, blocking collectives: 40.7 us -> none
    psum x1 -> x0, blocking collectives: 39.4 us -> none  [on_device(): grad_modulation = lax.psum(mod_terms, ('ulysses', 'blk'))]
    all_gather x2 -> x0, blocking collectives: 39.1 us -> none  [the longest x1 21 us: on_device(): lax.all_gather(jnp.transpose(log_total, (0, 2, 1)), 'blk', axis=1, tiled=...]
  transfers between devices with their start and end apart: 15 -> 0, of which waited for: 11 -> 0; matrix products, arithmetic and copies ran while one was open for 19% -> 0% of each run, Pallas kernels for 0% -> 0%
where the time goes in v2:
time: 173 us; the launch traced here: 172 us
  Pallas kernels  170 us (98%)
    pallas_call x1, Pallas kernels, on_device_fast(): pl.pallas_call(partial(block_kernel, names), out_shape=tuple((jax.ShapeDt...  167 us

profile of v2, /device:TPU:5, one launch (start us, length us, event | category | flops | bytes accessed | tf_op | source)
XLA Modules:
  0.0 172.0 jit_solution(7085472038567657231)
XLA Ops:
  0.6 0.0 copy-start
  0.7 0.6 copy-done
  1.3 0.6 broadcast_in_dim.19.refs_4_
  1.9 167.3 %shard_map.246 = (bf16[128,768]{1,0:T(8,128)(2,1)}, f32[128,768]{1,0:T(8,128)}, f32[1,128]{1,0:T(1,128)}, f32[16,256]{1,0:T(8,128)}, bf16[2,96,896]{2,1,0:T(8,12...) custom-call(bf16[128,768]{1,0:T(8,128)(2,1)} %refs_0_.1, bf16[128,768]{1,0:T(8,128)(2,1)} %refs_1_.1, ...), custom_call_target="tpu_custom_call" | custom-call | tf_op jit(solution)/shard_map/pallas_call | solution.py:1440
  169.2 2.7 %shard_map.247 = (bf16[128,768]{1,0:T(8,128)(2,1)}, f32[128,768]{1,0:T(8,128)}, f32[1,128]{1,0:T(1,128)}, f32[144,128]{1,0:T(8,128)}, f32[1,144]{1,0:T(1,128)}, ...) custom-call(bf16[128,768]{1,0:T(8,128)(2,1)} %get-tuple-element.33.r, ...), custom_call_target="tpu_custom_call" | custom-call | tf_op jit(solution)/shard_map/pallas_call | solution.py:1457
Async XLA Ops:
  0.6 0.7 copy-start

commit v3 on v2

--- a/solution.py
+++ b/solution.py
@@ -1,4 +1,5 @@
 from functools import partial
+import itertools
 import math
 import types
 
@@ -11,6 +12,7 @@
 from jax.sharding import PartitionSpec as P
 
 HEAD_DIM = 64
+BOTH = ("ulysses", "blk")
 
 
 eps = 1e-05
@@ -108,16 +110,16 @@
         reduce_full,
         reduce_shift,
     ) = (
-        lax.all_gather(ada_weight, ("ulysses", "blk"), axis=1, tiled=True),
-        lax.all_gather(ada_bias, ("ulysses", "blk"), axis=0, tiled=True),
-        lax.all_gather(first_gain, ("ulysses", "blk"), axis=0, tiled=True),
-        lax.all_gather(second_gain, ("ulysses", "blk"), axis=0, tiled=True),
-        lax.all_gather(project_weight, ("ulysses", "blk"), axis=1, tiled=True),
-        lax.all_gather(output_weight, ("ulysses", "blk"), axis=0, tiled=True),
-        lax.all_gather(expand_weight, ("ulysses", "blk"), axis=1, tiled=True),
-        lax.all_gather(expand_bias, ("ulysses", "blk"), axis=0, tiled=True),
-        lax.all_gather(reduce_weight, ("ulysses", "blk"), axis=0, tiled=True),
-        lax.all_gather(reduce_bias, ("ulysses", "blk"), axis=0, tiled=True),
+        lax.all_gather(ada_weight, BOTH, axis=1, tiled=True),
+        lax.all_gather(ada_bias, BOTH, axis=0, tiled=True),
+        lax.all_gather(first_gain, BOTH, axis=0, tiled=True),
+        lax.all_gather(second_gain, BOTH, axis=0, tiled=True),
+        lax.all_gather(project_weight, BOTH, axis=1, tiled=True),
+        lax.all_gather(output_weight, BOTH, axis=0, tiled=True),
+        lax.all_gather(expand_weight, BOTH, axis=1, tiled=True),
+        lax.all_gather(expand_bias, BOTH, axis=0, tiled=True),
+        lax.all_gather(reduce_weight, BOTH, axis=0, tiled=True),
+        lax.all_gather(reduce_bias, BOTH, axis=0, tiled=True),
     )
     ada_float = ada_full.astype(jnp.float32)
     modulation = jnp.dot(condition, ada_float, precision=highest) + ada_shift.astype(jnp.float32)
@@ -364,21 +366,21 @@
             grad_gate_two,
         ]
     )
-    grad_modulation = lax.psum(mod_terms, ("ulysses", "blk"))
+    grad_modulation = lax.psum(mod_terms, BOTH)
     grad_condition = jnp.dot(ada_float, grad_modulation, precision=highest)
     piece_width = ada_weight.shape[1]
     flat_index = lax.axis_index("ulysses") * cycle_size + cycle_place
     mod_piece = lax.dynamic_slice_in_dim(grad_modulation, flat_index * piece_width, piece_width, 0)
     grad_ada = condition[:, None] * mod_piece[None, :]
     shards = (
-        lax.psum_scatter(grad_gain_one, ("ulysses", "blk"), scatter_dimension=0, tiled=True),
-        lax.psum_scatter(grad_gain_two, ("ulysses", "blk"), scatter_dimension=0, tiled=True),
-        lax.psum_scatter(grad_project, ("ulysses", "blk"), scatter_dimension=1, tiled=True),
-        lax.psum_scatter(grad_output, ("ulysses", "blk"), scatter_dimension=0, tiled=True),
-        lax.psum_scatter(grad_expand, ("ulysses", "blk"), scatter_dimension=1, tiled=True),
-        lax.psum_scatter(grad_expand_shift, ("ulysses", "blk"), scatter_dimension=0, tiled=True),
-        lax.psum_scatter(grad_reduce, ("ulysses", "blk"), scatter_dimension=0, tiled=True),
-        lax.psum_scatter(grad_reduce_shift, ("ulysses", "blk"), scatter_dimension=0, tiled=True),
+        lax.psum_scatter(grad_gain_one, BOTH, scatter_dimension=0, tiled=True),
+        lax.psum_scatter(grad_gain_two, BOTH, scatter_dimension=0, tiled=True),
+        lax.psum_scatter(grad_project, BOTH, scatter_dimension=1, tiled=True),
+        lax.psum_scatter(grad_output, BOTH, scatter_dimension=0, tiled=True),
+        lax.psum_scatter(grad_expand, BOTH, scatter_dimension=1, tiled=True),
+        lax.psum_scatter(grad_expand_shift, BOTH, scatter_dimension=0, tiled=True),
+        lax.psum_scatter(grad_reduce, BOTH, scatter_dimension=0, tiled=True),
+        lax.psum_scatter(grad_reduce_shift, BOTH, scatter_dimension=0, tiled=True),
     )
     return (
         result,
@@ -399,8 +401,8 @@
 
 MESH = pl.DeviceIdType.MESH
 Y, ZH, ZL, X, C = 16, 8, 4, 2, 1
-TP = (0, X, ZL, X + ZL)
-DP = (0, C, Y, Y + C, ZH, ZH + C, ZH + Y, ZH + Y + C)
+ATTN = (0, X, ZH, X + ZH)
+MLP = (0, X, ZL, X + ZL)
 BLK = 128
 f32 = jnp.float32
 bf16 = jnp.bfloat16
@@ -439,25 +441,25 @@
     return device[0] * 16 + device[1]
 
 
-def share(offset):
+def share(offset, far):
     y, zh, zl, x, c = flip(offset)
-    return zh * 4 + y * 2 + c
+    return c * 4 + y * 2 + (zl if far == ZL else zh)
 
 
 def rank(offset):
     y, zh, zl, x, c = flip(offset)
-    return zl * 2 + x
+    return zh * 2 + x
 
 
 def member(which, slot):
-    return device_at((slot // 2) % 2, slot // 4, which // 2, which % 2, slot % 2)
-
-
-def enter(offsets):
+    return device_at((slot // 2) % 2, which // 2, slot % 2, which % 2, slot // 4)
+
+
+def greet(offsets):
     barrier = pltpu.get_barrier_semaphore()
     for offset in offsets:
         pl.semaphore_signal(barrier, inc=1, device_id=peer(offset), device_id_type=MESH)
-    pl.semaphore_wait(barrier, len(offsets))
+    return lambda: pl.semaphore_wait(barrier, len(offsets))
 
 
 def remote_to(source, target, send_sem, recv_sem, device):
@@ -498,84 +500,160 @@
 
 
 class Gather:
-    def __init__(self, view, send_sem, recv_sem):
-        self.view, self.send_sem, self.recv_sem = view, send_sem, recv_sem
-        self.sent = []
-
-    def send(self, have, to):
-        slot = self.view(share(have))
-        index = len(self.sent)
-        copy = remote(
-            slot, slot, self.send_sem.at[index], self.recv_sem.at[DP.index(have + to)], to
-        )
-        copy.start()
-        self.sent.append(copy)
-
-    def arrive(self, what):
-        slot = self.view(share(what))
-        remote(
-            slot, slot, self.send_sem.at[0], self.recv_sem.at[DP.index(what)], C
-        ).wait_recv()
+    def __init__(self, view, send_sem, recv_sem, far, pieces):
+        own, core = share(0, far), share(C, far)
+        z, y = share(far, far), share(Y, far)
+        both = share(Y + far, far)
+        half = own // 4 * 4
+        other = core // 4 * 4
+        self.out = [
+            remote(view(own, 1), view(own, 1), send_sem.at[1], recv_sem.at[1], Y),
+            remote(view(z, 1), view(z, 1), send_sem.at[2], recv_sem.at[2], Y),
+            remote(view(half, 4), view(half, 4), send_sem.at[3], recv_sem.at[3], C),
+        ]
+        self.parts = [
+            tuple(
+                remote(
+                    piece(view(where, 1)), piece(view(where, 1)), send_sem.at[index],
+                    recv_sem.at[index], far,
+                )
+                for where in (own, z)
+            )
+            for index, piece in zip((0, 4), pieces)
+        ]
+        self.into = [
+            remote(view(where, size), view(where, size), send_sem.at[index], recv_sem.at[index], to)
+            for index, where, size, to in ((1, y, 1, Y), (2, both, 1, Y), (3, other, 4, C))
+        ]
 
     def near(self):
-        self.send(0, Y)
-        self.send(0, C)
-
-    def far(self):
-        self.send(0, ZH)
+        self.out[0].start()
+
+    def far(self, which=0):
+        self.parts[which][0].start()
 
     def second(self):
-        self.arrive(ZH)
-        self.send(ZH, Y)
-        self.send(ZH, C)
+        for _out, into in self.parts:
+            into.wait_recv()
+        self.out[1].start()
 
     def third(self):
-        self.arrive(Y)
-        self.send(Y, C)
-        self.arrive(ZH + Y)
-        self.send(ZH + Y, C)
+        self.into[0].wait_recv()
+        self.into[1].wait_recv()
+        self.out[2].start()
 
     def last(self):
-        for what in (C, Y + C, ZH + C, ZH + Y + C):
-            self.arrive(what)
+        self.into[2].wait_recv()
 
     def finish(self):
-        for copy in self.sent:
+        for copy in self.out:
             copy.wait_send()
+        for out, _into in self.parts:
+            out.wait_send()
+
+
+class Spread:
+    def __init__(self, view, place_of, order, send_sem, recv_sem):
+        self.out, self.into = [], []
+        size = 1
+        for index, to in enumerate(order):
+            mine, other = (place_of(flip(to_where)) // size * size for to_where in (0, to))
+            sems = (send_sem.at[index], recv_sem.at[index])
+            self.out.append(remote(view(mine, size), view(mine, size), *sems, to))
+            self.into.append(remote(view(other, size), view(other, size), *sems, to))
+            size *= 2
+
+    def step(self, index):
+        if index:
+            self.into[index - 1].wait_recv()
+        self.out[index].start()
+
+    def last(self):
+        self.into[-1].wait_recv()
+
+    def finish(self):
+        for copy in self.out:
+            copy.wait_send()
 
 
 class Scatter:
-    KEPT = {C: (0, Y, ZH, Y + ZH), Y: (0, ZH), ZH: (0,)}
-
-    def __init__(self, view, inbox, send_sem, recv_sem):
+    def __init__(self, view, inbox, send_sem, recv_sem, far):
         self.view, self.inbox = view, inbox
+        own = share(0, far)
+        core, y, z = share(C, far), share(Y, far), share(far, far)
+        self.plan = {
+            C: (core // 4 * 4, own // 4 * 4, 4, 0), Y: (y // 2 * 2, own // 2 * 2, 2, 4),
+            far: (z, own, 1, 6),
+        }
         self.send_sem, self.recv_sem = send_sem, recv_sem
-        self.base = {C: 0, Y: 4, ZH: 6}
         self.copies = {}
 
     def step(self, to):
-        self.copies[to] = []
-        for index, offset in enumerate(self.KEPT[to]):
-            number = self.base[to] + index
-            copy = remote(
-                self.view(share(offset + to)), self.inbox(number),
-                self.send_sem.at[number], self.recv_sem.at[number], to,
+        goes, _stays, size, slot = self.plan[to]
+        index = len(self.copies)
+        self.copies[to] = remote(
+            self.view(goes, size), self.inbox(slot, size), self.send_sem.at[index],
+            self.recv_sem.at[index], to,
+        )
+        self.copies[to].start()
+
+    def add(self, to):
+        self.copies[to].wait_recv()
+        _goes, stays, size, slot = self.plan[to]
+        block = self.view(stays, size)
+        block[...] = (
+            block[...].astype(f32) + self.inbox(slot, size)[...].astype(f32)
+        ).astype(bf16)
+
+    def finish(self):
+        for copy in self.copies.values():
+            copy.wait_send()
+
+
+class Total:
+    def __init__(self, first, mid, last, send_sem, recv_sem):
+        self.first, self.mid, self.last = first, mid, last
+        y, zh, zl, x, c = place()
+        self.own = (y * 2 + zh, zl * 2 + x, c)
+        self.copies = [
+            remote(
+                ref.at[own], ref.at[own], send_sem.at[3 * which + index],
+                recv_sem.at[3 * which + index], to,
             )
+            for which, (ref, own, offsets) in enumerate(
+                (
+                    (first, self.own[0], (Y, ZH, Y + ZH)), (last, self.own[1], (ZL, X, ZL + X)),
+                    (mid, self.own[2], (C,)),
+                )
+            )
+            for index, to in enumerate(offsets)
+        ]
+
+    def start(self, value):
+        self.first[self.own[0]] = value
+        for copy in self.copies[0:3]:
             copy.start()
-            self.copies[to].append(copy)
-
-    def add(self, to):
-        for index, offset in enumerate(self.KEPT[to]):
-            self.copies[to][index].wait_recv()
-            block = self.view(share(offset))
-            block[...] = (
-                block[...].astype(f32) + self.inbox(self.base[to] + index)[...].astype(f32)
-            ).astype(bf16)
+
+    def second(self):
+        for copy in self.copies[0:3]:
+            copy.wait_recv()
+        self.mid[self.own[2]] = self.first[0] + self.first[1] + self.first[2] + self.first[3]
+        self.copies[6].start()
+
+    def third(self):
+        self.copies[6].wait_recv()
+        self.last[self.own[1]] = self.mid[0] + self.mid[1]
+        for copy in self.copies[3:6]:
+            copy.start()
+
+    def result(self):
+        for copy in self.copies[3:6]:
+            copy.wait_recv()
+        return self.last[0] + self.last[1] + self.last[2] + self.last[3]
 
     def finish(self):
-        for copies in self.copies.values():
-            for copy in copies:
-                copy.wait_send()
+        for copy in self.copies:
+            copy.wait_send()
 
 
 def turn(value, cosine, sine):
@@ -621,30 +699,47 @@
 def block_kernel(names, *refs):
     s = types.SimpleNamespace(**dict(zip(names, refs)))
     rows, width = s.tokens.shape
+    wide = width + BLK
     heads = s.query.shape[0]
-    count = s.output_weight.shape[0]
-    per = s.reduce_weight.shape[0]
+    count = s.output_weight_hbm.shape[0]
+    per = s.reduce_weight_hbm.shape[0]
     units = 8 * per
     scale = HEAD_DIM ** (-0.5)
     me = flat(peer(0))
-    own = share(0)
+    own, own_mlp = share(0, ZL), share(0, ZH)
     my_rank = rank(0)
 
     def here(slot):
         return slice(slot * rows, (slot + 1) * rows)
 
-    tables = []
-    for slot in range(4):
-        start = pl.multiple_of(peer(TP[slot])[1] * rows, rows)
-        for which, (source, target) in enumerate(((s.cos_hbm, s.cos), (s.sin_hbm, s.sin))):
-            copy = pltpu.make_async_copy(
-                source.at[pl.ds(start, rows)],
-                target.at[pl.ds(slot * rows, rows)],
-                s.table_sem.at[slot * 2 + which],
-            )
-            copy.start()
-            tables.append(copy)
+    loads = {}
+
+    def load(name, target=None):
+        number = len(loads)
+        copy = pltpu.make_async_copy(
+            getattr(s, name + "_hbm"), getattr(s, name) if target is None else target,
+            s.load_sem.at[number],
+        )
+        copy.start()
+        loads[name] = copy
+
+    for name in (
+        "ada", "condition", "ada_bias", "first_gain", "second_gain", "reduce_bias",
+        "project_weight",
+    ):
+        load(name)
+    def out_place(bits):
+        y, zh, zl, x, c = bits
+        return c * 16 + y * 8 + zh * 4 + zl * 2 + x
+
+    entered = greet(range(1, 32))
     piece = s.ada.shape[0]
+    for name in ("ada", "condition", "ada_bias", "first_gain", "second_gain", "reduce_bias"):
+        loads[name].wait()
+    for index in range(width // BLK):
+        s.adaw[out_place(flip(0)), :, index * BLK : (index + 1) * BLK] = s.ada[
+            index * count : (index + 1) * count, :
+        ]
     s.vec_own[...] = jnp.zeros_like(s.vec_own)
     s.vec_own[0:8, 0:piece] = exact(
         jnp.broadcast_to(s.condition[...], (8, s.condition.shape[1])),
@@ -655,19 +750,48 @@
         s.vec_own[8 + index : 9 + index, 0:count] = ref[...].astype(f32)
     mod_shift = (me % 8) * 16
     gain_shift = ((3 * me) % 16) * 8
-    s.vecs[me, 0:1, :] = pltpu.roll(s.vec_own[0:8, :], mod_shift, 1)[0:1, :]
-    s.vecs[me, 1:4, :] = pltpu.roll(s.vec_own[8:16, :], gain_shift, 1)[0:3, :]
-    s.cot[0] = s.cotangent[...]
-    s.expand[own, :, 0:width] = s.expand_weight[...]
-    lane = lax.broadcasted_iota(jnp.int32, (per, BLK), 1)
-    s.expand[own, :, width:] = jnp.where(
-        lane == 0, to_column(s.expand_bias[...].astype(f32)), 0.0
-    ).astype(bf16)
-    s.reduce[own] = s.reduce_weight[...]
-    s.outw[me] = s.output_weight[...]
-
-    enter(range(1, 32))
-
+    y, zh, zl, x, c = place()
+    vec_own = y * 16 + x * 8 + c * 4 + zh * 2 + zl
+    s.vecs[vec_own, 0:1, :] = pltpu.roll(s.vec_own[0:8, :], mod_shift, 1)[0:1, :]
+    s.vecs[vec_own, 1:4, :] = pltpu.roll(s.vec_own[8:16, :], gain_shift, 1)[0:3, :]
+    lane = lax.broadcasted_iota(jnp.int32, (rows, BLK), 1)
+    ones = jnp.where(lane == 0, 1.0, 0.0).astype(bf16)
+    for slot in range(4):
+        s.mix[slot, :, width:] = ones
+        s.plain[here(slot), width:] = ones
+    loads["project_weight"].wait()
+    entered()
+
+    def token_copy(have, to):
+        slot = ATTN.index(have + to)
+        return remote(
+            s.tok.at[ATTN.index(have)] if have else s.tokens, s.tok.at[slot],
+            s.tok_ss.at[slot], s.tok_rs.at[slot], to,
+        )
+
+    token_copies = [token_copy(0, X), token_copy(0, ZH), token_copy(ZH, X)]
+    vec_steps = []
+    for index, (size, offsets) in enumerate(
+        ((1, (ZL, ZH, ZL + ZH)), (4, (C, X, X + C)), (16, (Y,)))
+    ):
+        where = s.vecs.at[pl.ds(vec_own // size * size, size)]
+        vec_steps.append(
+            [
+                remote(
+                    where, where, s.vec_ss.at[3 * index + number], s.vec_rs.at[3 * index + number],
+                    to,
+                )
+                for number, to in enumerate(offsets)
+            ]
+        )
+
+    def vec_step(index):
+        for copy in vec_steps[index - 1] if index else ():
+            copy.wait_recv()
+        for copy in vec_steps[index] if index < 3 else ():
+            copy.start()
+
+    vec_step(0)
     def chunk_out(index):
         number = 3 * me + index
         part, place_in = number // 32, number % 32
@@ -691,22 +815,54 @@
         def _():
             near.start()
 
-    def vec_copy(offset, device):
-        return remote_to(
-            s.vecs.at[device], s.vecs.at[device], s.vec_ss.at[offset], s.vec_rs.at[offset],
-            peer_loop(offset),
-        )
-
-    @pl.loop(1, 32)
-    def _(offset):
-        vec_copy(offset, me).start()
-
-    token_copies = [
-        remote(s.tokens, s.tok.at[slot], s.tok_ss.at[slot], s.tok_rs.at[slot], TP[slot])
-        for slot in range(1, 4)
-    ]
-    for copy in token_copies:
+    for name in ("tokens", "expand_bias"):
+        load(name)
+    load("expand_weight", s.er.at[own_mlp, :, pl.ds(0, width)])
+    load("reduce_weight", s.er.at[own_mlp, :, pl.ds(wide, width)])
+
+    load("output_weight", s.outw.at[out_place(flip(0))])
+    load("cotangent", s.cot.at[0])
+    tables = []
+    for slot in range(4):
+        start = pl.multiple_of(peer(ATTN[slot])[1] * rows, rows)
+        copy = pltpu.make_async_copy(
+            s.table_hbm.at[pl.ds(start, rows)], s.table.at[pl.ds(slot * rows, rows)],
+            s.table_sem.at[slot],
+        )
         copy.start()
+        tables.append(copy)
+    gather_er = Gather(
+        lambda slot, size: s.er.at[pl.ds(slot, size)], s.er_ss, s.er_rs, ZH,
+        (
+            lambda v: v.at[:, :, pl.ds(wide, width)],
+            lambda v: v.at[:, :, pl.ds(0, wide)],
+        ),
+    )
+    loads["expand_bias"].wait()
+    lane = lax.broadcasted_iota(jnp.int32, (per, BLK), 1)
+    s.er[own_mlp, :, width:wide] = jnp.where(
+        lane == 0, to_column(s.expand_bias[...].astype(f32)), 0.0
+    ).astype(bf16)
+    zero = jnp.zeros((HEAD_DIM, width), bf16)
+    for head in range(heads):
+        s.weight[head, HEAD_DIM:, :] = zero
+    s.state_m[...] = jnp.full_like(s.state_m, -1e30)
+    s.state_l[...] = jnp.zeros_like(s.state_l)
+    s.acc[...] = jnp.zeros_like(s.acc)
+    spread_out = Spread(
+        lambda slot, size: s.outw.at[pl.ds(slot, size)], out_place, (X, ZL, ZH, Y, C),
+        s.o_ss, s.o_rs,
+    )
+    spread_ada = Spread(
+        lambda slot, size: s.adaw.at[pl.ds(slot, size)], out_place, (X, ZL, ZH, Y, C),
+        s.ada_ss, s.ada_rs,
+    )
+    for name in ("expand_weight", "reduce_weight", "output_weight", "cotangent", "tokens"):
+        loads[name].wait()
+    vec_step(1)
+    gather_er.far(0)
+    spread_out.step(0)
+    spread_ada.step(0)
 
     for index in range(3):
         far, near, stays = chunk_out(index)
@@ -719,41 +875,35 @@
         def _():
             near.wait()
 
-    gather_kv = Gather(lambda slot: s.chunks.at[slot, pl.ds(1, 2)], s.akv_ss, s.akv_rs)
-    gather_q = Gather(lambda slot: s.chunks.at[slot, 0], s.aq_ss, s.aq_rs)
-    gather_e = Gather(lambda slot: s.expand.at[slot], s.e_ss, s.e_rs)
-    gather_r = Gather(lambda slot: s.reduce.at[slot], s.r_ss, s.r_rs)
-    gather_kv.far()
-    gather_kv.near()
-    gather_q.far()
-    gather_q.near()
-    outw_sent = []
-
-    def outw_copy(have, to, number):
-        slot = s.outw.at[flat(peer(have))]
-        return remote(slot, slot, s.o_ss.at[number], s.o_rs.at[number], to)
-
-    def outw_send(have, to, number):
-        copy = outw_copy(have, to, number)
-        copy.start()
-        outw_sent.append(copy)
-
-    def outw_arrive(what, number):
-        outw_copy(what, C, number).wait_recv()
-
-    outw_send(0, ZH, 0)
-
-    @pl.loop(1, 32)
-    def _(offset):
-        vec_copy(offset, flat(peer_loop(offset))).wait()
-
+    gather_a = Gather(
+        lambda slot, size: s.chunks.at[pl.ds(slot, size)], s.a_ss, s.a_rs, ZL, (lambda v: v,)
+    )
+    def cot_copy(have, to):
+        slot = MLP.index(have + to)
+        return remote(
+            s.cot.at[MLP.index(have)], s.cot.at[slot], s.cot_ss.at[slot], s.cot_rs.at[slot], to
+        )
+
+    cot_copies = [cot_copy(0, X), cot_copy(0, ZL), cot_copy(ZL, X)]
+    gather_a.far()
+    gather_a.near()
+    token_copies[1].start()
+    token_copies[0].start()
+    vec_step(2)
+    spread_out.step(1)
+    spread_ada.step(1)
+    gather_a.second()
+    cot_copies[1].start()
+    vec_step(3)
     s.mod_row[...] = jnp.zeros_like(s.mod_row)
     s.gain_rows[...] = jnp.zeros_like(s.gain_rows)
     for index in range(32):
+        y, zh, zl, x, c = ((index // weight) % 2 for weight in (Y, ZH, ZL, X, C))
+        found = y * 16 + x * 8 + c * 4 + zh * 2 + zl
         tile = (9 * index) // 8 * BLK
-        s.mod_row[0:1, tile : tile + 2 * BLK] += s.vecs[index, 0:1, :]
+        s.mod_row[0:1, tile : tile + 2 * BLK] += s.vecs[found, 0:1, :]
         tile = (3 * index) // 16 * BLK
-        s.gain_rows[0:3, tile : tile + 2 * BLK] += s.vecs[index, 1:4, :]
+        s.gain_rows[0:3, tile : tile + 2 * BLK] += s.vecs[found, 1:4, :]
     shift_one, scale_one, gate_one, shift_two, scale_two, gate_two = range(6)
     for index in range(6):
         s.mods[index : index + 1, :] = s.mod_row[0:1, index * width : (index + 1) * width]
@@ -764,31 +914,21 @@
     def mod(index):
         return s.mods[index : index + 1, :]
 
-    gather_kv.second()
-    gather_q.second()
-    outw_arrive(ZH, 0)
-    outw_send(0, Y, 1)
-    outw_send(ZH, Y, 2)
     for slot in range(4):
-        if slot:
-            token_copies[slot - 1].wait()
+        if slot == 1 or slot == 3:
+            token_copies[slot - 1].wait_recv()
+        if slot == 2:
+            token_copies[1].wait_recv()
+            token_copies[2].start()
+            cot_copies[0].start()
+            spread_out.step(2)
+            gather_er.far(1)
+            gather_er.near()
+            gather_a.third()
         source = s.tok[slot] if slot else s.tokens[...]
         normed, _unused = layer_norm(source.astype(f32))
         s.mixed[here(slot), :] = (normed * mod(9) + mod(shift_one)).astype(bf16)
-    gather_kv.third()
-    gather_q.third()
-    cot_copies = [
-        remote(s.cot.at[0], s.cot.at[slot], s.cot_ss.at[slot], s.cot_rs.at[slot], TP[slot])
-        for slot in range(1, 4)
-    ]
-    for copy in cot_copies:
-        copy.start()
-    gather_e.near()
-    gather_r.near()
-    zero = jnp.zeros((HEAD_DIM, width), bf16)
-    for head in range(heads):
-        s.weight[head, HEAD_DIM:, :] = zero
-
+        s.plain[here(slot), 0:width] = normed.astype(bf16)
     def assemble(part, base, low):
         for slot in range(8):
             for row, head, target in head_rows(slot * count, count, low):
@@ -796,13 +936,13 @@
                     slot, part, row : row + 8, :
                 ]
 
-    gather_kv.last()
+    gather_a.last()
     assemble(1, heads, True)
     assemble(2, heads, False)
     for copy in tables:
         copy.wait()
     kv_far = [
-        remote(s.kv.at[0, head], s.kv.at[2, head], s.kv_ss.at[head], s.kv_rs.at[head], ZH)
+        remote(s.kv.at[0, head], s.kv.at[2, head], s.kv_ss.at[head], s.kv_rs.at[head], ZL)
         for head in range(heads)
     ]
     kv_near = [
@@ -814,26 +954,17 @@
     ]
     for head in range(heads):
         both = dot_nt(s.mixed[...], s.weight[heads + head]).astype(bf16).astype(f32)
-        s.kv[0, head] = turn(both, s.cos[...], s.sin[...]).astype(bf16)
+        s.kv[0, head] = turn(both, s.table[:, 0:BLK], s.table[:, BLK:]).astype(bf16)
         kv_far[head].start()
         kv_near[head].start()
-    gather_q.last()
     assemble(0, 0, True)
     for head in range(heads):
         query = dot_nt(s.mixed[...], s.weight[head]).astype(bf16).astype(f32)
-        query = turn(query, s.cos[...], s.sin[...]).astype(bf16).astype(f32)
+        query = turn(query, s.table[:, 0:BLK], s.table[:, BLK:]).astype(bf16).astype(f32)
         s.query[head] = (query * scale).astype(bf16)
-    outw_arrive(Y, 1)
-    outw_arrive(Y + ZH, 2)
-    number = 3
-    for slot in range(1, 4):
-        for have in (0, ZH, Y, Y + ZH):
-            outw_send(have, TP[slot], number)
-            number += 1
-
-    s.state_m[...] = jnp.full_like(s.state_m, -1e30)
-    s.state_l[...] = jnp.zeros_like(s.state_l)
-    s.acc[...] = jnp.zeros_like(s.acc)
+    cot_copies[1].wait_recv()
+    cot_copies[2].start()
+
 
     def attend(slot, head):
         keys = s.kv[slot, head]
@@ -854,16 +985,6 @@
         attend(0, head)
         attend(1, head)
 
-    number = 3
-    for slot in range(1, 4):
-        for have in (0, ZH, Y, Y + ZH):
-            outw_arrive(have + TP[slot], number)
-            number += 1
-    for tp in TP:
-        for have in (0, ZH, Y, Y + ZH):
-            outw_send(have + tp, C, number)
-            number += 1
-
     def kv_forward(head):
         return remote(
             s.kv.at[2, head], s.kv.at[3, head], s.kv_ss.at[2 * heads + head],
@@ -873,10 +994,16 @@
     @pl.loop(0, heads)
     def _(head):
         remote(
-            s.kv.at[0, head], s.kv.at[2, head], s.kv_ss.at[head], s.kv_rs.at[head], ZH
+            s.kv.at[0, head], s.kv.at[2, head], s.kv_ss.at[head], s.kv_rs.at[head], ZL
         ).wait_recv()
         forward = kv_forward(head)
         forward.start()
+
+        @pl.when(head == 1)
+        def _():
+            spread_out.step(3)
+            gather_er.second()
+
         attend(2, head)
         forward.wait_recv()
         attend(3, head)
@@ -884,32 +1011,29 @@
         s.att[head] = value[HEAD_DIM:, :]
         s.logt[head] = s.state_m[head] + jnp.log(s.state_l[head])
 
-    gather_e.far()
-    gather_r.far()
-
     for slot in range(4):
         for head in range(heads):
             s.att_send[slot, head] = s.att[head, :, here(slot)]
     att_copies = [
         remote(
             s.att_send.at[slot], s.att_all.at[my_rank], s.att_ss.at[slot], s.att_rs.at[slot],
-            TP[slot],
+            ATTN[slot],
         )
         for slot in range(1, 4)
     ]
     for copy in att_copies:
         copy.start()
     s.att_all[my_rank] = s.att_send[0]
-    number = 15
-    for tp in TP:
-        for have in (0, ZH, Y, Y + ZH):
-            outw_arrive(have + tp + C, number)
-            number += 1
-    for index in range(32):
-        s.out_full[index * count : (index + 1) * count, :] = s.outw[index]
+    spread_out.step(4)
+    gather_er.third()
+    spread_out.last()
+    for y in range(2):
+        for zh, zl, x, c in itertools.product(range(2), repeat=4):
+            at = (y * 16 + zh * 8 + zl * 4 + x * 2 + c) * count
+            s.out_full[at : at + count, :] = s.outw[c * 16 + y * 8 + zh * 4 + zl * 2 + x]
     for slot in range(1, 4):
-        where = s.att_all.at[rank(TP[slot])]
-        remote(where, where, s.att_ss.at[slot], s.att_rs.at[slot], TP[slot]).wait_recv()
+        where = s.att_all.at[rank(ATTN[slot])]
+        remote(where, where, s.att_ss.at[slot], s.att_rs.at[slot], ATTN[slot]).wait_recv()
     s.attn[...] = dot_tn(s.att_all[...].reshape(width, rows), s.out_full[...])
     s.middle[...] = s.tokens[...].astype(f32) + mod(gate_one) * s.attn[...]
     normed, inverse = layer_norm(s.middle[...])
@@ -919,70 +1043,97 @@
     mix_copies = [
         remote(
             s.mix.at[0, :, pl.ds(0, width)], s.mix.at[slot, :, pl.ds(0, width)],
-            s.mix_ss.at[slot], s.mix_rs.at[slot], TP[slot],
+            s.mix_ss.at[slot], s.mix_rs.at[slot], MLP[slot],
         )
         for slot in range(1, 4)
     ]
-    for copy in mix_copies:
+    for copy in mix_copies[0:2]:
         copy.start()
-    gather_e.second()
-    lane = lax.broadcasted_iota(jnp.int32, (rows, BLK), 1)
-    ones = jnp.where(lane == 0, 1.0, 0.0).astype(bf16)
     for slot in range(4):
-        if slot:
-            cot_copies[slot - 1].wait()
-        s.mix[slot, :, width:] = ones
+        if slot == 1 or slot == 3:
+            cot_copies[slot - 1].wait_recv()
         s.branch[here(slot), :] = (mod(gate_two) * s.cot[slot].astype(f32)).astype(bf16)
-    gather_e.third()
-    gather_r.second()
-    gather_e.last()
+    gather_er.last()
+
+    def expand(lanes=wide):
+        return s.er[:, :, 0:lanes].reshape(units, lanes)
+
+    def reduce():
+        return s.er[:, :, wide:].reshape(units, width)
+
+    spread_ada.step(2)
+    gm_copies = [
+        remote(
+            s.gm_send.at[slot - 1], s.gm_recv.at[slot - 1], s.gm_ss.at[slot], s.gm_rs.at[slot],
+            MLP[slot],
+        )
+        for slot in range(1, 4)
+    ]
+    for first, last in ((0, 1), (1, 3), (3, 4)):
+        for slot in range(first, last):
+            if slot:
+                mix_copies[slot - 1].wait_recv()
+        if first == 1:
+            mix_copies[2].start()
+        these = slice(first * rows, last * rows)
+        mixed_two = s.mix[first:last].reshape((last - first) * rows, wide)
+        activated, slope = gelu_pair(dot_nt(mixed_two, expand()))
+        s.active[these, :] = activated.astype(bf16)
+        grad_hidden = (dot_nt(s.branch[these, :], reduce()) * slope).astype(bf16)
+        s.grad_hid[these, :] = grad_hidden
+        gm_part = dot_nn(grad_hidden, expand(width))
+        for slot in range(first, last):
+            part = gm_part[(slot - first) * rows : (slot - first + 1) * rows, :]
+            if slot:
+                s.gm_send[slot - 1] = part.astype(bf16)
+                gm_copies[slot - 1].start()
+            else:
+                s.grad_mixed[...] = part
+    for index in range(units // BLK):
+        lanes = slice(index * BLK, (index + 1) * BLK)
+        s.wide[lanes, 0:width] = dot_tn(s.active[:, lanes], s.branch[...])
     for index in range(8):
-        s.expand_full[index * per : (index + 1) * per, :] = s.expand[index]
-    gather_r.third()
-    gather_r.last()
+        s.blocks_r[index] = s.wide[index * per : (index + 1) * per, 0:width].astype(bf16)
+    scatter_r = Scatter(
+        lambda slot, size: s.blocks_r.at[pl.ds(slot, size)],
+        lambda slot, size: s.from_r.at[pl.ds(slot, size)], s.sr_ss, s.sr_rs, ZH
+    )
+    scatter_r.step(C)
+    for index in range(units // BLK):
+        lanes = slice(index * BLK, (index + 1) * BLK)
+        s.wide[lanes, :] = dot_tn(
+            s.grad_hid[:, lanes], s.mix[...].reshape(4 * rows, width + BLK)
+        )
+    scatter_r.add(C)
+    scatter_r.step(Y)
     for index in range(8):
-        s.reduce_full[index * per : (index + 1) * per, :] = s.reduce[index]
-
-    gm_copies, mlp_copies = [], []
-    for slot in range(4):
-        if slot:
-            mix_copies[slot - 1].wait_recv()
-        hidden = dot_nt(s.mix[slot], s.expand_full[...])
-        activated, slope = gelu_pair(hidden)
-        activated = activated.astype(bf16)
-        s.active[here(slot), :] = activated
-        grad_hidden = (dot_nt(s.branch[here(slot), :], s.reduce_full[...]) * slope).astype(bf16)
-        s.grad_hid[here(slot), :] = grad_hidden
-        gm_part = dot_nn(grad_hidden, s.expand_full[:, :width])
-        if slot:
-            s.gm_send[slot - 1] = gm_part.astype(bf16)
-            copy = remote(
-                s.gm_send.at[slot - 1], s.gm_recv.at[slot - 1], s.gm_ss.at[slot],
-                s.gm_rs.at[slot], TP[slot],
-            )
-            copy.start()
-            gm_copies.append(copy)
-        else:
-            s.grad_mixed[...] = gm_part
-    for slot in range(4):
-        mlp_part = dot_nn(s.active[here(slot), :], s.reduce_full[...])
-        if slot:
-            s.mlp_send[slot - 1] = mlp_part.astype(bf16)
-            copy = remote(
-                s.mlp_send.at[slot - 1], s.mlp_recv.at[slot - 1], s.mlp_ss.at[slot],
-                s.mlp_rs.at[slot], TP[slot],
-            )
-            copy.start()
-            mlp_copies.append(copy)
-        else:
-            s.mlp[...] = mlp_part + mod(8)
+        s.blocks_e[index] = s.wide[index * per : (index + 1) * per, :].astype(bf16)
+    scatter_e = Scatter(
+        lambda slot, size: s.blocks_e.at[pl.ds(slot, size)],
+        lambda slot, size: s.from_e.at[pl.ds(slot, size)], s.se_ss, s.se_rs, ZH
+    )
+    scatter_e.step(C)
+    def mlp_copy(slot, number, to):
+        return remote(
+            s.mlp_send.at[slot], s.mlp_recv.at[number], s.mlp_ss.at[slot], s.mlp_rs.at[number], to
+        )
+
+    mlp_copies = [mlp_copy(2, 2, X), mlp_copy(0, 0, X), mlp_copy(1, 1, ZL)]
+
+    def mlp_part(slot):
+        return dot_nn(s.active[here(slot), :], reduce())
+
+    s.mlp_send[2] = mlp_part(3).astype(bf16)
+    s.mlp_send[0] = mlp_part(1).astype(bf16)
+    s.mlp[...] = mlp_part(0) + mod(8)
+    s.mlp_near[...] = mlp_part(2)
     for copy in gm_copies:
         copy.wait()
     grad_mixed = (
         s.grad_mixed[...]
         + s.gm_recv[0].astype(f32) + s.gm_recv[1].astype(f32) + s.gm_recv[2].astype(f32)
     )
-    cot = s.cotangent[...].astype(f32)
+    cot = s.cot[0].astype(f32)
     normed = s.normed[...]
     grad_middle = cot + norm_back(grad_mixed * mod(10), normed, s.inverse[...])
     s.gmid[...] = grad_middle
@@ -993,58 +1144,47 @@
     )
     dout_copies = [
         remote(
-            s.dout_send.at[rank(TP[slot])], s.dout_recv.at[slot], s.dout_ss.at[slot],
-            s.dout_rs.at[slot], TP[slot],
+            s.dout_send.at[rank(ATTN[slot])], s.dout_recv.at[slot], s.dout_ss.at[slot],
+            s.dout_rs.at[slot], ATTN[slot],
         )
         for slot in range(1, 4)
     ]
     for copy in dout_copies:
         copy.start()
     s.dout_recv[0] = s.dout_send[my_rank]
-    ga_copies = [
-        remote(s.gattn.at[0], s.gattn.at[slot], s.ga_ss.at[slot], s.ga_rs.at[slot], TP[slot])
-        for slot in range(1, 4)
-    ]
-    for copy in ga_copies:
-        copy.start()
+    def ga_copy(have, to):
+        slot = ATTN.index(have + to)
+        return remote(
+            s.gattn.at[ATTN.index(have)], s.gattn.at[slot], s.ga_ss.at[slot], s.ga_rs.at[slot], to
+        )
+
+    ga_copies = [ga_copy(0, X), ga_copy(0, ZH), ga_copy(ZH, X)]
     weighted = column_sum(grad_mixed * normed)
     s.rowsum[2:3, :] = column_sum(grad_middle * s.attn[...])
     s.rowsum[3:4, :] = column_sum(grad_mixed)
     s.rowsum[4:5, :] = weighted * mod(7)
     s.rowsum[7:8, :] = weighted * (1.0 + mod(scale_two))
     s.rowsum[8:9, :] = column_sum(s.branch[here(0), :].astype(f32))
-
-    for index in range(units // BLK):
-        lanes = slice(index * BLK, (index + 1) * BLK)
-        s.wide[lanes, 0:width] = dot_tn(s.active[:, lanes], s.branch[...])
-    for index in range(8):
-        s.blocks_r[index] = s.wide[index * per : (index + 1) * per, 0:width].astype(bf16)
-    scatter_r = Scatter(lambda slot: s.blocks_r.at[slot], lambda k: s.from_r.at[k], s.sr_ss, s.sr_rs)
-    scatter_r.step(C)
-    for index in range(units // BLK):
-        lanes = slice(index * BLK, (index + 1) * BLK)
-        s.wide[lanes, :] = dot_tn(
-            s.grad_hid[:, lanes], s.mix[...].reshape(4 * rows, width + BLK)
-        )
-    for index in range(8):
-        s.blocks_e[index] = s.wide[index * per : (index + 1) * per, :].astype(bf16)
-    scatter_e = Scatter(lambda slot: s.blocks_e.at[slot], lambda k: s.from_e.at[k], s.se_ss, s.se_rs)
-    scatter_e.step(C)
-    scatter_r.add(C)
-    scatter_r.step(Y)
+    scatter_e.add(C)
+    scatter_e.step(Y)
 
     s.dout_t[...] = jnp.zeros_like(s.dout_t)
     for slot in range(4):
         if slot:
             dout_copies[slot - 1].wait()
+        if slot == 3:
+            ga_copies[1].start()
+            mlp_copies[0].start()
         for head in range(heads):
             s.dout_t[head, HEAD_DIM:, here(slot)] = s.dout_recv[slot, head]
     for head in range(heads):
         value = s.dout_t[head].astype(f32)
         s.dout[head] = value.T.astype(bf16)
         s.rdots[head] = column_sum(value[HEAD_DIM:, :] * s.att[head].astype(f32))
-    scatter_e.add(C)
-    scatter_e.step(Y)
+    scatter_r.add(Y)
+    scatter_r.step(ZH)
+    ga_copies[0].start()
+    mlp_copies[1].start()
     s.dq[...] = jnp.zeros_like(s.dq)
 
     def back(slot, head):
@@ -1071,18 +1211,103 @@
         part = back(2, head)
         first.wait_recv()
         s.dkv_send[heads + head] = (part + s.dkv_recv[head].astype(f32)).astype(bf16)
-        dkv_copy(1, head, ZH).start()
+        dkv_copy(1, head, ZL).start()
+
+    scatter_e.add(Y)
+    scatter_e.step(ZH)
+    spread_ada.step(3)
+    mlp_copies[0].wait_recv()
+    s.mlp_send[1] = (s.mlp_near[...] + s.mlp_recv[2].astype(f32)).astype(bf16)
+    mlp_copies[2].start()
 
     @pl.loop(0, heads)
     def _(head):
+        @pl.when(head == 1)
+        def _():
+            ga_copies[1].wait_recv()
+            ga_copies[2].start()
+
         s.dkv_send[2 * heads + head] = back(1, head).astype(bf16)
         dkv_copy(2, head, C).start()
         s.dkv[head] = back(0, head)
         value = s.dq[head].T * scale
-        s.dqkv[head] = turn(value, s.cos[...], -s.sin[...]).astype(bf16)
-
-    for copy in ga_copies:
-        copy.wait()
+        s.dqkv[head] = turn(value, s.table[:, 0:BLK], -s.table[:, BLK:]).astype(bf16)
+
+    spread_ada.step(4)
+    query_part = dot_nn(s.dqkv[0], s.weight[0])
+    for head in range(1, heads):
+        query_part = query_part + dot_nn(s.dqkv[head], s.weight[head])
+    s.part[...] = query_part
+    for head in range(heads):
+        dkv_copy(2, head, C).wait_recv()
+        s.dkv[head] += s.dkv_recv[2 * heads + head].astype(f32)
+    for head in range(heads):
+        dkv_copy(1, head, ZL).wait_recv()
+        value = s.dkv[head] + s.dkv_recv[heads + head].astype(f32)
+        s.dqkv[heads + head] = turn(value, s.table[:, 0:BLK], -s.table[:, BLK:]).astype(bf16)
+    kv_part = s.part[...]
+    for head in range(heads, 2 * heads):
+        kv_part = kv_part + dot_nn(s.dqkv[head], s.weight[head])
+
+    def part_copy(slot, number, to):
+        return remote(
+            s.part_send.at[slot], s.part_recv.at[number], s.part_ss.at[slot],
+            s.part_rs.at[number], to,
+        )
+
+    def part_half(slot, number, to, half):
+        lines = pl.ds(half * (rows // 2), rows // 2)
+        return remote(
+            s.part_send.at[slot, lines], s.part_recv.at[number, lines],
+            s.part_ss.at[slot + 3 * half], s.part_rs.at[number + 3 * half], to,
+        )
+
+    relays = [(part_half(2, 2, X, half), part_half(1, 1, ZH, half)) for half in range(2)]
+    part_copies = [part_copy(0, 0, X)]
+    s.part_send[2] = kv_part[here(3), :].astype(bf16)
+    for half in range(2):
+        relays[half][0].start()
+    s.part_send[0] = kv_part[here(1), :].astype(bf16)
+    s.part[here(2), :] = kv_part[here(2), :]
+    s.grad_mixed[...] = kv_part[here(0), :]
+
+    s.norm_sum[...] = jnp.zeros_like(s.norm_sum)
+    s.rowsum[9:16, :] = jnp.zeros((7, width), f32)
+    for head in range(2 * heads):
+        moment = dot_tn(s.dqkv[head], s.plain[...])
+        weights = s.weight[head].astype(f32)
+        s.norm_sum[0:1, :] += column_sum(weights * moment[:, width : width + 1])
+        s.norm_sum[1:2, :] += column_sum(weights * moment[:, 0:width])
+    s.rowsum[0:1, :] = s.norm_sum[0:1, :]
+    s.rowsum[1:2, :] = s.norm_sum[1:2, :] * mod(6)
+    s.rowsum[6:7, :] = s.norm_sum[1:2, :] * (1.0 + mod(scale_one))
+    for index in (1, 2):
+        mlp_copies[index].wait_recv()
+    mlp_branch = s.mlp[...] + s.mlp_recv[0].astype(f32) + s.mlp_recv[1].astype(f32)
+    s.result[...] = (s.middle[...] + mod(gate_two) * mlp_branch).astype(bf16)
+    s.rowsum[5:6, :] = column_sum(s.cot[0].astype(f32) * mlp_branch)
+    spread_ada.last()
+    for y in range(2):
+        for zh, zl, x, c in itertools.product(range(2), repeat=4):
+            at = (y * 16 + zh * 8 + zl * 4 + x * 2 + c) * piece
+            for index in range(width // BLK):
+                s.ada_full[at + index * count : at + (index + 1) * count, :] = s.adaw[
+                    c * 16 + y * 8 + zh * 4 + zl * 2 + x, :,
+                    index * BLK : (index + 1) * BLK,
+                ]
+    high = s.rowsum[0:8, :].astype(bf16)
+    low = (s.rowsum[0:8, :] - high.astype(f32)).astype(bf16)
+    both = jnp.concatenate([high, low], axis=0)
+    terms = jnp.zeros((1, BLK), f32)
+    for index in range(6):
+        found = dot_nn(both, s.ada_full[index * width : (index + 1) * width, :])
+        terms = terms + found[index : index + 1, :] + found[8 + index : 9 + index, :]
+    s.rowsum[9:10, 0:BLK] = terms
+    totals = Total(s.sum_first, s.sum_mid, s.sum_last, s.sum_ss, s.sum_rs)
+    totals.start(s.rowsum[...])
+
+    ga_copies[0].wait_recv()
+    ga_copies[2].wait_recv()
     gattn = s.gattn[...].reshape(4 * rows, width)
 
     def spread(part, low, of):
@@ -1094,93 +1319,49 @@
                 ].astype(bf16)
 
     for head in range(heads):
+        s.wide[head * BLK : (head + 1) * BLK, 0:width] = dot_tn(s.dqkv[head], s.mixed[...])
+        at = (heads + head) * BLK
+        s.wide[at : at + BLK, 0:width] = dot_tn(s.dqkv[heads + head], s.mixed[...])
+    spread(0, True, 0)
+    spread(1, True, 1)
+    spread(2, False, 1)
+    totals.second()
+    for head in range(heads):
         s.wide[head * BLK + HEAD_DIM : (head + 1) * BLK, 0:width] = dot_nn(s.att[head], gattn)
     spread(3, False, 0)
-    for head in range(heads):
-        at = (heads + head) * BLK
-        s.wide[at : at + BLK, 0:width] = dot_tn(s.dqkv[head], s.mixed[...])
-    spread(0, True, 1)
-
-    def scatter_part(part, ss, rs):
-        return Scatter(
-            lambda slot: s.blocks_a.at[slot, part],
-            lambda k: s.from_a.at[k, part],
-            ss, rs,
-        )
-
-    scatter_o = scatter_part(3, s.so_ss, s.so_rs)
-    scatter_q = scatter_part(0, s.sq_ss, s.sq_rs)
-    scatter_k = scatter_part(1, s.sk_ss, s.sk_rs)
-    scatter_v = scatter_part(2, s.sv_ss, s.sv_rs)
-    scatter_o.step(C)
-    scatter_q.step(C)
-    scatter_r.add(Y)
-    scatter_e.add(Y)
-    for copy in mlp_copies:
-        copy.wait()
-    mlp_branch = (
-        s.mlp[...]
-        + s.mlp_recv[0].astype(f32) + s.mlp_recv[1].astype(f32) + s.mlp_recv[2].astype(f32)
-    )
-    s.result[...] = (s.middle[...] + mod(gate_two) * mlp_branch).astype(bf16)
-    s.rowsum[5:6, :] = column_sum(s.cotangent[...].astype(f32) * mlp_branch)
-    query_part = dot_nn(s.dqkv[0], s.weight[0])
-    for head in range(1, heads):
-        query_part = query_part + dot_nn(s.dqkv[head], s.weight[head])
-    s.part[...] = query_part
-    scatter_o.add(C)
-    scatter_q.add(C)
-    scatter_o.step(Y)
-    scatter_q.step(Y)
-
-    for head in range(heads):
-        dkv_copy(2, head, C).wait_recv()
-        s.dkv[head] += s.dkv_recv[2 * heads + head].astype(f32)
-    for head in range(heads):
-        dkv_copy(1, head, ZH).wait_recv()
-        value = s.dkv[head] + s.dkv_recv[heads + head].astype(f32)
-        s.dqkv[heads + head] = turn(value, s.cos[...], -s.sin[...]).astype(bf16)
-    scatter_r.step(ZH)
-    scatter_e.step(ZH)
-
-    kv_part = s.part[...]
-    for head in range(heads, 2 * heads):
-        kv_part = kv_part + dot_nn(s.dqkv[head], s.weight[head])
-    part_copies = []
-    for slot in (3, 2, 1):
-        s.part_send[slot - 1] = kv_part[here(slot), :].astype(bf16)
-        copy = remote(
-            s.part_send.at[slot - 1], s.part_recv.at[slot - 1], s.part_ss.at[slot],
-            s.part_rs.at[slot], TP[slot],
-        )
-        copy.start()
-        part_copies.append(copy)
-    s.grad_mixed[...] = kv_part[here(0), :]
-    for head in range(heads):
-        s.wide[head * BLK : (head + 1) * BLK, 0:width] = dot_tn(
-            s.dqkv[heads + head], s.mixed[...]
-        )
-    spread(1, True, 0)
-    spread(2, False, 0)
-    scatter_k.step(C)
-    scatter_v.step(C)
-    scatter_o.add(Y)
-    scatter_q.add(Y)
+    scatter_a = Scatter(
+        lambda slot, size: s.blocks_a.at[pl.ds(slot, size)],
+        lambda slot, size: s.from_a.at[pl.ds(slot, size)],
+        s.sa_ss, s.sa_rs, ZL,
+    )
+    scatter_a.step(C)
+    totals.third()
+    for half in range(2):
+        lines = slice(half * (rows // 2), (half + 1) * (rows // 2))
+        relays[half][0].wait_recv()
+        s.part_send[1, lines, :] = (
+            s.part[2 * rows + lines.start : 2 * rows + lines.stop, :]
+            + s.part_recv[2, lines, :].astype(f32)
+        ).astype(bf16)
+        relays[half][1].start()
+    part_copies[0].start()
+    scatter_a.add(C)
+    scatter_a.step(Y)
 
     def chunk_back(part, half):
-        slot = half * 4 + own % 4
+        slot = own // 2 * 2 + half
         place_in = 8 * my_rank + slot
         if part < 3:
             number = 32 * part + place_in
             owner, at = number // 3, number % 3
         else:
             owner, at = place_in, 3
-        zh = own // 4
+        z = own % 2
         index = part * 2 + half
         source = s.blocks_a.at[slot, part]
-        target = s.owned.at[zh, at]
+        target = s.owned.at[z, at]
         far = remote_to(
-            source, target, s.back_ss.at[index], s.back_rs.at[zh * 4 + at],
+            source, target, s.back_ss.at[index], s.back_rs.at[z * 4 + at],
             (owner // 16, owner % 16),
         )
         near = pltpu.make_async_copy(source, target, s.local_sem.at[index])
@@ -1199,90 +1380,40 @@
                 def _():
                     near.start() if act else near.wait()
 
-    chunks_back((0, 3), True)
-    scatter_k.add(C)
-    scatter_v.add(C)
-    scatter_k.step(Y)
-    scatter_v.step(Y)
-    for copy in part_copies:
-        copy.wait()
+    sums = totals.result()
+    for index in range(6):
+        for tile in range(width // BLK):
+            s.tiles[index * (width // BLK) + tile] = sums[
+                index : index + 1, tile * BLK : (tile + 1) * BLK
+            ]
+    for tile in range(width // BLK):
+        s.gain_tiles[tile] = sums[6:9, tile * BLK : (tile + 1) * BLK]
+    s.gain_tiles[width // BLK] = jnp.zeros((3, BLK), f32)
+    s.vec_own[...] = jnp.zeros_like(s.vec_own)
+    for tile in range(2):
+        lanes = slice(tile * BLK, (tile + 1) * BLK)
+        s.vec_own[0:1, lanes] = s.tiles[(9 * me) // 8 + tile]
+        s.vec_own[9:12, lanes] = s.gain_tiles[(3 * me) // 16 + tile]
+    s.sums[0:8, :] = pltpu.roll(s.vec_own[0:8, :], (256 - mod_shift) % 256, 1)
+    s.sums[8:16, :] = pltpu.roll(s.vec_own[8:16, :], (256 - gain_shift) % 256, 1)
+    s.grad_cond[...] = sums[9:10, 0:BLK]
+    scatter_a.add(Y)
+    chunks_back(range(4), True)
+    normed_one, inverse_one = layer_norm(s.tokens[...].astype(f32))
+    s.grad_r[0] = s.blocks_r[own_mlp]
+    s.grad_e[0] = s.blocks_e[own_mlp]
+    for scatter, target in ((scatter_r, s.grad_r), (scatter_e, s.grad_e)):
+        scatter.copies[ZH].wait_recv()
+        target[1] = scatter.inbox(6, 1)[0]
+    part_copies[0].wait_recv()
+    for half in range(2):
+        relays[half][1].wait_recv()
     grad_mixed_one = (
-        s.grad_mixed[...]
-        + s.part_recv[0].astype(f32) + s.part_recv[1].astype(f32) + s.part_recv[2].astype(f32)
-    )
-    normed_one, inverse_one = layer_norm(s.tokens[...].astype(f32))
-    weighted = column_sum(grad_mixed_one * normed_one)
-    s.rowsum[0:1, :] = column_sum(grad_mixed_one)
-    s.rowsum[1:2, :] = weighted * mod(6)
-    s.rowsum[6:7, :] = weighted * (1.0 + mod(scale_one))
-    tiles = width // BLK
-    s.vec_send[...] = jnp.zeros_like(s.vec_send)
-    for owner in range(32):
-        for tile in range(2):
-            lanes = slice(tile * BLK, (tile + 1) * BLK)
-            at = (9 * owner) // 8 + tile
-            s.vec_send[owner, 0:1, lanes] = s.rowsum[
-                at // tiles : at // tiles + 1, (at % tiles) * BLK : (at % tiles + 1) * BLK
-            ]
-            at = (3 * owner) // 16 + tile
-            if at < tiles:
-                s.vec_send[owner, 1:4, lanes] = s.rowsum[6:9, at * BLK : (at + 1) * BLK]
-
-    def sum_copy(offset):
-        return remote_to(
-            s.vec_send.at[flat(peer_loop(offset))], s.vec_recv.at[offset],
-            s.sum_ss.at[offset], s.sum_rs.at[offset], peer_loop(offset),
-        )
-
-    @pl.loop(1, 32)
-    def _(offset):
-        sum_copy(offset).start()
-
-    scatter_k.add(Y)
-    scatter_v.add(Y)
-    chunks_back((1, 2), True)
+        s.grad_mixed[...] + s.part_recv[0].astype(f32) + s.part_recv[1].astype(f32)
+    )
     s.grad_tokens[...] = s.gmid[...] + norm_back(
         grad_mixed_one * mod(9), normed_one, inverse_one
     )
-    s.vec_recv[0] = s.vec_send[me]
-
-    @pl.loop(1, 32)
-    def _(offset):
-        sum_copy(offset).wait()
-
-    total = jnp.zeros(s.vec_recv.shape[1:], f32)
-    for index in range(32):
-        total = total + s.vec_recv[index]
-    s.vec_own[0:4, :] = total
-    s.vec_own[8:12, :] = total
-    s.sums[0:8, :] = pltpu.roll(s.vec_own[0:8, :], (256 - mod_shift) % 256, 1)
-    s.sums[8:16, :] = pltpu.roll(s.vec_own[8:16, :], (256 - gain_shift) % 256, 1)
-    s.cond_send[...] = exact(s.sums[0:8, 0:piece], s.ada[...].astype(f32), ((1,), (0,)))
-
-    def cond_copy(offset):
-        return remote_to(
-            s.cond_send.at[pl.ds(0, 1)], s.cond_recv.at[offset], s.cond_ss.at[offset],
-            s.cond_rs.at[offset], peer_loop(offset),
-        )
-
-    @pl.loop(1, 32)
-    def _(offset):
-        cond_copy(offset).start()
-
-    s.grad_r[0] = s.blocks_r[own]
-    s.grad_e[0] = s.blocks_e[own]
-    for index, scatter, target in ((0, scatter_r, s.grad_r), (1, scatter_e, s.grad_e)):
-        scatter.copies[ZH][0].wait_recv()
-        target[1] = scatter.inbox(6)[...]
-
-    @pl.loop(1, 32)
-    def _(offset):
-        cond_copy(offset).wait()
-
-    gradient = s.cond_send[0:1, :]
-    for index in range(1, 32):
-        gradient = gradient + s.cond_recv[index]
-    s.grad_cond[...] = gradient
 
     chunks_back(range(4), False)
     for at in range(4):
@@ -1292,29 +1423,32 @@
         else:
             part, place_in = 3, me
         slot = place_in % 8
-        for zh in range(2):
-            keeper = flat(member(place_in // 8, zh * 4 + slot % 4))
+        for z in range(2):
+            keeper = flat(member(place_in // 8, slot // 2 * 2 + z))
 
             @pl.when(keeper != me)
             def _():
-                target = s.owned.at[zh, at]
+                target = s.owned.at[z, at]
                 remote(
-                    target, target, s.back_ss.at[0], s.back_rs.at[zh * 4 + at], C
+                    target, target, s.back_ss.at[0], s.back_rs.at[z * 4 + at], C
                 ).wait_recv()
 
-    for copies in (kv_far, kv_near, mix_copies, outw_sent, att_copies):
+    for copies in (
+        kv_far, kv_near, cot_copies, mix_copies, att_copies, ga_copies, mlp_copies, token_copies,
+        part_copies, *relays, *vec_steps,
+    ):
         for copy in copies:
             copy.wait_send()
-    for gather in (gather_kv, gather_q, gather_e, gather_r):
-        gather.finish()
-    for scatter in (scatter_e, scatter_r, scatter_o, scatter_q, scatter_k, scatter_v):
-        scatter.finish()
+    for group in (
+        gather_a, gather_er, spread_out, spread_ada, scatter_e, scatter_r, scatter_a, totals,
+    ):
+        group.finish()
 
     @pl.loop(0, heads)
     def _(head):
         kv_forward(head).wait_send()
         dkv_copy(0, head, C).wait_send()
-        dkv_copy(1, head, ZH).wait_send()
+        dkv_copy(1, head, ZL).wait_send()
         dkv_copy(2, head, C).wait_send()
 
 
@@ -1355,10 +1489,7 @@
     angles = (np.arange(length, dtype=np.float32)[:, None] * frequency[None, :]).astype(np.float32)
     cosine, sine = np.cos(angles.astype(np.float64)), np.sin(angles.astype(np.float64))
     one, zero = np.ones((length, HEAD_DIM)), np.zeros((length, HEAD_DIM))
-    return (
-        np.concatenate([cosine, cosine, one], axis=1).astype(np.float32),
-        np.concatenate([-sine, sine, zero], axis=1).astype(np.float32),
-    )
+    return np.concatenate([cosine, cosine, one, -sine, sine, zero], axis=1).astype(np.float32)
 
 
 def on_device_fast(
@@ -1373,17 +1504,15 @@
     count = output_weight.shape[0]
     piece = ada_weight.shape[1]
     wide = width + BLK
-    cosine, sine = (
-        jnp.asarray(table) for table in rotary_blocks(lax.axis_size("blk") * rows)
-    )
+    table = jnp.asarray(rotary_blocks(lax.axis_size("blk") * rows))
     line = condition[None, :]
     inputs = dict(
         tokens=tokens, cotangent=cotangent, condition=line, ada=ada_weight.T,
-        ada_bias=ada_bias[None, :], first_gain=first_gain[None, :],
+        ada_bias=ada_bias, first_gain=first_gain[None, :],
         second_gain=second_gain[None, :], reduce_bias=reduce_bias[None, :],
         expand_bias=expand_bias[None, :],
         project_weight=project_weight.T.reshape(3, count, width), output_weight=output_weight,
-        expand_weight=expand_weight.T, reduce_weight=reduce_weight, cos_hbm=cosine, sin_hbm=sine,
+        expand_weight=expand_weight.T, reduce_weight=reduce_weight, table=table,
     )
     outputs = dict(
         result=((rows, width), bf16), grad_tokens=((rows, width), f32),
@@ -1392,13 +1521,21 @@
         owned=((2, 4, count, width), bf16),
     )
     head_block = (group, BLK)
+    kept = {
+        name: (inputs[name].shape, inputs[name].dtype)
+        for name in (
+            "tokens", "condition", "ada", "ada_bias", "first_gain", "second_gain", "reduce_bias",
+            "expand_bias", "project_weight",
+        )
+    }
     scratch = dict(
-        cos=(head_block, f32), sin=(head_block, f32), vec_own=((16, 256), f32),
+        **kept,
+        table=((group, 2 * BLK), f32), vec_own=((16, 256), f32),
         vecs=((32, 4, 256), f32), mod_row=((1, 6 * width), f32), gain_rows=((3, wide), f32),
         mods=((16, width), f32), chunks=((8, 3, count, width), bf16),
         tok=((4, rows, width), bf16), cot=((4, rows, width), bf16),
-        expand=((8, per, wide), bf16), reduce=((8, per, width), bf16),
-        outw=((32, count, width), bf16), out_full=((width, width), bf16),
+        er=((8, per, wide + width), bf16),
+        outw=((32, count, width), bf16), adaw=((32, count, width), bf16), ada_full=((6 * width, BLK), bf16), out_full=((width, width), bf16),
         weight=((2 * heads, BLK, width), bf16), mixed=((group, width), bf16),
         query=((heads,) + head_block, bf16), kv=((4, heads) + head_block, bf16),
         state_m=((heads, 1, group), f32), state_l=((heads, 1, group), f32),
@@ -1407,7 +1544,6 @@
         att_all=((4, heads, HEAD_DIM, rows), bf16), attn=((rows, width), f32),
         middle=((rows, width), f32), normed=((rows, width), f32), inverse=((rows, 1), f32),
         mix=((4, rows, wide), bf16), branch=((group, width), bf16),
-        expand_full=((units, wide), bf16), reduce_full=((units, width), bf16),
         active=((group, units), bf16), grad_hid=((group, units), bf16),
         gm_send=((3, rows, width), bf16), gm_recv=((3, rows, width), bf16),
         mlp_send=((3, rows, width), bf16), mlp_recv=((3, rows, width), bf16),
@@ -1423,27 +1559,26 @@
         dkv_send=((3 * heads,) + head_block, bf16), dkv_recv=((3 * heads,) + head_block, bf16),
         dqkv=((2 * heads,) + head_block, bf16), part=((group, width), f32),
         part_send=((3, rows, width), bf16), part_recv=((3, rows, width), bf16),
-        vec_send=((32, 4, 256), f32), vec_recv=((32, 4, 256), f32),
-        cond_send=((8, line.shape[1]), f32), cond_recv=((32, 1, line.shape[1]), f32),
+        plain=((group, wide), bf16), norm_sum=((8, width), f32),
+        sum_first=((4, 16, width), f32), sum_mid=((2, 16, width), f32),
+        sum_last=((4, 16, width), f32), tiles=((6 * width // BLK, 1, BLK), f32),
+        gain_tiles=((width // BLK + 1, 3, BLK), f32),
+        mlp_near=((rows, width), f32),
     )
     semaphores = dict(
-        table_sem=8, local_sem=8, chunk_ss=3, chunk_rs=3, vec_ss=32, vec_rs=32, tok_ss=4,
-        tok_rs=4, akv_ss=8, akv_rs=8, aq_ss=8, aq_rs=8, e_ss=8, e_rs=8, r_ss=8, r_rs=8, o_ss=31,
-        o_rs=31, cot_ss=4, cot_rs=4, kv_ss=3 * heads, kv_rs=3 * heads, att_ss=4, att_rs=4,
-        mix_ss=4, mix_rs=4, gm_ss=4, gm_rs=4, mlp_ss=4, mlp_rs=4, dout_ss=4, dout_rs=4, ga_ss=4,
-        ga_rs=4, sr_ss=7, sr_rs=7, se_ss=7, se_rs=7, so_ss=6, so_rs=6, sq_ss=6, sq_rs=6, sk_ss=6,
-        sk_rs=6, sv_ss=6, sv_rs=6, dkv_ss=3 * heads, dkv_rs=3 * heads, part_ss=4, part_rs=4,
-        back_ss=8, back_rs=8, sum_ss=32, sum_rs=32, cond_ss=32, cond_rs=32,
+        load_sem=16, table_sem=4, local_sem=8, chunk_ss=3, chunk_rs=3, vec_ss=7, vec_rs=7,
+        tok_ss=4, tok_rs=4, a_ss=4, a_rs=4, er_ss=5, er_rs=5, o_ss=5, o_rs=5, ada_ss=5, ada_rs=5, cot_ss=4, cot_rs=4,
+        kv_ss=3 * heads, kv_rs=3 * heads, att_ss=4, att_rs=4, mix_ss=4, mix_rs=4, gm_ss=4,
+        gm_rs=4, mlp_ss=4, mlp_rs=4, dout_ss=4, dout_rs=4, ga_ss=4, ga_rs=4, sr_ss=3, sr_rs=3,
+        se_ss=3, se_rs=3, sa_ss=2, sa_rs=2, dkv_ss=3 * heads,
+        dkv_rs=3 * heads, part_ss=6, part_rs=6, back_ss=8, back_rs=8, sum_ss=7, sum_rs=7,
     )
     whole = pl.BlockSpec(memory_space=pltpu.VMEM)
-    names = (*inputs, *outputs, *scratch, *semaphores)
+    names = (*(name + "_hbm" for name in inputs), *outputs, *scratch, *semaphores)
     staged = pl.pallas_call(
         partial(block_kernel, names),
         out_shape=tuple(jax.ShapeDtypeStruct(*spec) for spec in outputs.values()),
-        in_specs=[
-            pl.BlockSpec(memory_space=pl.ANY) if name.endswith("_hbm") else whole
-            for name in inputs
-        ],
+        in_specs=[pl.BlockSpec(memory_space=pl.ANY)] * len(inputs),
         out_specs=tuple(whole for _ in outputs),
         scratch_shapes=[pltpu.VMEM(*spec) for spec in scratch.values()]
         + [pltpu.SemaphoreType.DMA((number,)) for number in semaphores.values()],
@@ -1490,34 +1625,34 @@
         on_device_fast if mesh.shape["ulysses"] * mesh.shape["blk"] == 32 else on_device,
         mesh=mesh,
         in_specs=(
-            P(("ulysses", "blk"), None),
+            P(BOTH, None),
             P(),
-            P(None, ("ulysses", "blk")),
-            P(("ulysses", "blk")),
-            P(("ulysses", "blk")),
-            P(("ulysses", "blk")),
-            P(None, ("ulysses", "blk")),
-            P(("ulysses", "blk"), None),
-            P(None, ("ulysses", "blk")),
-            P(("ulysses", "blk")),
-            P(("ulysses", "blk"), None),
-            P(("ulysses", "blk")),
-            P(("ulysses", "blk"), None),
+            P(None, BOTH),
+            P(BOTH),
+            P(BOTH),
+            P(BOTH),
+            P(None, BOTH),
+            P(BOTH, None),
+            P(None, BOTH),
+            P(BOTH),
+            P(BOTH, None),
+            P(BOTH),
+            P(BOTH, None),
         ),
         out_specs=(
-            P(("ulysses", "blk"), None),
-            P(("ulysses", "blk"), None),
+            P(BOTH, None),
+            P(BOTH, None),
             P(),
-            P(None, ("ulysses", "blk")),
-            P(("ulysses", "blk")),
-            P(("ulysses", "blk")),
-            P(("ulysses", "blk")),
-            P(None, ("ulysses", "blk")),
-            P(("ulysses", "blk"), None),
-            P(None, ("ulysses", "blk")),
-            P(("ulysses", "blk")),
-            P(("ulysses", "blk"), None),
-            P(("ulysses", "blk")),
+            P(None, BOTH),
+            P(BOTH),
+            P(BOTH),
+            P(BOTH),
+            P(None, BOTH),
+            P(BOTH, None),
+            P(None, BOTH),
+            P(BOTH),
+            P(BOTH, None),
+            P(BOTH),
         ),
         check_vma=False,
     )

time: 173 us -> 148 us (0.86)
  Pallas kernels: 170 us -> 147 us
    pallas_call x1, Pallas kernels: 167 us -> 144 us  [on_device_fast(): pl.pallas_call(partial(block_kernel, names), out_shape=tuple((jax.ShapeDt...]
where the time goes in v3:
time: 148 us; the launch traced here: 147 us
  Pallas kernels  147 us (99%)
    pallas_call x1, Pallas kernels, on_device_fast(): pl.pallas_call(partial(block_kernel, names), out_shape=tuple((jax.ShapeDt...  144 us

profile of v3, /device:TPU:5, one launch (start us, length us, event | category | flops | bytes accessed | tf_op | source)
XLA Modules:
  0.0 147.4 jit_solution(15356991967873594341)
XLA Ops:
  0.6 143.9 %shard_map.237 = (bf16[128,768]{1,0:T(8,128)(2,1)}, f32[128,768]{1,0:T(8,128)}, f32[1,128]{1,0:T(1,128)}, f32[16,256]{1,0:T(8,128)}, bf16[2,96,896]{2,1,0:T(8,12...) custom-call(bf16[128,768]{1,0:T(8,128)(2,1)} %refs_0_.1, bf16[128,768]{1,0:T(8,128)(2,1)} %refs_1_.1, ...), custom_call_target="tpu_custom_call" | custom-call | tf_op jit(solution)/shard_map/pallas_call | solution.py:1578
  144.5 2.7 %shard_map.238 = (bf16[128,768]{1,0:T(8,128)(2,1)}, f32[128,768]{1,0:T(8,128)}, f32[1,128]{1,0:T(1,128)}, f32[144,128]{1,0:T(8,128)}, f32[1,144]{1,0:T(1,128)}, ...) custom-call(bf16[128,768]{1,0:T(8,128)(2,1)} %get-tuple-element.33.r, ...), custom_call_target="tpu_custom_call" | custom-call | tf_op jit(solution)/shard_map/pallas_call | solution.py:1592

commit v4 on v3

--- a/solution.py
+++ b/solution.py
@@ -611,45 +611,49 @@
 
 
 class Total:
-    def __init__(self, first, mid, last, send_sem, recv_sem):
-        self.first, self.mid, self.last = first, mid, last
+    def __init__(self, halves, inbox, first, last, send_sem, recv_sem):
+        self.halves, self.inbox, self.first, self.last = halves, inbox, first, last
         y, zh, zl, x, c = place()
-        self.own = (y * 2 + zh, zl * 2 + x, c)
+        self.core = c
+        self.own = (y * 2 + zh, zl * 2 + x)
+        sems = [(send_sem.at[index], recv_sem.at[index]) for index in range(8)]
         self.copies = [
-            remote(
-                ref.at[own], ref.at[own], send_sem.at[3 * which + index],
-                recv_sem.at[3 * which + index], to,
-            )
+            remote(ref.at[own], ref.at[own], *sems[3 * which + index], to)
             for which, (ref, own, offsets) in enumerate(
-                (
-                    (first, self.own[0], (Y, ZH, Y + ZH)), (last, self.own[1], (ZL, X, ZL + X)),
-                    (mid, self.own[2], (C,)),
-                )
+                ((first, self.own[0], (Y, ZH, Y + ZH)), (last, self.own[1], (ZL, X, ZL + X)))
             )
             for index, to in enumerate(offsets)
         ]
-
-    def start(self, value):
-        self.first[self.own[0]] = value
+        self.copies.append(remote(halves.at[1 - c], inbox.at[0], *sems[6], C))
+        self.copies.append(remote(inbox.at[1 + c], inbox.at[1 + c], *sems[7], C))
+
+    def start(self):
+        self.copies[6].start()
+
+    def second(self):
+        self.copies[6].wait_recv()
+        self.first[self.own[0]] = self.halves[self.core] + self.inbox[0]
         for copy in self.copies[0:3]:
             copy.start()
 
-    def second(self):
+    def third(self):
         for copy in self.copies[0:3]:
             copy.wait_recv()
-        self.mid[self.own[2]] = self.first[0] + self.first[1] + self.first[2] + self.first[3]
-        self.copies[6].start()
-
-    def third(self):
-        self.copies[6].wait_recv()
-        self.last[self.own[1]] = self.mid[0] + self.mid[1]
+        self.last[self.own[1]] = (
+            self.first[0] + self.first[1] + self.first[2] + self.first[3]
+        )
         for copy in self.copies[3:6]:
             copy.start()
 
-    def result(self):
+    def fourth(self):
         for copy in self.copies[3:6]:
             copy.wait_recv()
-        return self.last[0] + self.last[1] + self.last[2] + self.last[3]
+        self.inbox[1 + self.core] = self.last[0] + self.last[1] + self.last[2] + self.last[3]
+        self.copies[7].start()
+
+    def result(self):
+        self.copies[7].wait_recv()
+        return jnp.concatenate([self.inbox[1], self.inbox[2]], axis=0)
 
     def finish(self):
         for copy in self.copies:
@@ -860,7 +864,6 @@
     for name in ("expand_weight", "reduce_weight", "output_weight", "cotangent", "tokens"):
         loads[name].wait()
     vec_step(1)
-    gather_er.far(0)
     spread_out.step(0)
     spread_ada.step(0)
 
@@ -922,7 +925,7 @@
             token_copies[2].start()
             cot_copies[0].start()
             spread_out.step(2)
-            gather_er.far(1)
+            gather_er.far(0)
             gather_er.near()
             gather_a.third()
         source = s.tok[slot] if slot else s.tokens[...]
@@ -936,6 +939,7 @@
                     slot, part, row : row + 8, :
                 ]
 
+    gather_er.far(1)
     gather_a.last()
     assemble(1, heads, True)
     assemble(2, heads, False)
@@ -964,6 +968,7 @@
         s.query[head] = (query * scale).astype(bf16)
     cot_copies[1].wait_recv()
     cot_copies[2].start()
+    spread_out.step(3)
 
 
     def attend(slot, head):
@@ -1001,7 +1006,6 @@
 
         @pl.when(head == 1)
         def _():
-            spread_out.step(3)
             gather_er.second()
 
         attend(2, head)
@@ -1127,8 +1131,18 @@
     s.mlp_send[0] = mlp_part(1).astype(bf16)
     s.mlp[...] = mlp_part(0) + mod(8)
     s.mlp_near[...] = mlp_part(2)
+    for index in range(units // BLK):
+        lanes = slice(index * BLK, (index + 1) * BLK)
+        s.wide[lanes, 0:width] = dot_tn(s.active[:, lanes], s.cot[...].reshape(4 * rows, width))
+    gate_sum = mod(8) * column_sum(s.cot[0].astype(f32))
+    for index in range(8):
+        gate_sum = gate_sum + column_sum(
+            s.er[index, :, wide:].astype(f32) * s.wide[index * per : (index + 1) * per, 0:width]
+        )
+    s.rowsum[5:6, :] = gate_sum
     for copy in gm_copies:
         copy.wait()
+    mlp_copies[0].start()
     grad_mixed = (
         s.grad_mixed[...]
         + s.gm_recv[0].astype(f32) + s.gm_recv[1].astype(f32) + s.gm_recv[2].astype(f32)
@@ -1174,7 +1188,6 @@
             dout_copies[slot - 1].wait()
         if slot == 3:
             ga_copies[1].start()
-            mlp_copies[0].start()
         for head in range(heads):
             s.dout_t[head, HEAD_DIM:, here(slot)] = s.dout_recv[slot, head]
     for head in range(heads):
@@ -1213,12 +1226,7 @@
         s.dkv_send[heads + head] = (part + s.dkv_recv[head].astype(f32)).astype(bf16)
         dkv_copy(1, head, ZL).start()
 
-    scatter_e.add(Y)
-    scatter_e.step(ZH)
     spread_ada.step(3)
-    mlp_copies[0].wait_recv()
-    s.mlp_send[1] = (s.mlp_near[...] + s.mlp_recv[2].astype(f32)).astype(bf16)
-    mlp_copies[2].start()
 
     @pl.loop(0, heads)
     def _(head):
@@ -1238,9 +1246,38 @@
     for head in range(1, heads):
         query_part = query_part + dot_nn(s.dqkv[head], s.weight[head])
     s.part[...] = query_part
+    ga_copies[0].wait_recv()
+    ga_copies[2].wait_recv()
+    gattn = s.gattn[...].reshape(4 * rows, width)
+
+    def spread(part, low, of):
+        for slot in range(8):
+            for row, head, target in head_rows(slot * count, count, low):
+                s.blocks_a[(part + 1) % 4 // 2, slot, (part + 1) % 2, row : row + 8, :] = s.wide[
+                    of * heads * BLK + head * BLK + target
+                    : of * heads * BLK + head * BLK + target + 8, 0:width
+                ].astype(bf16)
+
+    def scatter_pair(pair, ss, rs):
+        return Scatter(
+            lambda slot, size: s.blocks_a.at[pair, pl.ds(slot, size)],
+            lambda slot, size: s.from_a.at[pair, pl.ds(slot, size)],
+            ss, rs, ZL,
+        )
+
+    for head in range(heads):
+        s.wide[head * BLK + HEAD_DIM : (head + 1) * BLK, 0:width] = dot_nn(s.att[head], gattn)
+        at = (heads + head) * BLK
+        s.wide[at : at + BLK, 0:width] = dot_tn(s.dqkv[head], s.mixed[...])
+    spread(3, False, 0)
+    spread(0, True, 1)
+    scatter_oq = scatter_pair(0, s.soq_ss, s.soq_rs)
+    scatter_kv = scatter_pair(1, s.skv_ss, s.skv_rs)
+    scatter_oq.step(C)
     for head in range(heads):
         dkv_copy(2, head, C).wait_recv()
         s.dkv[head] += s.dkv_recv[2 * heads + head].astype(f32)
+    scatter_e.add(Y)
     for head in range(heads):
         dkv_copy(1, head, ZL).wait_recv()
         value = s.dkv[head] + s.dkv_recv[heads + head].astype(f32)
@@ -1267,9 +1304,16 @@
     s.part_send[2] = kv_part[here(3), :].astype(bf16)
     for half in range(2):
         relays[half][0].start()
+    scatter_e.step(ZH)
+    mlp_copies[0].wait_recv()
+    s.mlp_send[1] = (s.mlp_near[...] + s.mlp_recv[2].astype(f32)).astype(bf16)
+    mlp_copies[2].start()
     s.part_send[0] = kv_part[here(1), :].astype(bf16)
     s.part[here(2), :] = kv_part[here(2), :]
     s.grad_mixed[...] = kv_part[here(0), :]
+
+    scatter_oq.add(C)
+    scatter_oq.step(Y)
 
     s.norm_sum[...] = jnp.zeros_like(s.norm_sum)
     s.rowsum[9:16, :] = jnp.zeros((7, width), f32)
@@ -1281,11 +1325,6 @@
     s.rowsum[0:1, :] = s.norm_sum[0:1, :]
     s.rowsum[1:2, :] = s.norm_sum[1:2, :] * mod(6)
     s.rowsum[6:7, :] = s.norm_sum[1:2, :] * (1.0 + mod(scale_one))
-    for index in (1, 2):
-        mlp_copies[index].wait_recv()
-    mlp_branch = s.mlp[...] + s.mlp_recv[0].astype(f32) + s.mlp_recv[1].astype(f32)
-    s.result[...] = (s.middle[...] + mod(gate_two) * mlp_branch).astype(bf16)
-    s.rowsum[5:6, :] = column_sum(s.cot[0].astype(f32) * mlp_branch)
     spread_ada.last()
     for y in range(2):
         for zh, zl, x, c in itertools.product(range(2), repeat=4):
@@ -1303,39 +1342,19 @@
         found = dot_nn(both, s.ada_full[index * width : (index + 1) * width, :])
         terms = terms + found[index : index + 1, :] + found[8 + index : 9 + index, :]
     s.rowsum[9:10, 0:BLK] = terms
-    totals = Total(s.sum_first, s.sum_mid, s.sum_last, s.sum_ss, s.sum_rs)
-    totals.start(s.rowsum[...])
-
-    ga_copies[0].wait_recv()
-    ga_copies[2].wait_recv()
-    gattn = s.gattn[...].reshape(4 * rows, width)
-
-    def spread(part, low, of):
-        for slot in range(8):
-            for row, head, target in head_rows(slot * count, count, low):
-                s.blocks_a[slot, part, row : row + 8, :] = s.wide[
-                    of * heads * BLK + head * BLK + target
-                    : of * heads * BLK + head * BLK + target + 8, 0:width
-                ].astype(bf16)
+    totals = Total(s.sum_halves, s.sum_inbox, s.sum_first, s.sum_last, s.sum_ss, s.sum_rs)
+    s.sum_halves[0] = s.rowsum[0:8, :]
+    s.sum_halves[1] = s.rowsum[8:16, :]
+    totals.start()
 
     for head in range(heads):
-        s.wide[head * BLK : (head + 1) * BLK, 0:width] = dot_tn(s.dqkv[head], s.mixed[...])
-        at = (heads + head) * BLK
-        s.wide[at : at + BLK, 0:width] = dot_tn(s.dqkv[heads + head], s.mixed[...])
-    spread(0, True, 0)
-    spread(1, True, 1)
-    spread(2, False, 1)
+        s.wide[head * BLK : (head + 1) * BLK, 0:width] = dot_tn(
+            s.dqkv[heads + head], s.mixed[...]
+        )
     totals.second()
-    for head in range(heads):
-        s.wide[head * BLK + HEAD_DIM : (head + 1) * BLK, 0:width] = dot_nn(s.att[head], gattn)
-    spread(3, False, 0)
-    scatter_a = Scatter(
-        lambda slot, size: s.blocks_a.at[pl.ds(slot, size)],
-        lambda slot, size: s.from_a.at[pl.ds(slot, size)],
-        s.sa_ss, s.sa_rs, ZL,
-    )
-    scatter_a.step(C)
-    totals.third()
+    spread(1, True, 0)
+    spread(2, False, 0)
+    scatter_kv.step(C)
     for half in range(2):
         lines = slice(half * (rows // 2), (half + 1) * (rows // 2))
         relays[half][0].wait_recv()
@@ -1345,8 +1364,9 @@
         ).astype(bf16)
         relays[half][1].start()
     part_copies[0].start()
-    scatter_a.add(C)
-    scatter_a.step(Y)
+    scatter_kv.add(C)
+    scatter_kv.step(Y)
+    scatter_oq.add(Y)
 
     def chunk_back(part, half):
         slot = own // 2 * 2 + half
@@ -1358,7 +1378,7 @@
             owner, at = place_in, 3
         z = own % 2
         index = part * 2 + half
-        source = s.blocks_a.at[slot, part]
+        source = s.blocks_a.at[(part + 1) % 4 // 2, slot, (part + 1) % 2]
         target = s.owned.at[z, at]
         far = remote_to(
             source, target, s.back_ss.at[index], s.back_rs.at[z * 4 + at],
@@ -1380,6 +1400,16 @@
                 def _():
                     near.start() if act else near.wait()
 
+    chunks_back((0, 3), True)
+    totals.third()
+    for index in (1, 2):
+        mlp_copies[index].wait_recv()
+    mlp_branch = s.mlp[...] + s.mlp_recv[0].astype(f32) + s.mlp_recv[1].astype(f32)
+    s.result[...] = (s.middle[...] + mod(gate_two) * mlp_branch).astype(bf16)
+    normed_one, inverse_one = layer_norm(s.tokens[...].astype(f32))
+    scatter_kv.add(Y)
+    chunks_back((1, 2), True)
+    totals.fourth()
     sums = totals.result()
     for index in range(6):
         for tile in range(width // BLK):
@@ -1397,9 +1427,6 @@
     s.sums[0:8, :] = pltpu.roll(s.vec_own[0:8, :], (256 - mod_shift) % 256, 1)
     s.sums[8:16, :] = pltpu.roll(s.vec_own[8:16, :], (256 - gain_shift) % 256, 1)
     s.grad_cond[...] = sums[9:10, 0:BLK]
-    scatter_a.add(Y)
-    chunks_back(range(4), True)
-    normed_one, inverse_one = layer_norm(s.tokens[...].astype(f32))
     s.grad_r[0] = s.blocks_r[own_mlp]
     s.grad_e[0] = s.blocks_e[own_mlp]
     for scatter, target in ((scatter_r, s.grad_r), (scatter_e, s.grad_e)):
@@ -1440,7 +1467,7 @@
         for copy in copies:
             copy.wait_send()
     for group in (
-        gather_a, gather_er, spread_out, spread_ada, scatter_e, scatter_r, scatter_a, totals,
+        gather_a, gather_er, spread_out, spread_ada, scatter_e, scatter_r, scatter_oq, scatter_kv, totals,
     ):
         group.finish()
 
@@ -1551,17 +1578,17 @@
         gattn=((4, rows, width), bf16), dout_send=((4, heads, HEAD_DIM, rows), bf16),
         dout_recv=((4, heads, HEAD_DIM, rows), bf16), rowsum=((16, width), f32),
         wide=((units, wide), f32), blocks_r=((8, per, width), bf16),
-        blocks_e=((8, per, wide), bf16), blocks_a=((8, 4, count, width), bf16),
+        blocks_e=((8, per, wide), bf16), blocks_a=((2, 8, 2, count, width), bf16),
         from_r=((7, per, width), bf16), from_e=((7, per, wide), bf16),
-        from_a=((6, 4, count, width), bf16), dout_t=((heads, BLK, group), bf16),
+        from_a=((2, 6, 2, count, width), bf16), dout_t=((heads, BLK, group), bf16),
         dout=((heads,) + head_block, bf16), rdots=((heads, 1, group), f32),
         dq=((heads, BLK, group), f32), dkv=((heads,) + head_block, f32),
         dkv_send=((3 * heads,) + head_block, bf16), dkv_recv=((3 * heads,) + head_block, bf16),
         dqkv=((2 * heads,) + head_block, bf16), part=((group, width), f32),
         part_send=((3, rows, width), bf16), part_recv=((3, rows, width), bf16),
         plain=((group, wide), bf16), norm_sum=((8, width), f32),
-        sum_first=((4, 16, width), f32), sum_mid=((2, 16, width), f32),
-        sum_last=((4, 16, width), f32), tiles=((6 * width // BLK, 1, BLK), f32),
+        sum_halves=((2, 8, width), f32), sum_inbox=((3, 8, width), f32),
+        sum_first=((4, 8, width), f32), sum_last=((4, 8, width), f32), tiles=((6 * width // BLK, 1, BLK), f32),
         gain_tiles=((width // BLK + 1, 3, BLK), f32),
         mlp_near=((rows, width), f32),
     )
@@ -1570,8 +1597,8 @@
         tok_ss=4, tok_rs=4, a_ss=4, a_rs=4, er_ss=5, er_rs=5, o_ss=5, o_rs=5, ada_ss=5, ada_rs=5, cot_ss=4, cot_rs=4,
         kv_ss=3 * heads, kv_rs=3 * heads, att_ss=4, att_rs=4, mix_ss=4, mix_rs=4, gm_ss=4,
         gm_rs=4, mlp_ss=4, mlp_rs=4, dout_ss=4, dout_rs=4, ga_ss=4, ga_rs=4, sr_ss=3, sr_rs=3,
-        se_ss=3, se_rs=3, sa_ss=2, sa_rs=2, dkv_ss=3 * heads,
-        dkv_rs=3 * heads, part_ss=6, part_rs=6, back_ss=8, back_rs=8, sum_ss=7, sum_rs=7,
+        se_ss=3, se_rs=3, soq_ss=2, soq_rs=2, skv_ss=2, skv_rs=2, dkv_ss=3 * heads,
+        dkv_rs=3 * heads, part_ss=6, part_rs=6, back_ss=8, back_rs=8, sum_ss=8, sum_rs=8,
     )
     whole = pl.BlockSpec(memory_space=pltpu.VMEM)
     names = (*(name + "_hbm" for name in inputs), *outputs, *scratch, *semaphores)

time: 148 us -> 140 us (0.946)
  Pallas kernels: 147 us -> 139 us
    pallas_call x1, Pallas kernels: 144 us -> 136 us  [on_device_fast(): pl.pallas_call(partial(block_kernel, names), out_shape=tuple((jax.ShapeDt...]
where the time goes in v4:
time: 140 us; the launch traced here: 139 us
  Pallas kernels  139 us (99%)
    pallas_call x1, Pallas kernels, on_device_fast(): pl.pallas_call(partial(block_kernel, names), out_shape=tuple((jax.ShapeDt...  136 us

profile of v4, /device:TPU:5, one launch (start us, length us, event | category | flops | bytes accessed | tf_op | source)
XLA Modules:
  0.0 139.5 jit_solution(5658284527412110880)
XLA Ops:
  0.6 136.0 %shard_map.237 = (bf16[128,768]{1,0:T(8,128)(2,1)}, f32[128,768]{1,0:T(8,128)}, f32[1,128]{1,0:T(1,128)}, f32[16,256]{1,0:T(8,128)}, bf16[2,96,896]{2,1,0:T(8,12...) custom-call(bf16[128,768]{1,0:T(8,128)(2,1)} %refs_0_.1, bf16[128,768]{1,0:T(8,128)(2,1)} %refs_1_.1, ...), custom_call_target="tpu_custom_call" | custom-call | tf_op jit(solution)/shard_map/pallas_call | solution.py:1605
  136.6 2.7 %shard_map.238 = (bf16[128,768]{1,0:T(8,128)(2,1)}, f32[128,768]{1,0:T(8,128)}, f32[1,128]{1,0:T(1,128)}, f32[144,128]{1,0:T(8,128)}, f32[1,144]{1,0:T(1,128)}, ...) custom-call(bf16[128,768]{1,0:T(8,128)(2,1)} %get-tuple-element.33.r, ...), custom_call_target="tpu_custom_call" | custom-call | tf_op jit(solution)/shard_map/pallas_call | solution.py:1619

commit v5 on v4

--- a/solution.py
+++ b/solution.py
@@ -504,51 +504,45 @@
         own, core = share(0, far), share(C, far)
         z, y = share(far, far), share(Y, far)
         both = share(Y + far, far)
-        half = own // 4 * 4
-        other = core // 4 * 4
-        self.out = [
-            remote(view(own, 1), view(own, 1), send_sem.at[1], recv_sem.at[1], Y),
-            remote(view(z, 1), view(z, 1), send_sem.at[2], recv_sem.at[2], Y),
-            remote(view(half, 4), view(half, 4), send_sem.at[3], recv_sem.at[3], C),
+        half, other = own // 4 * 4, core // 4 * 4
+
+        def pair(mine, theirs, index, to, piece=lambda v: v):
+            return tuple(
+                remote(piece(where), piece(where), send_sem.at[index], recv_sem.at[index], to)
+                for where in (mine, theirs)
+            )
+
+        self.y_own = pair(view(own, 1), view(y, 1), 0, Y)
+        self.cores = pair(view(half, 4), view(other, 4), 1, C)
+        self.over_z = [
+            pair(view(own, 1), view(z, 1), 2 + 2 * index, far, piece)
+            for index, piece in enumerate(pieces)
         ]
-        self.parts = [
-            tuple(
-                remote(
-                    piece(view(where, 1)), piece(view(where, 1)), send_sem.at[index],
-                    recv_sem.at[index], far,
-                )
-                for where in (own, z)
-            )
-            for index, piece in zip((0, 4), pieces)
+        self.over_y = [
+            pair(view(z, 1), view(both, 1), 3 + 2 * index, Y, piece)
+            for index, piece in enumerate(pieces)
         ]
-        self.into = [
-            remote(view(where, size), view(where, size), send_sem.at[index], recv_sem.at[index], to)
-            for index, where, size, to in ((1, y, 1, Y), (2, both, 1, Y), (3, other, 4, C))
-        ]
 
     def near(self):
-        self.out[0].start()
+        self.y_own[0].start()
 
     def far(self, which=0):
-        self.parts[which][0].start()
-
-    def second(self):
-        for _out, into in self.parts:
+        self.over_z[which][0].start()
+
+    def second(self, which=0):
+        self.over_z[which][1].wait_recv()
+        self.over_y[which][0].start()
+
+    def third(self):
+        for _out, into in (self.y_own, *self.over_y):
             into.wait_recv()
-        self.out[1].start()
-
-    def third(self):
-        self.into[0].wait_recv()
-        self.into[1].wait_recv()
-        self.out[2].start()
+        self.cores[0].start()
 
     def last(self):
-        self.into[2].wait_recv()
+        self.cores[1].wait_recv()
 
     def finish(self):
-        for copy in self.out:
-            copy.wait_send()
-        for out, _into in self.parts:
+        for out, _into in (self.y_own, self.cores, *self.over_z, *self.over_y):
             out.wait_send()
 
 
@@ -990,6 +984,8 @@
         attend(0, head)
         attend(1, head)
 
+    gather_er.second(0)
+
     def kv_forward(head):
         return remote(
             s.kv.at[2, head], s.kv.at[3, head], s.kv_ss.at[2 * heads + head],
@@ -1006,7 +1002,7 @@
 
         @pl.when(head == 1)
         def _():
-            gather_er.second()
+            gather_er.second(1)
 
         attend(2, head)
         forward.wait_recv()
@@ -1044,12 +1040,17 @@
     s.normed[...] = normed
     s.inverse[...] = inverse
     s.mix[0, :, :width] = (normed * mod(10) + mod(shift_two)).astype(bf16)
+    def mix_copy(source, slot, number, lines, to):
+        return remote(
+            s.mix.at[source, lines, pl.ds(0, width)], s.mix.at[slot, lines, pl.ds(0, width)],
+            s.mix_ss.at[number], s.mix_rs.at[number], to,
+        )
+
     mix_copies = [
-        remote(
-            s.mix.at[0, :, pl.ds(0, width)], s.mix.at[slot, :, pl.ds(0, width)],
-            s.mix_ss.at[slot], s.mix_rs.at[slot], MLP[slot],
-        )
-        for slot in range(1, 4)
+        mix_copy(0, 1, 0, pl.ds(0, rows), X),
+        mix_copy(0, 2, 1, pl.ds(0, rows), ZL),
+        mix_copy(1, 3, 2, pl.ds(0, rows // 2), ZL),
+        mix_copy(2, 3, 3, pl.ds(rows // 2, rows // 2), X),
     ]
     for copy in mix_copies[0:2]:
         copy.start()
@@ -1074,11 +1075,13 @@
         for slot in range(1, 4)
     ]
     for first, last in ((0, 1), (1, 3), (3, 4)):
-        for slot in range(first, last):
-            if slot:
-                mix_copies[slot - 1].wait_recv()
         if first == 1:
-            mix_copies[2].start()
+            for index in range(2):
+                mix_copies[index].wait_recv()
+                mix_copies[2 + index].start()
+        elif first == 3:
+            mix_copies[2].wait_recv()
+            mix_copies[3].wait_recv()
         these = slice(first * rows, last * rows)
         mixed_two = s.mix[first:last].reshape((last - first) * rows, wide)
         activated, slope = gelu_pair(dot_nt(mixed_two, expand()))
@@ -1226,6 +1229,8 @@
         s.dkv_send[heads + head] = (part + s.dkv_recv[head].astype(f32)).astype(bf16)
         dkv_copy(1, head, ZL).start()
 
+    scatter_e.add(Y)
+    scatter_e.step(ZH)
     spread_ada.step(3)
 
     @pl.loop(0, heads)
@@ -1277,7 +1282,6 @@
     for head in range(heads):
         dkv_copy(2, head, C).wait_recv()
         s.dkv[head] += s.dkv_recv[2 * heads + head].astype(f32)
-    scatter_e.add(Y)
     for head in range(heads):
         dkv_copy(1, head, ZL).wait_recv()
         value = s.dkv[head] + s.dkv_recv[heads + head].astype(f32)
@@ -1304,7 +1308,6 @@
     s.part_send[2] = kv_part[here(3), :].astype(bf16)
     for half in range(2):
         relays[half][0].start()
-    scatter_e.step(ZH)
     mlp_copies[0].wait_recv()
     s.mlp_send[1] = (s.mlp_near[...] + s.mlp_recv[2].astype(f32)).astype(bf16)
     mlp_copies[2].start()
@@ -1594,7 +1597,7 @@
     )
     semaphores = dict(
         load_sem=16, table_sem=4, local_sem=8, chunk_ss=3, chunk_rs=3, vec_ss=7, vec_rs=7,
-        tok_ss=4, tok_rs=4, a_ss=4, a_rs=4, er_ss=5, er_rs=5, o_ss=5, o_rs=5, ada_ss=5, ada_rs=5, cot_ss=4, cot_rs=4,
+        tok_ss=4, tok_rs=4, a_ss=4, a_rs=4, er_ss=6, er_rs=6, o_ss=5, o_rs=5, ada_ss=5, ada_rs=5, cot_ss=4, cot_rs=4,
         kv_ss=3 * heads, kv_rs=3 * heads, att_ss=4, att_rs=4, mix_ss=4, mix_rs=4, gm_ss=4,
         gm_rs=4, mlp_ss=4, mlp_rs=4, dout_ss=4, dout_rs=4, ga_ss=4, ga_rs=4, sr_ss=3, sr_rs=3,
         se_ss=3, se_rs=3, soq_ss=2, soq_rs=2, skv_ss=2, skv_rs=2, dkv_ss=3 * heads,

time: 140 us -> 136 us (0.971); the launches traced: 139 us -> 133 us
  Pallas kernels: 139 us -> 133 us
    pallas_call x1, Pallas kernels: 136 us -> 130 us  [on_device_fast(): pl.pallas_call(partial(block_kernel, names), out_shape=tuple((jax.ShapeDt...]
where the time goes in v5:
time: 136 us; the launch traced here: 133 us
  Pallas kernels  133 us (98%)
    pallas_call x1, Pallas kernels, on_device_fast(): pl.pallas_call(partial(block_kernel, names), out_shape=tuple((jax.ShapeDt...  130 us

profile of v5, /device:TPU:5, one launch (start us, length us, event | category | flops | bytes accessed | tf_op | source)
XLA Modules:
  0.0 133.5 jit_solution(17847087565780817641)
XLA Ops:
  0.6 130.0 %shard_map.237 = (bf16[128,768]{1,0:T(8,128)(2,1)}, f32[128,768]{1,0:T(8,128)}, f32[1,128]{1,0:T(1,128)}, f32[16,256]{1,0:T(8,128)}, bf16[2,96,896]{2,1,0:T(8,12...) custom-call(bf16[128,768]{1,0:T(8,128)(2,1)} %refs_0_.1, bf16[128,768]{1,0:T(8,128)(2,1)} %refs_1_.1, ...), custom_call_target="tpu_custom_call" | custom-call | tf_op jit(solution)/shard_map/pallas_call | solution.py:1608
  130.6 2.7 %shard_map.238 = (bf16[128,768]{1,0:T(8,128)(2,1)}, f32[128,768]{1,0:T(8,128)}, f32[1,128]{1,0:T(1,128)}, f32[144,128]{1,0:T(8,128)}, f32[1,144]{1,0:T(1,128)}, ...) custom-call(bf16[128,768]{1,0:T(8,128)(2,1)} %get-tuple-element.33.r, ...), custom_call_target="tpu_custom_call" | custom-call | tf_op jit(solution)/shard_map/pallas_call | solution.py:1622

commit v6 on v5

--- a/solution.py
+++ b/solution.py
@@ -767,7 +767,17 @@
             s.tok_ss.at[slot], s.tok_rs.at[slot], to,
         )
 
-    token_copies = [token_copy(0, X), token_copy(0, ZH), token_copy(ZH, X)]
+    def token_half(have, to, half, number):
+        lines = pl.ds(half * (rows // 2), rows // 2)
+        slot = ATTN.index(have + to)
+        source = s.tok.at[ATTN.index(have), lines] if have else s.tokens.at[lines]
+        return remote(
+            source, s.tok.at[slot, lines], s.tok_ss.at[number], s.tok_rs.at[number], to
+        )
+
+    token_copies = [token_copy(0, X)]
+    token_z = [token_half(0, ZH, half, 2 + half) for half in range(2)]
+    token_on = [token_half(ZH, X, half, 4 + half) for half in range(2)]
     vec_steps = []
     for index, (size, offsets) in enumerate(
         ((1, (ZL, ZH, ZL + ZH)), (4, (C, X, X + C)), (16, (Y,)))
@@ -884,7 +894,8 @@
     cot_copies = [cot_copy(0, X), cot_copy(0, ZL), cot_copy(ZL, X)]
     gather_a.far()
     gather_a.near()
-    token_copies[1].start()
+    token_z[0].start()
+    token_z[1].start()
     token_copies[0].start()
     vec_step(2)
     spread_out.step(1)
@@ -912,11 +923,16 @@
         return s.mods[index : index + 1, :]
 
     for slot in range(4):
-        if slot == 1 or slot == 3:
-            token_copies[slot - 1].wait_recv()
+        if slot == 1:
+            token_copies[0].wait_recv()
+        if slot == 3:
+            token_on[0].wait_recv()
+            token_on[1].wait_recv()
         if slot == 2:
-            token_copies[1].wait_recv()
-            token_copies[2].start()
+            token_z[0].wait_recv()
+            token_z[1].wait_recv()
+            token_on[0].start()
+            token_on[1].start()
             cot_copies[0].start()
             spread_out.step(2)
             gather_er.far(0)
@@ -962,11 +978,10 @@
         s.query[head] = (query * scale).astype(bf16)
     cot_copies[1].wait_recv()
     cot_copies[2].start()
-    spread_out.step(3)
-
-
-    def attend(slot, head):
-        keys = s.kv[slot, head]
+
+
+    def attend(slot, head, count_of=1):
+        keys = s.kv[slot : slot + count_of, head].reshape(count_of * 4 * rows, BLK)
         scores = dot_nt(keys, s.query[head])
         before = s.state_m[head]
         maximum = jnp.maximum(before, jnp.max(scores, axis=0, keepdims=True))
@@ -981,8 +996,12 @@
 
     @pl.loop(0, heads)
     def _(head):
-        attend(0, head)
-        attend(1, head)
+        attend(0, head, 2)
+
+        @pl.when(head == 0)
+        def _():
+            spread_out.step(3)
+
 
     gather_er.second(0)
 
@@ -992,24 +1011,24 @@
             s.kv_rs.at[2 * heads + head], C,
         )
 
-    @pl.loop(0, heads)
-    def _(head):
-        remote(
-            s.kv.at[0, head], s.kv.at[2, head], s.kv_ss.at[head], s.kv_rs.at[head], ZL
-        ).wait_recv()
-        forward = kv_forward(head)
-        forward.start()
-
-        @pl.when(head == 1)
-        def _():
-            gather_er.second(1)
-
-        attend(2, head)
-        forward.wait_recv()
+    def finish_head(head):
+        forwards[head].wait_recv()
         attend(3, head)
         value = (s.acc[head] / s.state_l[head]).astype(bf16)
         s.att[head] = value[HEAD_DIM:, :]
         s.logt[head] = s.state_m[head] + jnp.log(s.state_l[head])
+
+    forwards = []
+    for head in range(heads):
+        kv_far[head].wait_recv()
+        forwards.append(kv_forward(head))
+        forwards[head].start()
+        attend(2, head)
+        if head == 1:
+            gather_er.second(1)
+        if head:
+            finish_head(head - 1)
+    finish_head(heads - 1)
 
     for slot in range(4):
         for head in range(heads):
@@ -1204,7 +1223,7 @@
     s.dq[...] = jnp.zeros_like(s.dq)
 
     def back(slot, head):
-        keys = s.kv[slot, head]
+        keys = s.kv[slot : slot + 2, head].reshape(2 * 4 * rows, BLK)
         query = s.query[head]
         shares = jnp.exp(dot_nt(keys, query) - s.logt[head])
         grad_shares = dot_nn(keys, s.dout_t[head])
@@ -1221,10 +1240,11 @@
 
     @pl.loop(0, heads)
     def _(head):
-        s.dkv_send[head] = back(3, head).astype(bf16)
+        both = back(2, head)
+        s.dkv_send[head] = both[4 * rows :].astype(bf16)
         first = dkv_copy(0, head, C)
         first.start()
-        part = back(2, head)
+        part = both[: 4 * rows]
         first.wait_recv()
         s.dkv_send[heads + head] = (part + s.dkv_recv[head].astype(f32)).astype(bf16)
         dkv_copy(1, head, ZL).start()
@@ -1235,26 +1255,22 @@
 
     @pl.loop(0, heads)
     def _(head):
-        @pl.when(head == 1)
+        @pl.when(head == 2)
         def _():
             ga_copies[1].wait_recv()
             ga_copies[2].start()
 
-        s.dkv_send[2 * heads + head] = back(1, head).astype(bf16)
+        both = back(0, head)
+        s.dkv_send[2 * heads + head] = both[4 * rows :].astype(bf16)
         dkv_copy(2, head, C).start()
-        s.dkv[head] = back(0, head)
+        s.dkv[head] = both[: 4 * rows]
         value = s.dq[head].T * scale
         s.dqkv[head] = turn(value, s.table[:, 0:BLK], -s.table[:, BLK:]).astype(bf16)
 
-    spread_ada.step(4)
     query_part = dot_nn(s.dqkv[0], s.weight[0])
     for head in range(1, heads):
         query_part = query_part + dot_nn(s.dqkv[head], s.weight[head])
     s.part[...] = query_part
-    ga_copies[0].wait_recv()
-    ga_copies[2].wait_recv()
-    gattn = s.gattn[...].reshape(4 * rows, width)
-
     def spread(part, low, of):
         for slot in range(8):
             for row, head, target in head_rows(slot * count, count, low):
@@ -1271,11 +1287,16 @@
         )
 
     for head in range(heads):
-        s.wide[head * BLK + HEAD_DIM : (head + 1) * BLK, 0:width] = dot_nn(s.att[head], gattn)
         at = (heads + head) * BLK
         s.wide[at : at + BLK, 0:width] = dot_tn(s.dqkv[head], s.mixed[...])
+    spread(0, True, 1)
+    ga_copies[0].wait_recv()
+    ga_copies[2].wait_recv()
+    gattn = s.gattn[...].reshape(4 * rows, width)
+
+    for head in range(heads):
+        s.wide[head * BLK + HEAD_DIM : (head + 1) * BLK, 0:width] = dot_nn(s.att[head], gattn)
     spread(3, False, 0)
-    spread(0, True, 1)
     scatter_oq = scatter_pair(0, s.soq_ss, s.soq_rs)
     scatter_kv = scatter_pair(1, s.skv_ss, s.skv_rs)
     scatter_oq.step(C)
@@ -1286,6 +1307,7 @@
         dkv_copy(1, head, ZL).wait_recv()
         value = s.dkv[head] + s.dkv_recv[heads + head].astype(f32)
         s.dqkv[heads + head] = turn(value, s.table[:, 0:BLK], -s.table[:, BLK:]).astype(bf16)
+    spread_ada.step(4)
     kv_part = s.part[...]
     for head in range(heads, 2 * heads):
         kv_part = kv_part + dot_nn(s.dqkv[head], s.weight[head])
@@ -1404,6 +1426,22 @@
                     near.start() if act else near.wait()
 
     chunks_back((0, 3), True)
+    for copies in (
+        kv_far, kv_near, cot_copies, mix_copies, att_copies, ga_copies, mlp_copies,
+        token_copies, token_z, token_on, *vec_steps,
+    ):
+        for copy in copies:
+            copy.wait_send()
+    for group in (gather_a, gather_er, spread_out, spread_ada, scatter_e, scatter_r):
+        group.finish()
+
+    @pl.loop(0, heads)
+    def _(head):
+        kv_forward(head).wait_send()
+        dkv_copy(0, head, C).wait_send()
+        dkv_copy(1, head, ZL).wait_send()
+        dkv_copy(2, head, C).wait_send()
+
     totals.third()
     for index in (1, 2):
         mlp_copies[index].wait_recv()
@@ -1413,6 +1451,21 @@
     scatter_kv.add(Y)
     chunks_back((1, 2), True)
     totals.fourth()
+    s.grad_r[0] = s.blocks_r[own_mlp]
+    s.grad_e[0] = s.blocks_e[own_mlp]
+    for scatter, target in ((scatter_r, s.grad_r), (scatter_e, s.grad_e)):
+        scatter.copies[ZH].wait_recv()
+        target[1] = scatter.inbox(6, 1)[0]
+    part_copies[0].wait_recv()
+    for half in range(2):
+        relays[half][1].wait_recv()
+    grad_mixed_one = (
+        s.grad_mixed[...] + s.part_recv[0].astype(f32) + s.part_recv[1].astype(f32)
+    )
+    s.grad_tokens[...] = s.gmid[...] + norm_back(
+        grad_mixed_one * mod(9), normed_one, inverse_one
+    )
+
     sums = totals.result()
     for index in range(6):
         for tile in range(width // BLK):
@@ -1430,20 +1483,6 @@
     s.sums[0:8, :] = pltpu.roll(s.vec_own[0:8, :], (256 - mod_shift) % 256, 1)
     s.sums[8:16, :] = pltpu.roll(s.vec_own[8:16, :], (256 - gain_shift) % 256, 1)
     s.grad_cond[...] = sums[9:10, 0:BLK]
-    s.grad_r[0] = s.blocks_r[own_mlp]
-    s.grad_e[0] = s.blocks_e[own_mlp]
-    for scatter, target in ((scatter_r, s.grad_r), (scatter_e, s.grad_e)):
-        scatter.copies[ZH].wait_recv()
-        target[1] = scatter.inbox(6, 1)[0]
-    part_copies[0].wait_recv()
-    for half in range(2):
-        relays[half][1].wait_recv()
-    grad_mixed_one = (
-        s.grad_mixed[...] + s.part_recv[0].astype(f32) + s.part_recv[1].astype(f32)
-    )
-    s.grad_tokens[...] = s.gmid[...] + norm_back(
-        grad_mixed_one * mod(9), normed_one, inverse_one
-    )
 
     chunks_back(range(4), False)
     for at in range(4):
@@ -1463,23 +1502,11 @@
                     target, target, s.back_ss.at[0], s.back_rs.at[z * 4 + at], C
                 ).wait_recv()
 
-    for copies in (
-        kv_far, kv_near, cot_copies, mix_copies, att_copies, ga_copies, mlp_copies, token_copies,
-        part_copies, *relays, *vec_steps,
-    ):
+    for copies in (part_copies, *relays):
         for copy in copies:
             copy.wait_send()
-    for group in (
-        gather_a, gather_er, spread_out, spread_ada, scatter_e, scatter_r, scatter_oq, scatter_kv, totals,
-    ):
+    for group in (scatter_oq, scatter_kv, totals):
         group.finish()
-
-    @pl.loop(0, heads)
-    def _(head):
-        kv_forward(head).wait_send()
-        dkv_copy(0, head, C).wait_send()
-        dkv_copy(1, head, ZL).wait_send()
-        dkv_copy(2, head, C).wait_send()
 
 
 def finish_kernel(
@@ -1597,7 +1624,7 @@
     )
     semaphores = dict(
         load_sem=16, table_sem=4, local_sem=8, chunk_ss=3, chunk_rs=3, vec_ss=7, vec_rs=7,
-        tok_ss=4, tok_rs=4, a_ss=4, a_rs=4, er_ss=6, er_rs=6, o_ss=5, o_rs=5, ada_ss=5, ada_rs=5, cot_ss=4, cot_rs=4,
+        tok_ss=6, tok_rs=6, a_ss=4, a_rs=4, er_ss=6, er_rs=6, o_ss=5, o_rs=5, ada_ss=5, ada_rs=5, cot_ss=4, cot_rs=4,
         kv_ss=3 * heads, kv_rs=3 * heads, att_ss=4, att_rs=4, mix_ss=4, mix_rs=4, gm_ss=4,
         gm_rs=4, mlp_ss=4, mlp_rs=4, dout_ss=4, dout_rs=4, ga_ss=4, ga_rs=4, sr_ss=3, sr_rs=3,
         se_ss=3, se_rs=3, soq_ss=2, soq_rs=2, skv_ss=2, skv_rs=2, dkv_ss=3 * heads,

time: 136 us -> 133 us (0.978); the launches traced: 133 us -> 133 us
  no operation moved by 1% of the time
where the time goes in v6:
time: 133 us
  Pallas kernels  132 us (99%)
    pallas_call x1, Pallas kernels, on_device_fast(): pl.pallas_call(partial(block_kernel, names), out_shape=tuple((jax.ShapeDt...  130 us
    pallas_call x1, Pallas kernels, on_device_fast(): pl.pallas_call(finish_kernel, out_shape=tuple((jax.ShapeDtypeStruct(shape...  2.69 us

profile of v6, /device:TPU:5, one launch (start us, length us, event | category | flops | bytes accessed | tf_op | source)
XLA Modules:
  0.0 133.1 jit_solution(1005305003107516609)
XLA Ops:
  0.6 129.6 %shard_map.237 = (bf16[128,768]{1,0:T(8,128)(2,1)}, f32[128,768]{1,0:T(8,128)}, f32[1,128]{1,0:T(1,128)}, f32[16,256]{1,0:T(8,128)}, bf16[2,96,896]{2,1,0:T(8,12...) custom-call(bf16[128,768]{1,0:T(8,128)(2,1)} %refs_0_.1, bf16[128,768]{1,0:T(8,128)(2,1)} %refs_1_.1, ...), custom_call_target="tpu_custom_call" | custom-call | tf_op jit(solution)/shard_map/pallas_call | solution.py:1635
  130.3 2.7 %shard_map.238 = (bf16[128,768]{1,0:T(8,128)(2,1)}, f32[128,768]{1,0:T(8,128)}, f32[1,128]{1,0:T(1,128)}, f32[144,128]{1,0:T(8,128)}, f32[1,144]{1,0:T(1,128)}, ...) custom-call(bf16[128,768]{1,0:T(8,128)(2,1)} %get-tuple-element.33.r, ...), custom_call_target="tpu_custom_call" | custom-call | tf_op jit(solution)/shard_map/pallas_call | solution.py:1649

commit v7 on v6

--- a/solution.py
+++ b/solution.py
@@ -1164,7 +1164,6 @@
     s.rowsum[5:6, :] = gate_sum
     for copy in gm_copies:
         copy.wait()
-    mlp_copies[0].start()
     grad_mixed = (
         s.grad_mixed[...]
         + s.gm_recv[0].astype(f32) + s.gm_recv[1].astype(f32) + s.gm_recv[2].astype(f32)
@@ -1219,6 +1218,7 @@
     scatter_r.add(Y)
     scatter_r.step(ZH)
     ga_copies[0].start()
+    mlp_copies[0].start()
     mlp_copies[1].start()
     s.dq[...] = jnp.zeros_like(s.dq)
 
@@ -1267,6 +1267,7 @@
         value = s.dq[head].T * scale
         s.dqkv[head] = turn(value, s.table[:, 0:BLK], -s.table[:, BLK:]).astype(bf16)
 
+    spread_ada.step(4)
     query_part = dot_nn(s.dqkv[0], s.weight[0])
     for head in range(1, heads):
         query_part = query_part + dot_nn(s.dqkv[head], s.weight[head])
@@ -1300,6 +1301,26 @@
     scatter_oq = scatter_pair(0, s.soq_ss, s.soq_rs)
     scatter_kv = scatter_pair(1, s.skv_ss, s.skv_rs)
     scatter_oq.step(C)
+    s.norm_sum[...] = jnp.zeros_like(s.norm_sum)
+    s.rowsum[9:16, :] = jnp.zeros((7, width), f32)
+
+    def norm_sums(which):
+        for head in which:
+            moment = dot_tn(s.dqkv[head], s.plain[...])
+            weights = s.weight[head].astype(f32)
+            s.norm_sum[0:1, :] += column_sum(weights * moment[:, width : width + 1])
+            s.norm_sum[1:2, :] += column_sum(weights * moment[:, 0:width])
+
+    norm_sums(range(heads))
+    spread_ada.last()
+    for y in range(2):
+        for zh, zl, x, c in itertools.product(range(2), repeat=4):
+            at = (y * 16 + zh * 8 + zl * 4 + x * 2 + c) * piece
+            for index in range(width // BLK):
+                s.ada_full[at + index * count : at + (index + 1) * count, :] = s.adaw[
+                    c * 16 + y * 8 + zh * 4 + zl * 2 + x, :,
+                    index * BLK : (index + 1) * BLK,
+                ]
     for head in range(heads):
         dkv_copy(2, head, C).wait_recv()
         s.dkv[head] += s.dkv_recv[2 * heads + head].astype(f32)
@@ -1307,7 +1328,6 @@
         dkv_copy(1, head, ZL).wait_recv()
         value = s.dkv[head] + s.dkv_recv[heads + head].astype(f32)
         s.dqkv[heads + head] = turn(value, s.table[:, 0:BLK], -s.table[:, BLK:]).astype(bf16)
-    spread_ada.step(4)
     kv_part = s.part[...]
     for head in range(heads, 2 * heads):
         kv_part = kv_part + dot_nn(s.dqkv[head], s.weight[head])
@@ -1340,25 +1360,10 @@
     scatter_oq.add(C)
     scatter_oq.step(Y)
 
-    s.norm_sum[...] = jnp.zeros_like(s.norm_sum)
-    s.rowsum[9:16, :] = jnp.zeros((7, width), f32)
-    for head in range(2 * heads):
-        moment = dot_tn(s.dqkv[head], s.plain[...])
-        weights = s.weight[head].astype(f32)
-        s.norm_sum[0:1, :] += column_sum(weights * moment[:, width : width + 1])
-        s.norm_sum[1:2, :] += column_sum(weights * moment[:, 0:width])
+    norm_sums(range(heads, 2 * heads))
     s.rowsum[0:1, :] = s.norm_sum[0:1, :]
     s.rowsum[1:2, :] = s.norm_sum[1:2, :] * mod(6)
     s.rowsum[6:7, :] = s.norm_sum[1:2, :] * (1.0 + mod(scale_one))
-    spread_ada.last()
-    for y in range(2):
-        for zh, zl, x, c in itertools.product(range(2), repeat=4):
-            at = (y * 16 + zh * 8 + zl * 4 + x * 2 + c) * piece
-            for index in range(width // BLK):
-                s.ada_full[at + index * count : at + (index + 1) * count, :] = s.adaw[
-                    c * 16 + y * 8 + zh * 4 + zl * 2 + x, :,
-                    index * BLK : (index + 1) * BLK,
-                ]
     high = s.rowsum[0:8, :].astype(bf16)
     low = (s.rowsum[0:8, :] - high.astype(f32)).astype(bf16)
     both = jnp.concatenate([high, low], axis=0)

time: 133 us -> 132 us (level)
    pallas_call x1, Pallas kernels: 130 us -> 128 us  [on_device_fast(): pl.pallas_call(partial(block_kernel, names), out_shape=tuple((jax.ShapeDt...]
where the time goes in v7:
time: 132 us; the launch traced here: 131 us
  Pallas kernels  131 us (99%)
    pallas_call x1, Pallas kernels, on_device_fast(): pl.pallas_call(partial(block_kernel, names), out_shape=tuple((jax.ShapeDt...  128 us
    pallas_call x1, Pallas kernels, on_device_fast(): pl.pallas_call(finish_kernel, out_shape=tuple((jax.ShapeDtypeStruct(shape...  2.69 us

profile of v7, /device:TPU:5, one launch (start us, length us, event | category | flops | bytes accessed | tf_op | source)
XLA Modules:
  0.0 131.4 jit_solution(17563858303509071177)
XLA Ops:
  0.6 127.9 %shard_map.237 = (bf16[128,768]{1,0:T(8,128)(2,1)}, f32[128,768]{1,0:T(8,128)}, f32[1,128]{1,0:T(1,128)}, f32[16,256]{1,0:T(8,128)}, bf16[2,96,896]{2,1,0:T(8,12...) custom-call(bf16[128,768]{1,0:T(8,128)(2,1)} %refs_0_.1, bf16[128,768]{1,0:T(8,128)(2,1)} %refs_1_.1, ...), custom_call_target="tpu_custom_call" | custom-call | tf_op jit(solution)/shard_map/pallas_call | solution.py:1640
  128.6 2.7 %shard_map.238 = (bf16[128,768]{1,0:T(8,128)(2,1)}, f32[128,768]{1,0:T(8,128)}, f32[1,128]{1,0:T(1,128)}, f32[144,128]{1,0:T(8,128)}, f32[1,144]{1,0:T(1,128)}, ...) custom-call(bf16[128,768]{1,0:T(8,128)(2,1)} %get-tuple-element.33.r, ...), custom_call_target="tpu_custom_call" | custom-call | tf_op jit(solution)/shard_map/pallas_call | solution.py:1654
